TPU v7x, 128 devices: a whole 4x4x4 slice. The times are simulated.
128 devices in a mesh: segment: 2 (over y_lo), space: 32 (over x, z, core), mirror: 2 (over y_hi).
Axes of the slice: x: 4, y: 4 (y_hi: 2, y_lo: 2; y = y_hi * 2 + y_lo), z: 4, core: 2. Of those that a mesh axis runs over, the one named last changes fastest.
Arguments:
- arrivals: bfloat16 [2, 2, 512, 128, 256], P('mirror', 'segment', 'space'), may hold values from -6 to 6
- stashed: bfloat16 [2, 2, 512, 128, 256], P('mirror', 'segment', 'space'), may hold values from -6 to 6
- weights: bfloat16 [2, 2, 2, 3, 3, 256, 256], P('mirror', 'segment'), may hold values from -0.125 to 0.125
Outputs:
- departures: bfloat16 [2, 2, 512, 128, 256], P('mirror', 'segment', 'space')
- grad_sum: float32 [2, 2, 256, 2, 3, 3, 256], P('mirror', 'segment', 'space')
All inputs are finite; a program needn't handle non-finite values.
Results may differ from a plain program's by a relative error of at most 0.0053.
Values may be sent and summed in bfloat16 or wider, within the bound.
No kernel may reach another device: no remote copies, remote signals or barrier semaphores. Data moves between devices by JAX's collectives and lax.ppermute only.
A program may use at most 128 MiB of HBM per device.

v0:
```python
import functools
import math

import jax
import jax.numpy as jnp
from jax import lax
from jax.experimental import pallas as pl
from jax.experimental.pallas import tpu as pltpu
from jax.sharding import Mesh
from jax.sharding import PartitionSpec as P

SPACE = ("space_0", "space_1", "space_2")
BF16 = jnp.bfloat16
F32 = jnp.float32
COLS = 128
CH = 256
TAPS = 9 * CH
MIB = 1 << 20


def rows(first, count):
    start = first * COLS
    if not isinstance(start, int):
        start = pl.multiple_of(start, COLS)
    return pl.ds(start, count * COLS)


def repeat(steps, body):
    def step(index, carry):
        body(index)
        return carry

    lax.fori_loop(0, steps, step, 0)


def store3(dst, row, val, count):
    size = count * COLS
    col = lax.broadcasted_iota(jnp.int32, (size, CH), 0) & (COLS - 1)
    val = val.astype(F32)
    left = jnp.where(col == 0, 0.0, pltpu.roll(val, 1, 0))
    right = jnp.where(col == COLS - 1, 0.0, pltpu.roll(val, size - 1, 0))
    where = rows(row, count)
    dst[where, 0:CH] = left.astype(BF16)
    dst[where, CH : 2 * CH] = val.astype(BF16)
    dst[where, 2 * CH :] = right.astype(BF16)


def fill3(dst, row, src, first, count):
    for step in range(0, count, 2):
        size = min(2, count - step)
        store3(dst, row + step, src[rows(first + step, size), :], size)


def conv(src3, first, count, weights, which, transposed):
    total = None
    for a in range(3):
        for b in range(3):
            window = src3[rows(first + a, count), b * CH : (b + 1) * CH]
            if transposed:
                part = lax.dot_general(
                    window,
                    weights[which, 2 - a, 2 - b],
                    (((1,), (1,)), ((), ())),
                    preferred_element_type=F32,
                )
            else:
                part = jnp.dot(window, weights[which, a, b], preferred_element_type=F32)
            total = part if total is None else total + part
    return total


def outer(left, right):
    return lax.dot_general(left, right, (((0,), (0,)), ((), ())), preferred_element_type=F32)


def put_grad(dst, conv_index, a, val):
    for b in range(3):
        at = conv_index * TAPS + (3 * a + b) * CH
        if not isinstance(at, int):
            at = pl.multiple_of(at, CH)
        dst[:, pl.ds(at, CH)] = val[:, (2 - b) * CH : (3 - b) * CH]


def get_grad(src, conv_index, a):
    parts = []
    for b in (2, 1, 0):
        at = conv_index * TAPS + (3 * a + b) * CH
        parts.append(src[:, at : at + CH])
    return jnp.concatenate(parts, axis=1)


def activate(pre):
    sig = jax.nn.sigmoid(pre)
    return pre * sig, sig * (1.0 + pre * (1.0 - sig))


def is_leading():
    return lax.axis_index("segment") == lax.axis_index("mirror")


def by_role(body):
    leading = is_leading()

    @pl.when(leading)
    def _():
        body(True)

    @pl.when(jnp.logical_not(leading))
    def _():
        body(False)


def edge_flags():
    place = lax.axis_index(SPACE)
    count = lax.axis_size(SPACE)
    return (place > 0).astype(F32), (place < count - 1).astype(F32)


def kernel_load(arr_hbm, sta_hbm, w_hbm, low, high, arr, sta, w, sems):
    two = 2 * COLS
    size = arr_hbm.shape[0]
    moves = (
        (arr_hbm.at[pl.ds(size - two, two)], low.at[0]),
        (sta_hbm.at[pl.ds(size - two, two)], low.at[1]),
        (arr_hbm.at[pl.ds(0, two)], high.at[0]),
        (sta_hbm.at[pl.ds(0, two)], high.at[1]),
        (w_hbm.at[0], w.at[0]),
        (sta_hbm, sta),
        (arr_hbm, arr),
        (w_hbm.at[1], w.at[1]),
    )
    copies = [pltpu.make_async_copy(src, dst, sems.at[i]) for i, (src, dst) in enumerate(moves)]
    for copy in copies:
        copy.start()
    for copy in copies:
        copy.wait()


def kernel_a(arr, sta, w, out_m, act_m, hid_m, slope_m, s3, a3, c3):
    def body(leading):
        fill3(s3, 0, sta, 2, 12)
        fill3(a3, 0, arr, 2, 12)

        def inner(step):
            row = 5 * step
            pre = conv(s3, row, 5, w, 0, False)
            hid, slope = activate(pre)
            hid_m[rows(row, 5), :] = hid.astype(BF16)
            slope_m[rows(row, 5), :] = slope
            if leading:
                act, _ = activate(conv(a3, row, 5, w, 0, False))
            else:
                act = conv(a3, row, 5, w, 1, True) * slope
            act_m[rows(row, 5), :] = act.astype(BF16)
            store3(c3, row, act, 5)

        def last(step):
            row = 4 * step
            total = conv(c3, row, 4, w, 1 if leading else 0, not leading)
            out_m[rows(row, 4), :] = (total + arr[rows(4 + row, 4), :].astype(F32)).astype(BF16)

        repeat(2, inner)
        repeat(2, last)

    by_role(body)


def kernel_b(arr, sta, up, down, act_m, w, out_e, act_e, hid_e, slope_e, s3, a3, c3):
    has_up, has_down = edge_flags()

    def body(leading):
        for half in range(2):
            if half == 0:
                store3(s3, 0, up[1], 2)
                fill3(s3, 2, sta, 0, 4)
                store3(a3, 0, up[0], 2)
                fill3(a3, 2, arr, 0, 4)
            else:
                fill3(s3, 6, sta, 12, 4)
                store3(s3, 10, down[1], 2)
                fill3(a3, 6, arr, 12, 4)
                store3(a3, 10, down[0], 2)
            pre = conv(s3, 6 * half, 4, w, 0, False)
            hid, slope = activate(pre)
            spot = lax.broadcasted_iota(jnp.int32, (4 * COLS, CH), 0) // COLS
            if half == 0:
                mask = jnp.where(spot == 0, has_up, 1.0)
            else:
                mask = jnp.where(spot == 3, has_down, 1.0)
            hid_e[rows(4 * half, 4), :] = (hid * mask).astype(BF16)
            slope_e[rows(4 * half, 4), :] = slope
            if leading:
                act, _ = activate(conv(a3, 6 * half, 4, w, 0, False))
            else:
                act = conv(a3, 6 * half, 4, w, 1, True) * slope
            act = act * mask
            act_e[rows(4 * half, 4), :] = act.astype(BF16)
            if half == 0:
                store3(c3, 0, act, 4)
                fill3(c3, 4, act_m, 0, 2)
            else:
                fill3(c3, 6, act_m, 8, 2)
                store3(c3, 8, act, 4)
            total = conv(c3, 6 * half, 4, w, 1 if leading else 0, not leading)
            kept = arr[rows(12 * half, 4), :].astype(F32)
            out_e[rows(4 * half, 4), :] = (total + kept).astype(BF16)

    by_role(body)


def kernel_c(
    got_m, arr, sta, up, down, act_m, act_e, hid_m, hid_e, slope_m, w, act2_m, grad, r3, y3, z3, whole
):
    def body(leading):
        fill3(r3, 0, got_m, 0, 8)
        total = conv(r3, 0, 6, w, 1 if leading else 0, leading)
        if leading:
            act = total * slope_m[rows(2, 6), :]
            act2_m[...] = act.astype(BF16)
            store3(z3, 0, act, 6)
            for a in range(3):
                put_grad(grad, 1, a, outer(hid_m[rows(a, 8), :], r3[rows(0, 8), :]))
                put_grad(grad, 0, a, outer(sta[rows(4 + a, 6), :], z3[rows(0, 6), :]))
        else:
            act, _ = activate(total)
            act2_m[...] = act.astype(BF16)

            def shift_arr(step):
                store3(y3, 2 * step, arr[rows(2 * step, 2), :], 2)

            repeat(8, shift_arr)
            whole[rows(0, 4), :] = hid_e[rows(0, 4), :]
            whole[rows(4, 10), :] = hid_m[...]
            whole[rows(14, 4), :] = hid_e[rows(4, 4), :]

            def second_grad(a):
                put_grad(grad, 1, a, outer(whole[rows(a, 16), :], y3[...]))

            def first_grad(a):
                put_grad(grad, 0, a, outer(whole[rows(a, 16), :], z3[...]))

            repeat(3, second_grad)
            fill3(z3, 0, act_e, 1, 3)
            fill3(z3, 3, act_m, 0, 10)
            fill3(z3, 13, act_e, 4, 3)
            whole[rows(0, 1), :] = up[1, rows(1, 1), :]
            whole[rows(1, 16), :] = sta[...]
            whole[rows(17, 1), :] = down[1, rows(0, 1), :]
            repeat(3, first_grad)

    by_role(body)


def kernel_d(got_m, got_e, sta, hid_m, hid_e, slope_m, slope_e, grad_in, w, act2_e, grad, r3, z3, h6):
    def body(leading):
        fill3(r3, 0, got_e, 0, 4)
        fill3(r3, 4, got_m, 0, 2)
        fill3(r3, 6, got_m, 6, 2)
        fill3(r3, 8, got_e, 4, 4)
        for half in range(2):
            total = conv(r3, 6 * half, 4, w, 1 if leading else 0, leading)
            if leading:
                if half == 0:
                    slope = jnp.concatenate([slope_e[rows(2, 2), :], slope_m[rows(0, 2), :]], axis=0)
                else:
                    slope = jnp.concatenate([slope_m[rows(8, 2), :], slope_e[rows(4, 2), :]], axis=0)
                act = total * slope
                store3(z3, 4 * half, act, 4)
            else:
                act, _ = activate(total)
            act2_e[rows(4 * half, 4), :] = act.astype(BF16)
        if leading:
            h6[rows(0, 4), :] = hid_e[rows(0, 4), :]
            h6[rows(4, 2), :] = hid_m[rows(0, 2), :]
            h6[rows(6, 2), :] = hid_m[rows(8, 2), :]
            h6[rows(8, 4), :] = hid_e[rows(4, 4), :]
            for a in range(3):
                more = outer(h6[rows(a, 4), :], r3[rows(0, 4), :])
                more = more + outer(h6[rows(6 + a, 4), :], r3[rows(8, 4), :])
                put_grad(grad, 1, a, get_grad(grad_in, 1, a) + more)
                more = outer(sta[rows(a, 4), :], z3[rows(0, 4), :])
                more = more + outer(sta[rows(10 + a, 4), :], z3[rows(4, 4), :])
                put_grad(grad, 0, a, get_grad(grad_in, 0, a) + more)

    by_role(body)


def kernel_e(
    scale, got_e, got_up, got_down, sta, up, down, slope_e, grad_c, grad_d, w, act2_h, send, keep, r3, z3, x2, tot
):
    has_up, has_down = edge_flags()
    core = lax.axis_index("space_2")

    def emit(src, from_at, to_at, width):
        for pair in range(8):
            for dst, side in ((keep, core), (send, 1 - core)):
                first = pl.multiple_of(32 * pair + 8 * side, 8)
                second = pl.multiple_of(32 * pair + 16 + 8 * side, 8)
                val = jnp.concatenate(
                    [
                        src[pl.ds(first, 8), from_at : from_at + width],
                        src[pl.ds(second, 8), from_at : from_at + width],
                    ],
                    axis=0,
                )
                dst[pl.ds(16 * pair, 16), to_at : to_at + width] = (val * scale).astype(dst.dtype)

    def body(leading):
        store3(r3, 0, got_up[...], 2)
        fill3(r3, 2, got_e, 0, 2)
        fill3(r3, 4, got_e, 6, 2)
        store3(r3, 6, got_down[...], 2)
        spot = lax.broadcasted_iota(jnp.int32, (2 * COLS, CH), 0) // COLS
        for half in range(2):
            total = conv(r3, 4 * half, 2, w, 1 if leading else 0, leading)
            if leading:
                act = total * slope_e[rows(6 * half, 2), :]
            else:
                act, _ = activate(total)
            if half == 0:
                act = act * jnp.where(spot == 0, has_up, 1.0)
            else:
                act = act * jnp.where(spot == 1, has_down, 1.0)
            act2_h[rows(2 * half, 2), :] = act.astype(BF16)
        if leading:
            store3(z3, 0, act2_h[rows(1, 2), :], 2)
            x2[rows(0, 1), :] = up[1, rows(1, 1), :]
            x2[rows(1, 2), :] = sta[rows(0, 2), :]
            x2[rows(3, 2), :] = sta[rows(14, 2), :]
            x2[rows(5, 1), :] = down[1, rows(0, 1), :]
            for a in range(3):
                left = jnp.concatenate([x2[rows(a, 1), :], x2[rows(3 + a, 1), :]], axis=0)
                put_grad(tot, 0, a, get_grad(grad_d, 0, a) + outer(left, z3[...]))
            emit(tot, 0, 0, TAPS)
            emit(grad_d, TAPS, TAPS, TAPS)
        else:
            emit(grad_c, 0, 0, 2 * TAPS)

    by_role(body)


def kernel_f(got_m, got_e, act2_m, act2_e, act2_h, w, out, c3, kept):
    def body(leading):
        fill3(c3, 0, act2_h, 0, 2)
        fill3(c3, 2, act2_e, 0, 4)
        fill3(c3, 6, act2_m, 0, 6)
        fill3(c3, 12, act2_e, 4, 4)
        fill3(c3, 16, act2_h, 2, 2)
        kept[rows(0, 4), :] = got_e[rows(0, 4), :]
        kept[rows(4, 8), :] = got_m[...]
        kept[rows(12, 4), :] = got_e[rows(4, 4), :]

        def block(step):
            row = 4 * step
            total = conv(c3, row, 4, w, 0 if leading else 1, leading)
            out[rows(row, 4), :] = (total + kept[rows(row, 4), :].astype(F32)).astype(BF16)

        repeat(4, block)

    by_role(body)


def call(body, name, outs, scratch, args, row_units, limit=18):
    block = pl.BlockSpec(memory_space=pltpu.VMEM)
    return pl.pallas_call(
        body,
        out_shape=[jax.ShapeDtypeStruct(shape, dtype) for shape, dtype in outs],
        in_specs=[block] * len(args),
        out_specs=[block] * len(outs),
        scratch_shapes=[pltpu.VMEM(shape, dtype) for shape, dtype in scratch],
        compiler_params=pltpu.CompilerParams(vmem_limit_bytes=limit * MIB),
        cost_estimate=pl.CostEstimate(
            flops=int(row_units * 2 * COLS * TAPS * CH),
            bytes_accessed=4 * MIB,
            transcendentals=0,
        ),
        name=name,
    )(*args)


def body(arrivals, stashed, weights):
    arr = arrivals.reshape(-1, CH)
    sta = stashed.reshape(-1, CH)
    w = weights[0, 0]
    tile = arr.shape[0] // COLS
    space = lax.axis_size(SPACE)
    scale = 1.0 / math.sqrt(tile * space * COLS)

    def img(count, dtype=BF16):
        return ((count * COLS, CH), dtype)

    def img3(count):
        return ((count * COLS, 3 * CH), BF16)

    grad_shape = ((CH, 2 * TAPS), F32)

    two = 2 * COLS
    vmem = pl.BlockSpec(memory_space=pltpu.VMEM)
    edge = jax.ShapeDtypeStruct((2, two, CH), BF16)
    low, high, arr, sta, w = pl.pallas_call(
        kernel_load,
        out_shape=[edge, edge] + [jax.ShapeDtypeStruct(v.shape, BF16) for v in (arr, sta, w)],
        in_specs=[pl.BlockSpec(memory_space=pltpu.HBM)] * 3,
        out_specs=[vmem] * 5,
        scratch_shapes=[pltpu.SemaphoreType.DMA((8,))],
        compiler_params=pltpu.CompilerParams(vmem_limit_bytes=8 * MIB),
        name="load",
    )(arr, sta, w)
    ahead = [(i, i + 1) for i in range(space - 1)]
    back = [(j, i) for i, j in ahead]
    up = lax.ppermute(low, SPACE, ahead)
    down = lax.ppermute(high, SPACE, back)

    out_m, act_m, hid_m, slope_m = call(
        kernel_a,
        "first_middle",
        [img(8), img(10), img(10), img(10, F32)],
        [img3(12), img3(12), img3(10)],
        (arr, sta, w),
        28,
    )
    swap = [(0, 1), (1, 0)]
    got_m = lax.ppermute(out_m, "segment", swap)
    out_e, act_e, hid_e, slope_e = call(
        kernel_b,
        "first_edges",
        [img(8), img(8), img(8), img(8, F32)],
        [img3(12), img3(12), img3(12)],
        (arr, sta, up, down, act_m, w),
        24,
    )
    got_e = lax.ppermute(out_e, "segment", swap)
    both = ("segment",) + SPACE
    across_ahead = [((s * space + i), ((1 - s) * space + j)) for s in range(2) for i, j in ahead]
    across_back = [((s * space + i), ((1 - s) * space + j)) for s in range(2) for i, j in back]

    tail, head = out_e[-two:], out_e[:two]
    act2_m, grad_c = call(
        kernel_c,
        "second_middle",
        [img(6), grad_shape],
        [img3(8), img3(16), img3(16), img(18)],
        (got_m, arr, sta, up, down, act_m, act_e, hid_m, hid_e, slope_m, w),
        38,
    )
    act2_m, tail, head = lax.optimization_barrier((act2_m, tail, head))
    got_up = lax.ppermute(tail, both, across_ahead)
    got_down = lax.ppermute(head, both, across_back)
    act2_e, grad_d = call(
        kernel_d,
        "second_edges",
        [img(8), grad_shape],
        [img3(12), img3(8), img(12)],
        (got_m, got_e, sta, hid_m, hid_e, slope_m, slope_e, grad_c, w),
        24,
    )
    act2_h, send, keep = call(
        functools.partial(kernel_e, scale),
        "second_halo",
        [img(4), ((CH // 2, 2 * TAPS), BF16), ((CH // 2, 2 * TAPS), F32)],
        [img3(8), img3(2), img(6), ((CH, TAPS), F32)],
        (got_e, got_up, got_down, sta, up, down, slope_e, grad_c, grad_d, w),
        8,
    )
    (departing,) = call(
        kernel_f,
        "second_out",
        [img(16)],
        [img3(18), img(16)],
        (got_m, got_e, act2_m, act2_e, act2_h, w),
        16,
    )

    chips = space // 2
    share = CH // space
    other = lax.ppermute(send, "space_2", swap)
    pieces = (keep + other.astype(F32)).astype(BF16).reshape(chips, share, 2 * TAPS)
    pieces = lax.all_to_all(pieces, ("space_0", "space_1"), 0, 0, tiled=True)
    owned = jnp.sum(pieces.astype(F32), axis=0)
    owned, departing = lax.optimization_barrier((owned, departing))
    pairs = [(i, i ^ 3) for i in range(4)]
    partner = lax.ppermute(owned.astype(BF16), ("segment", "mirror"), pairs)
    combined = owned + partner.astype(F32)
    return (
        departing.reshape(arrivals.shape),
        combined.reshape(1, 1, share, 2, 3, 3, CH),
    )


def solution(mesh):
    split = Mesh(
        mesh.devices.reshape(mesh.shape["segment"], 4, 4, 2, mesh.shape["mirror"]),
        ("segment", "space_0", "space_1", "space_2", "mirror"),
    )
    in_specs = (
        P("mirror", "segment", SPACE, None, None),
        P("mirror", "segment", SPACE, None, None),
        P("mirror", "segment", None, None, None, None, None),
    )
    out_specs = (
        P("mirror", "segment", SPACE, None, None),
        P("mirror", "segment", SPACE, None, None, None, None),
    )
    return jax.shard_map(body, mesh=split, in_specs=in_specs, out_specs=out_specs, check_vma=False)
```

profile of v0, /device:TPU:0, one launch (start us, length us, event | category | flops | bytes accessed | tf_op | source)
XLA Modules:
  0.0 97.9 jit_solution(3841620218852965648)
XLA Ops:
  0.6 1.7 %copy-done = bf16[1,1,2,3,3,256,256]{6,5,4,3,2,1,0:T(8,128)(2,1)S(1)} copy-done((bf16[1,1,2,3,3,256,256]{6,5,4,3,2,1,0:T(8,128)(2,1)S(1)}, bf16[1,1,2,3,3,256,256]{6,5,4,3,2,1,0:T(8,128)(2,1)}, u32[]{:S(2)}) %copy-start) | copy-done | bytes 2359320
  2.3 1.2 %copy-done.1 = bf16[1,1,16,128,256]{4,3,2,1,0:T(8,128)(2,1)S(1)} copy-done((bf16[1,1,16,128,256]{4,3,2,1,0:T(8,128)(2,1)S(1)}, bf16[1,1,16,128,256]{4,3,2,1,0:T(8,128)(2,1)}, u32[]{:S(2)}) %copy-start.1) | copy-done | bytes 1048600
  3.5 1.2 %copy-done.2 = bf16[1,1,16,128,256]{4,3,2,1,0:T(8,128)(2,1)S(1)} copy-done((bf16[1,1,16,128,256]{4,3,2,1,0:T(8,128)(2,1)S(1)}, bf16[1,1,16,128,256]{4,3,2,1,0:T(8,128)(2,1)}, u32[]{:S(2)}) %copy-start.2) | copy-done | bytes 1048600
  4.7 1.3 %load.1 = (bf16[2,256,256]{2,1,0:T(8,128)(2,1)S(1)}, bf16[2,256,256]{2,1,0:T(8,128)(2,1)S(1)}, bf16[2048,256]{1,0:T(8,128)(2,1)S(1)}, bf16[2048,256]{1,0:T(8,128)(2,1)S(1)}, bf16[2,3,3,256,256]{4,3,2,1,0:T(8,128)(2,1)S(1)}) custom-call(bf16[2048,256]{1,0:T(8,128)(2,1)S(1)} %bitcast.7, bf16[2048,256]{1,0:T(8,128)(2,1)S(1)} %bitcast.8, ...), custom_call_target="tpu_custom_call" | custom-call | tf_op jit(solution)/shard_map/load/pallas_call | solution.py:400
  6.1 1.3 %collective-permute-start = (bf16[2,256,256]{2,1,0:T(8,128)(2,1)S(1)}, bf16[2,256,256]{2,1,0:T(8,128)(2,1)S(1)}, u32[]{:S(2)}, u32[]{:S(2)}) collective-permute-start(bf16[2,256,256]{2,1,0:T(8,128)(2,1)S(1)} %get-tuple-element.29), channel_id=1, source_target_pairs={{0,2},{2,4},{4,6},{6,8},{8,10},{10,12},{12,14},{14,16},{16,18},{18... | collective-permute-start | bytes 786440 | tf_op jit(solution)/shard_map/ppermute | solution.py:411
  7.4 1.3 %collective-permute-start.1 = (bf16[2,256,256]{2,1,0:T(8,128)(2,1)S(1)}, bf16[2,256,256]{2,1,0:T(8,128)(2,1)S(1)}, u32[]{:S(2)}, u32[]{:S(2)}) collective-permute-start(bf16[2,256,256]{2,1,0:T(8,128)(2,1)S(1)} %get-tuple-element.30), channel_id=1, source_target_pairs={{2,0},{4,2},{6,4},{8,6},{10,8},{12,10},{14,12},{16,14},{18,16},{20... | collective-permute-start | bytes 786440 | tf_op jit(solution)/shard_map/ppermute | solution.py:412
  8.7 6.1 %first_middle.1 = (bf16[1024,256]{1,0:T(8,128)(2,1)S(1)}, bf16[1280,256]{1,0:T(8,128)(2,1)S(1)}, bf16[1280,256]{1,0:T(8,128)(2,1)S(1)}, f32[1280,256]{1,0:T(8,128)S(1)}) custom-call(bf16[2048,256]{1,0:T(8,128)(2,1)S(1)} %get-tuple-element.27.arr, bf16[2048,256]{1,0:T(8,128)(2,1)S(1)} %get-tuple-element.28.sta, ...), custom_call_target="tpu_custom_call" | custom-call | flops 4227858432 | bytes 4194304 | tf_op jit(solution)/shard_map/first_middle/pallas_call | solution.py:365
  14.8 2.2 %collective-permute-start.3 = (bf16[1024,256]{1,0:T(8,128)(2,1)S(1)}, bf16[1024,256]{1,0:T(8,128)(2,1)S(1)}, u32[]{:S(2)}, u32[]{:S(2)}) collective-permute-start(bf16[1024,256]{1,0:T(8,128)(2,1)S(1)} %get-tuple-element.34), channel_id=1, source_target_pairs={{0,64},{64,0},{1,65},{65,1},{2,66},{66,2},{3,67},{67,3},{4,68},{68... | collective-permute-start | bytes 1572872 | tf_op jit(solution)/shard_map/ppermute | solution.py:423
  17.0 5.4 %first_edges.1 = (bf16[1024,256]{1,0:T(8,128)(2,1)S(1)}, bf16[1024,256]{1,0:T(8,128)(2,1)S(1)}, bf16[1024,256]{1,0:T(8,128)(2,1)S(1)}, f32[1024,256]{1,0:T(8,128)S(1)}) custom-call(bf16[2048,256]{1,0:T(8,128)(2,1)S(1)} %get-tuple-element.27.arr, bf16[2048,256]{1,0:T(8,128)(2,1)S(1)} %get-tuple-element.28.sta, ...), custom_call_target="tpu_custom_call" | custom-call | flops 3623878656 | bytes 4194304 | tf_op jit(solution)/shard_map/first_edges/pallas_call | solution.py:365
  22.6 4.9 %collective-permute-done.3.got_m = bf16[1024,256]{1,0:T(8,128)(2,1)S(1)} collective-permute-done((bf16[1024,256]{1,0:T(8,128)(2,1)S(1)}, bf16[1024,256]{1,0:T(8,128)(2,1)S(1)}, u32[]{:S(2)}, u32[]{:S(2)}) %collective-permute-start.3) | collective-permute-done | bytes 524320 | tf_op jit(solution)/shard_map/ppermute | solution.py:423
  27.5 4.4 %second_middle.1 = (bf16[768,256]{1,0:T(8,128)(2,1)S(1)}, f32[256,4608]{1,0:T(8,128)S(1)}) custom-call(bf16[1024,256]{1,0:T(8,128)(2,1)S(1)} %collective-permute-done.3.got_m, bf16[2048,256]{1,0:T(8,128)(2,1)S(1)} %get-tuple-element.27.arr, bf16[2048,256]{1,0:T(8,128)(2,1)S(1)} %get-tuple-element.28.sta, bf16[2,256,256]{2,1,0:T(8,128)(2,1)S(1)} %collective-permute-done.up, ...), custom_call_target="tpu_custom_call" | custom-call | flops 5737807872 | bytes 4194304 | tf_op jit(solution)/shard_map/second_middle/pallas_call | solution.py:365
  31.9 11.9 %collective-permute-start.4 = (bf16[256,256]{1,0:T(8,128)(2,1)S(1)}, bf16[256,256]{1,0:T(8,128)(2,1)S(1)}, u32[]{:S(2)}, u32[]{:S(2)}) collective-permute-start(bf16[256,256]{1,0:T(8,128)(2,1)S(1)} %get-tuple-element.40), channel_id=1, source_target_pairs={{0,66},{2,68},{4,70},{6,72},{8,74},{10,76},{12,78},{14,80},{16,82}... | collective-permute-start | bytes 393224 | tf_op jit(solution)/shard_map/ppermute | solution.py:447
  43.8 1.3 %collective-permute-start.5 = (bf16[256,256]{1,0:T(8,128)(2,1)S(1)}, bf16[256,256]{1,0:T(8,128)(2,1)S(1)}, u32[]{:S(2)}, u32[]{:S(2)}) collective-permute-start(bf16[256,256]{1,0:T(8,128)(2,1)S(1)} %get-tuple-element.41), channel_id=1, source_target_pairs={{2,64},{4,66},{6,68},{8,70},{10,72},{12,74},{14,76},{16,78},{18,80... | collective-permute-start | bytes 393224 | tf_op jit(solution)/shard_map/ppermute | solution.py:448
  45.2 4.2 %second_edges.1 = (bf16[1024,256]{1,0:T(8,128)(2,1)S(1)}, f32[256,4608]{1,0:T(8,128)S(1)}) custom-call(bf16[1024,256]{1,0:T(8,128)(2,1)S(1)} %collective-permute-done.3.got_m, bf16[1024,256]{1,0:T(8,128)(2,1)S(1)} %collective-permute-done.2.got_e, bf16[2048,256]{1,0:T(8,128)(2,1)S(1)} %get-tuple-element.28.sta, ...), custom_call_target="tpu_custom_call" | custom-call | flops 3623878656 | bytes 4194304 | tf_op jit(solution)/shard_map/second_edges/pallas_call | solution.py:365
  50.1 2.0 %second_halo.1 = (bf16[512,256]{1,0:T(8,128)(2,1)S(1)}, bf16[128,4608]{1,0:T(8,128)(2,1)S(1)}, f32[128,4608]{1,0:T(8,128)S(1)}) custom-call(bf16[1024,256]{1,0:T(8,128)(2,1)S(1)} %collective-permute-done.2.got_e, bf16[256,256]{1,0:T(8,128)(2,1)S(1)} %collective-permute-done.4.got_up, bf16[256,256]{1,0:T(8,128)(2,1)S(1)} %collective-permute-done.5.got_down, ...), custom_call_target="tpu_custom_call" | custom-call | flops 1207959552 | bytes 4194304 | tf_op jit(solution)/shard_map/second_halo/pallas_call | solution.py:365
  52.9 3.3 %collective-permute-start.6 = (bf16[128,4608]{1,0:T(8,128)(2,1)S(1)}, bf16[128,4608]{1,0:T(8,128)(2,1)S(1)}, u32[]{:S(2)}, u32[]{:S(2)}) collective-permute-start(bf16[128,4608]{1,0:T(8,128)(2,1)S(1)} %get-tuple-element.46), channel_id=1, source_target_pairs={{0,2},{2,0},{1,3},{3,1},{4,6},{6,4},{5,7},{7,5},{8,10},{10,8},{9,1... | collective-permute-start | bytes 3538952 | tf_op jit(solution)/shard_map/ppermute | solution.py:476
  56.2 2.5 %collective-permute-done.6 = bf16[128,4608]{1,0:T(8,128)(2,1)S(1)} collective-permute-done((bf16[128,4608]{1,0:T(8,128)(2,1)S(1)}, bf16[128,4608]{1,0:T(8,128)(2,1)S(1)}, u32[]{:S(2)}, u32[]{:S(2)}) %collective-permute-start.6) | collective-permute-done | bytes 1179680 | tf_op jit(solution)/shard_map/ppermute | solution.py:476
  58.7 1.3 %fusion = bf16[16,8,4608]{2,1,0:T(8,128)(2,1)} fusion(f32[128,4608]{1,0:T(8,128)S(1)} %get-tuple-element.45, bf16[128,4608]{1,0:T(8,128)(2,1)S(1)} %collective-permute-done.6), kind=kLoop, calls=%fused_computation.2 | loop fusion | flops 1769472 | bytes 4718592 | tf_op jit(solution)/shard_map/reshape | solution.py:477
  59.9 10.1 %all-to-all-start = ((bf16[16,8,4608]{2,1,0:T(8,128)(2,1)}), bf16[16,8,4608]{2,1,0:T(8,128)(2,1)}, u32[]{:S(2)}, u32[]{:S(2)}) async-start(bf16[16,8,4608]{2,1,0:T(8,128)(2,1)} %fusion), calls=%async_computation | async-start | bytes 2359296 | tf_op jit(solution)/shard_map/all_to_all | solution.py:478
  73.0 4.8 %second_out.1 = bf16[2048,256]{1,0:T(8,128)(2,1)} custom-call(bf16[1024,256]{1,0:T(8,128)(2,1)S(1)} %collective-permute-done.3.got_m, bf16[1024,256]{1,0:T(8,128)(2,1)S(1)} %collective-permute-done.2.got_e, bf16[768,256]{1,0:T(8,128)(2,1)S(1)} %copy-done.8, bf16[1024,256]{1,0:T(8,128)(2,1)S(1)} %copy-done.6, bf16[512,256]{1,0:T(8,128)(2,1)S(1)} %copy-done.4, ...), custom_call_target="tpu_custom_call" | custom-call | flops 2415919104 | bytes 4194304 | tf_op jit(solution)/shard_map/second_out/pallas_call | solution.py:365
  77.7 12.2 %all-to-all-done = bf16[16,8,4608]{2,1,0:T(8,128)(2,1)} async-done(((bf16[16,8,4608]{2,1,0:T(8,128)(2,1)}), bf16[16,8,4608]{2,1,0:T(8,128)(2,1)}, u32[]{:S(2)}, u32[]{:S(2)}) %all-to-all-start) | async-done | bytes 1179680 | tf_op jit(solution)/shard_map/all_to_all | solution.py:478
  89.9 1.4 %convert_reduce_fusion = f32[8,4608]{1,0:T(8,128)S(1)} fusion(bf16[16,8,4608]{2,1,0:T(8,128)(2,1)} %all-to-all-done), kind=kLoop, calls=%fused_computation | loop fusion | flops 1142784 | bytes 1327104 | tf_op jit(solution)/shard_map/reduce_sum | solution.py:479
  91.3 2.3 %collective-permute-start.7 = (bf16[8,4608]{1,0:T(8,128)(2,1)S(1)}, bf16[8,4608]{1,0:T(8,128)(2,1)S(1)}, u32[]{:S(2)}, u32[]{:S(2)}) collective-permute-start(bf16[8,4608]{1,0:T(8,128)(2,1)S(1)} %convert_element_type.18), channel_id=1, source_target_pairs={{0,65},{1,64},{64,1},{65,0},{2,67},{3,66},{66,3},{67,2},{4,69},{5,... | collective-permute-start | bytes 221192 | tf_op jit(solution)/shard_map/ppermute | solution.py:482
  93.6 3.4 %collective-permute-done.7 = bf16[8,4608]{1,0:T(8,128)(2,1)S(1)} collective-permute-done((bf16[8,4608]{1,0:T(8,128)(2,1)S(1)}, bf16[8,4608]{1,0:T(8,128)(2,1)S(1)}, u32[]{:S(2)}, u32[]{:S(2)}) %collective-permute-start.7) | collective-permute-done | bytes 73760 | tf_op jit(solution)/shard_map/ppermute | solution.py:482
  (26 shorter events, 5.5 us)
Async XLA Ops:
  0.6 1.7 %copy-start = (bf16[1,1,2,3,3,256,256]{6,5,4,3,2,1,0:T(8,128)(2,1)S(1)}, bf16[1,1,2,3,3,256,256]{6,5,4,3,2,1,0:T(8,128)(2,1)}, u32[]{:S(2)}) copy-start(bf16[1,1,2,3,3,256,256]{6,5,4,3,2,1,0:T(8,128)(2,1)} %param.5) | copy-start | bytes 7077892
  2.3 1.2 %copy-start.1 = (bf16[1,1,16,128,256]{4,3,2,1,0:T(8,128)(2,1)S(1)}, bf16[1,1,16,128,256]{4,3,2,1,0:T(8,128)(2,1)}, u32[]{:S(2)}) copy-start(bf16[1,1,16,128,256]{4,3,2,1,0:T(8,128)(2,1)} %param.3) | copy-start | bytes 3145732
  3.5 1.2 %copy-start.2 = (bf16[1,1,16,128,256]{4,3,2,1,0:T(8,128)(2,1)S(1)}, bf16[1,1,16,128,256]{4,3,2,1,0:T(8,128)(2,1)}, u32[]{:S(2)}) copy-start(bf16[1,1,16,128,256]{4,3,2,1,0:T(8,128)(2,1)} %param.4) | copy-start | bytes 3145732
  6.1 10.9 %collective-permute-start = (bf16[2,256,256]{2,1,0:T(8,128)(2,1)S(1)}, bf16[2,256,256]{2,1,0:T(8,128)(2,1)S(1)}, u32[]{:S(2)}, u32[]{:S(2)}) collective-permute-start(bf16[2,256,256]{2,1,0:T(8,128)(2,1)S(1)} %get-tuple-element.29), channel_id=1, source_target_pairs={{0,2},{2,4},{4,6},{6,8},{8,10},{10,12},{12,14},{14,16},{16,18},{18... | collective-permute-start | bytes 786440 | tf_op jit(solution)/shard_map/ppermute | solution.py:411
  7.4 9.6 %collective-permute-start.1 = (bf16[2,256,256]{2,1,0:T(8,128)(2,1)S(1)}, bf16[2,256,256]{2,1,0:T(8,128)(2,1)S(1)}, u32[]{:S(2)}, u32[]{:S(2)}) collective-permute-start(bf16[2,256,256]{2,1,0:T(8,128)(2,1)S(1)} %get-tuple-element.30), channel_id=1, source_target_pairs={{2,0},{4,2},{6,4},{8,6},{10,8},{12,10},{14,12},{16,14},{18,16},{20... | collective-permute-start | bytes 786440 | tf_op jit(solution)/shard_map/ppermute | solution.py:412
  14.8 12.6 %collective-permute-start.3 = (bf16[1024,256]{1,0:T(8,128)(2,1)S(1)}, bf16[1024,256]{1,0:T(8,128)(2,1)S(1)}, u32[]{:S(2)}, u32[]{:S(2)}) collective-permute-start(bf16[1024,256]{1,0:T(8,128)(2,1)S(1)} %get-tuple-element.34), channel_id=1, source_target_pairs={{0,64},{64,0},{1,65},{65,1},{2,66},{66,2},{3,67},{67,3},{4,68},{68... | collective-permute-start | bytes 1572872 | tf_op jit(solution)/shard_map/ppermute | solution.py:423
  22.4 22.7 %collective-permute-start.2 = (bf16[1024,256]{1,0:T(8,128)(2,1)S(1)}, bf16[1024,256]{1,0:T(8,128)(2,1)S(1)}, u32[]{:S(2)}, u32[]{:S(2)}) collective-permute-start(bf16[1024,256]{1,0:T(8,128)(2,1)S(1)} %get-tuple-element.33), channel_id=1, source_target_pairs={{0,64},{64,0},{1,65},{65,1},{2,66},{66,2},{3,67},{67,3},{4,68},{68... | collective-permute-start | bytes 1572872 | tf_op jit(solution)/shard_map/ppermute | solution.py:432
  31.9 17.4 %copy-start.7 = (bf16[768,256]{1,0:T(8,128)(2,1)}, bf16[768,256]{1,0:T(8,128)(2,1)S(1)}, u32[]{:S(2)}) copy-start(bf16[768,256]{1,0:T(8,128)(2,1)S(1)} %get-tuple-element.47.act2_m) | copy-start | bytes 1179652
  31.9 17.4 %collective-permute-start.4 = (bf16[256,256]{1,0:T(8,128)(2,1)S(1)}, bf16[256,256]{1,0:T(8,128)(2,1)S(1)}, u32[]{:S(2)}, u32[]{:S(2)}) collective-permute-start(bf16[256,256]{1,0:T(8,128)(2,1)S(1)} %get-tuple-element.40), channel_id=1, source_target_pairs={{0,66},{2,68},{4,70},{6,72},{8,74},{10,76},{12,78},{14,80},{16,82}... | collective-permute-start | bytes 393224 | tf_op jit(solution)/shard_map/ppermute | solution.py:447
  43.8 6.3 %collective-permute-start.5 = (bf16[256,256]{1,0:T(8,128)(2,1)S(1)}, bf16[256,256]{1,0:T(8,128)(2,1)S(1)}, u32[]{:S(2)}, u32[]{:S(2)}) collective-permute-start(bf16[256,256]{1,0:T(8,128)(2,1)S(1)} %get-tuple-element.41), channel_id=1, source_target_pairs={{2,64},{4,66},{6,68},{8,70},{10,72},{12,74},{14,76},{16,78},{18,80... | collective-permute-start | bytes 393224 | tf_op jit(solution)/shard_map/ppermute | solution.py:448
  49.3 2.8 %copy-start.5 = (bf16[1024,256]{1,0:T(8,128)(2,1)}, bf16[1024,256]{1,0:T(8,128)(2,1)S(1)}, u32[]{:S(2)}) copy-start(bf16[1024,256]{1,0:T(8,128)(2,1)S(1)} %get-tuple-element.48.act2_e) | copy-start | bytes 1572868
  52.2 0.7 copy-start.3
  52.9 5.8 %collective-permute-start.6 = (bf16[128,4608]{1,0:T(8,128)(2,1)S(1)}, bf16[128,4608]{1,0:T(8,128)(2,1)S(1)}, u32[]{:S(2)}, u32[]{:S(2)}) collective-permute-start(bf16[128,4608]{1,0:T(8,128)(2,1)S(1)} %get-tuple-element.46), channel_id=1, source_target_pairs={{0,2},{2,0},{1,3},{3,1},{4,6},{6,4},{5,7},{7,5},{8,10},{10,8},{9,1... | collective-permute-start | bytes 3538952 | tf_op jit(solution)/shard_map/ppermute | solution.py:476
  59.9 30.0 %all-to-all-start = ((bf16[16,8,4608]{2,1,0:T(8,128)(2,1)}), bf16[16,8,4608]{2,1,0:T(8,128)(2,1)}, u32[]{:S(2)}, u32[]{:S(2)}) async-start(bf16[16,8,4608]{2,1,0:T(8,128)(2,1)} %fusion), calls=%async_computation | async-start | bytes 2359296 | tf_op jit(solution)/shard_map/all_to_all | solution.py:478
  70.0 1.0 copy-start.4
  70.9 1.0 %copy-start.6 = (bf16[1024,256]{1,0:T(8,128)(2,1)S(1)}, bf16[1024,256]{1,0:T(8,128)(2,1)}, u32[]{:S(2)}) copy-start(bf16[1024,256]{1,0:T(8,128)(2,1)} %copy-done.5) | copy-start | bytes 1572868
  72.0 1.0 %copy-start.8 = (bf16[768,256]{1,0:T(8,128)(2,1)S(1)}, bf16[768,256]{1,0:T(8,128)(2,1)}, u32[]{:S(2)}) copy-start(bf16[768,256]{1,0:T(8,128)(2,1)} %copy-done.7) | copy-start | bytes 1179652
  91.3 5.6 %collective-permute-start.7 = (bf16[8,4608]{1,0:T(8,128)(2,1)S(1)}, bf16[8,4608]{1,0:T(8,128)(2,1)S(1)}, u32[]{:S(2)}, u32[]{:S(2)}) collective-permute-start(bf16[8,4608]{1,0:T(8,128)(2,1)S(1)} %convert_element_type.18), channel_id=1, source_target_pairs={{0,65},{1,64},{64,1},{65,0},{2,67},{3,66},{66,3},{67,2},{4,69},{5,... | collective-permute-start | bytes 221192 | tf_op jit(solution)/shard_map/ppermute | solution.py:482
where the time goes:
time: 98.4 us; the launch traced here: 97.9 us
  starting transfers between devices  33.7 us (34%)
  Pallas kernels  28.2 us (29%)
  waiting for transfers between devices  23.7 us (24%)
  local copies, waits for them, and re-layouts  8.68 us (9%)
  other arithmetic  2.72 us (3%)
    pallas_call x6, Pallas kernels, call(): pl.pallas_call(body, out_shape=[jax.ShapeDtypeStruct(shape, dtype) for sh...  26.9 us
    all_to_all x1, waiting for transfers between devices, body(): pieces = lax.all_to_all(pieces, ('space_0', 'space_1'), 0, 0, tiled=True)  12.2 us
    ppermute x1, starting transfers between devices, body(): got_up = lax.ppermute(tail, both, across_ahead)  11.9 us
    all_to_all x1, starting transfers between devices, body(): pieces = lax.all_to_all(pieces, ('space_0', 'space_1'), 0, 0, tiled=True)  10.1 us
    unnamed x19, local copies, waits for them, and re-layouts  8.55 us
    ppermute x1, waiting for transfers between devices, body(): got_m = lax.ppermute(out_m, 'segment', swap)  4.9 us
    ppermute x1, waiting for transfers between devices, body(): partner = lax.ppermute(owned.astype(BF16), ('segment', 'mirror'), pairs)  3.38 us
    ppermute x1, starting transfers between devices, body(): other = lax.ppermute(send, 'space_2', swap)  3.31 us
  transfers between devices with their start and end apart: 9, of which 5 were waited for; matrix products, arithmetic and copies ran while one was open for 0% of the time, Pallas kernels for 25%

commit v1 on v0

--- a/solution.py
+++ b/solution.py
@@ -16,6 +16,7 @@
 CH = 256
 TAPS = 9 * CH
 MIB = 1 << 20
+LIMIT_A = 49
 
 
 def rows(first, count):
@@ -116,30 +117,32 @@
     return (place > 0).astype(F32), (place < count - 1).astype(F32)
 
 
-def kernel_load(arr_hbm, sta_hbm, w_hbm, low, high, arr, sta, w, sems):
+def kernel_a(
+    arr_hbm, sta_hbm, w_hbm, out_m, act_m, hid_m, slope_m, low, high, arr, sta, s3, a3, c3, w, sems
+):
     two = 2 * COLS
     size = arr_hbm.shape[0]
     moves = (
+        (sta_hbm, sta),
+        (arr_hbm, arr),
+        (w_hbm.at[0], w.at[0]),
+        (w_hbm.at[1], w.at[1]),
         (arr_hbm.at[pl.ds(size - two, two)], low.at[0]),
         (sta_hbm.at[pl.ds(size - two, two)], low.at[1]),
         (arr_hbm.at[pl.ds(0, two)], high.at[0]),
         (sta_hbm.at[pl.ds(0, two)], high.at[1]),
-        (w_hbm.at[0], w.at[0]),
-        (sta_hbm, sta),
-        (arr_hbm, arr),
-        (w_hbm.at[1], w.at[1]),
     )
     copies = [pltpu.make_async_copy(src, dst, sems.at[i]) for i, (src, dst) in enumerate(moves)]
     for copy in copies:
         copy.start()
-    for copy in copies:
+    copies[0].wait()
+    fill3(s3, 0, sta, 2, 12)
+    copies[1].wait()
+    fill3(a3, 0, arr, 2, 12)
+    for copy in copies[2:]:
         copy.wait()
 
-
-def kernel_a(arr, sta, w, out_m, act_m, hid_m, slope_m, s3, a3, c3):
-    def body(leading):
-        fill3(s3, 0, sta, 2, 12)
-        fill3(a3, 0, arr, 2, 12)
+    def body(leading):
 
         def inner(step):
             row = 5 * step
@@ -159,8 +162,10 @@
             total = conv(c3, row, 4, w, 1 if leading else 0, not leading)
             out_m[rows(row, 4), :] = (total + arr[rows(4 + row, 4), :].astype(F32)).astype(BF16)
 
-        repeat(2, inner)
-        repeat(2, last)
+        for step in range(2):
+            inner(step)
+        for step in range(2):
+            last(step)
 
     by_role(body)
 
@@ -360,14 +365,15 @@
     by_role(body)
 
 
-def call(body, name, outs, scratch, args, row_units, limit=18):
+def call(body, name, outs, scratch, args, row_units, limit=18, space=pltpu.VMEM, sems=0):
     block = pl.BlockSpec(memory_space=pltpu.VMEM)
+    semaphores = [pltpu.SemaphoreType.DMA((sems,))] if sems else []
     return pl.pallas_call(
         body,
         out_shape=[jax.ShapeDtypeStruct(shape, dtype) for shape, dtype in outs],
-        in_specs=[block] * len(args),
+        in_specs=[pl.BlockSpec(memory_space=space)] * len(args),
         out_specs=[block] * len(outs),
-        scratch_shapes=[pltpu.VMEM(shape, dtype) for shape, dtype in scratch],
+        scratch_shapes=[pltpu.VMEM(shape, dtype) for shape, dtype in scratch] + semaphores,
         compiler_params=pltpu.CompilerParams(vmem_limit_bytes=limit * MIB),
         cost_estimate=pl.CostEstimate(
             flops=int(row_units * 2 * COLS * TAPS * CH),
@@ -395,32 +401,25 @@
     grad_shape = ((CH, 2 * TAPS), F32)
 
     two = 2 * COLS
-    vmem = pl.BlockSpec(memory_space=pltpu.VMEM)
-    edge = jax.ShapeDtypeStruct((2, two, CH), BF16)
-    low, high, arr, sta, w = pl.pallas_call(
-        kernel_load,
-        out_shape=[edge, edge] + [jax.ShapeDtypeStruct(v.shape, BF16) for v in (arr, sta, w)],
-        in_specs=[pl.BlockSpec(memory_space=pltpu.HBM)] * 3,
-        out_specs=[vmem] * 5,
-        scratch_shapes=[pltpu.SemaphoreType.DMA((8,))],
-        compiler_params=pltpu.CompilerParams(vmem_limit_bytes=8 * MIB),
-        name="load",
-    )(arr, sta, w)
+    edge = ((2, two, CH), BF16)
+    out_m, act_m, hid_m, slope_m, low, high, arr, sta = call(
+        kernel_a,
+        "first_middle",
+        [img(8), img(10), img(10), img(10, F32), edge, edge, img(16), img(16)],
+        [img3(12), img3(12), img3(10), (w.shape, BF16)],
+        (arr, sta, w),
+        28,
+        limit=LIMIT_A,
+        space=pltpu.HBM,
+        sems=8,
+    )
     ahead = [(i, i + 1) for i in range(space - 1)]
     back = [(j, i) for i, j in ahead]
+    swap = [(0, 1), (1, 0)]
+    got_m = lax.ppermute(out_m, "segment", swap)
+    act_m, low, high = lax.optimization_barrier((act_m, low, high))
     up = lax.ppermute(low, SPACE, ahead)
     down = lax.ppermute(high, SPACE, back)
-
-    out_m, act_m, hid_m, slope_m = call(
-        kernel_a,
-        "first_middle",
-        [img(8), img(10), img(10), img(10, F32)],
-        [img3(12), img3(12), img3(10)],
-        (arr, sta, w),
-        28,
-    )
-    swap = [(0, 1), (1, 0)]
-    got_m = lax.ppermute(out_m, "segment", swap)
     out_e, act_e, hid_e, slope_e = call(
         kernel_b,
         "first_edges",
@@ -430,11 +429,6 @@
         24,
     )
     got_e = lax.ppermute(out_e, "segment", swap)
-    both = ("segment",) + SPACE
-    across_ahead = [((s * space + i), ((1 - s) * space + j)) for s in range(2) for i, j in ahead]
-    across_back = [((s * space + i), ((1 - s) * space + j)) for s in range(2) for i, j in back]
-
-    tail, head = out_e[-two:], out_e[:two]
     act2_m, grad_c = call(
         kernel_c,
         "second_middle",
@@ -443,9 +437,8 @@
         (got_m, arr, sta, up, down, act_m, act_e, hid_m, hid_e, slope_m, w),
         38,
     )
-    act2_m, tail, head = lax.optimization_barrier((act2_m, tail, head))
-    got_up = lax.ppermute(tail, both, across_ahead)
-    got_down = lax.ppermute(head, both, across_back)
+    got_up = lax.ppermute(got_e[-two:], SPACE, ahead)
+    got_down = lax.ppermute(got_e[:two], SPACE, back)
     act2_e, grad_d = call(
         kernel_d,
         "second_edges",

time: 98.4 us -> 93.3 us (0.948)
  starting transfers between devices: 33.7 us -> 28.1 us
  local copies, waits for them, and re-layouts: 8.68 us -> 4.58 us
  waiting for transfers between devices: 23.7 us -> 27.5 us
    ppermute x2, starting transfers between devices: 13.2 us -> 6.02 us  [the longest x1 4.73 us: body(): got_up = lax.ppermute(got_e[-two:], SPACE, ahead)]
    ppermute x1, waiting for transfers between devices: 0.01 us -> 6.73 us  [body(): got_e = lax.ppermute(out_e, 'segment', swap)]
    unnamed x19 -> x17, local copies, waits for them, and re-layouts: 8.55 us -> 4.45 us
    ppermute x1, waiting for transfers between devices: 4.9 us -> 1.42 us  [body(): got_m = lax.ppermute(out_m, 'segment', swap)]
    pallas_call x6, Pallas kernels: 26.9 us -> 29.1 us  [call(): pl.pallas_call(body, out_shape=[jax.ShapeDtypeStruct(shape, dtype) for sh...]
    ppermute x1, waiting for transfers between devices: 0.01 us -> 2.19 us  [body(): down = lax.ppermute(high, SPACE, back)]
    all_to_all x1, starting transfers between devices: 10.1 us -> 8.52 us  [body(): pieces = lax.all_to_all(pieces, ('space_0', 'space_1'), 0, 0, tiled=True)]
    pallas_call x1 -> x0, Pallas kernels: 1.35 us -> none  [body(): pl.pallas_call(kernel_load, out_shape=[edge, edge] + [jax.ShapeDtypeStruc...]
  transfers between devices with their start and end apart: 9 -> 9, of which waited for: 5 -> 6; matrix products, arithmetic and copies ran while one was open for 0% -> 0% of each run, Pallas kernels for 25% -> 20%
where the time goes in v1:
time: 93.3 us; the launch traced here: 92.9 us
  Pallas kernels  29.1 us (31%)
  starting transfers between devices  28.1 us (30%)
  waiting for transfers between devices  27.5 us (29%)
  local copies, waits for them, and re-layouts  4.58 us (5%)
  other arithmetic  2.71 us (3%)
    pallas_call x6, Pallas kernels, call(): pl.pallas_call(body, out_shape=[jax.ShapeDtypeStruct(shape, dtype) for sh...  29.1 us
    all_to_all x1, waiting for transfers between devices, body(): pieces = lax.all_to_all(pieces, ('space_0', 'space_1'), 0, 0, tiled=True)  12.2 us
    all_to_all x1, starting transfers between devices, body(): pieces = lax.all_to_all(pieces, ('space_0', 'space_1'), 0, 0, tiled=True)  8.52 us
    ppermute x1, waiting for transfers between devices, body(): got_e = lax.ppermute(out_e, 'segment', swap)  6.73 us
    ppermute x1, starting transfers between devices, body(): got_up = lax.ppermute(got_e[-two:], SPACE, ahead)  4.73 us
    unnamed x17, local copies, waits for them, and re-layouts  4.45 us
    ppermute x1, starting transfers between devices, body(): other = lax.ppermute(send, 'space_2', swap)  4.3 us
    ppermute x1, starting transfers between devices, body(): partner = lax.ppermute(owned.astype(BF16), ('segment', 'mirror'), pairs)  3.1 us
  transfers between devices with their start and end apart: 9, of which 6 were waited for; matrix products, arithmetic and copies ran while one was open for 0% of the time, Pallas kernels for 20%

profile of v1, /device:TPU:0, one launch (start us, length us, event | category | flops | bytes accessed | tf_op | source)
XLA Modules:
  0.0 92.9 jit_solution(15174474929269611837)
XLA Ops:
  0.6 8.3 %first_middle.1 = (bf16[1024,256]{1,0:T(8,128)(2,1)S(1)}, bf16[1280,256]{1,0:T(8,128)(2,1)S(1)}, bf16[1280,256]{1,0:T(8,128)(2,1)S(1)}, f32[1280,256]{1,0:T(8,12...) custom-call(bf16[2048,256]{1,0:T(8,128)(2,1)} %bitcast.12, ...), custom_call_target="tpu_custom_call" | custom-call | flops 4227858432 | bytes 4194304 | tf_op jit(solution)/shard_map/first_middle/pallas_call | solution.py:371
  9.0 1.3 %collective-permute-start = (bf16[2,256,256]{2,1,0:T(8,128)(2,1)S(1)}, bf16[2,256,256]{2,1,0:T(8,128)(2,1)S(1)}, u32[]{:S(2)}, u32[]{:S(2)}) collective-permute-start(bf16[2,256,256]{2,1,0:T(8,128)(2,1)S(1)} %get-tuple-element.31), channel_id=1, source_target_pairs={{0,2},{2,4},{4,6},{6,8},{8,10},{10,12},{12,14},{14,16},{16,18},{18... | collective-permute-start | bytes 786440 | tf_op jit(solution)/shard_map/ppermute | solution.py:421
  10.3 1.3 %collective-permute-start.1 = (bf16[2,256,256]{2,1,0:T(8,128)(2,1)S(1)}, bf16[2,256,256]{2,1,0:T(8,128)(2,1)S(1)}, u32[]{:S(2)}, u32[]{:S(2)}) collective-permute-start(bf16[2,256,256]{2,1,0:T(8,128)(2,1)S(1)} %get-tuple-element.32), channel_id=1, source_target_pairs={{2,0},{4,2},{6,4},{8,6},{10,8},{12,10},{14,12},{16,14},{18,16},{20... | collective-permute-start | bytes 786440 | tf_op jit(solution)/shard_map/ppermute | solution.py:422
  11.6 2.2 %collective-permute-start.5 = (bf16[1024,256]{1,0:T(8,128)(2,1)S(1)}, bf16[1024,256]{1,0:T(8,128)(2,1)S(1)}, u32[]{:S(2)}, u32[]{:S(2)}) collective-permute-start(bf16[1024,256]{1,0:T(8,128)(2,1)S(1)} %get-tuple-element.36), channel_id=1, source_target_pairs={{0,64},{64,0},{1,65},{65,1},{2,66},{66,2},{3,67},{67,3},{4,68},{68... | collective-permute-start | bytes 1572872 | tf_op jit(solution)/shard_map/ppermute | solution.py:419
  13.8 2.2 %collective-permute-done.1.down = bf16[2,256,256]{2,1,0:T(8,128)(2,1)S(1)} collective-permute-done((bf16[2,256,256]{2,1,0:T(8,128)(2,1)S(1)}, bf16[2,256,256]{2,1,0:T(8,128)(2,1)S(1)}, u32[]{:S(2)}, u32[]{:S(2)}) %collective-permute-start.1) | collective-permute-done | bytes 262176 | tf_op jit(solution)/shard_map/ppermute | solution.py:422
  16.0 5.4 %first_edges.1 = (bf16[1024,256]{1,0:T(8,128)(2,1)S(1)}, bf16[1024,256]{1,0:T(8,128)(2,1)S(1)}, bf16[1024,256]{1,0:T(8,128)(2,1)S(1)}, f32[1024,256]{1,0:T(8,128)S(1)}) custom-call(bf16[2048,256]{1,0:T(8,128)(2,1)S(1)} %get-tuple-element.26.arr, bf16[2048,256]{1,0:T(8,128)(2,1)S(1)} %get-tuple-element.27.sta, ...), custom_call_target="tpu_custom_call" | custom-call | flops 3623878656 | bytes 4194304 | tf_op jit(solution)/shard_map/first_edges/pallas_call | solution.py:371
  21.4 1.4 %collective-permute-start.2 = (bf16[1024,256]{1,0:T(8,128)(2,1)S(1)}, bf16[1024,256]{1,0:T(8,128)(2,1)S(1)}, u32[]{:S(2)}, u32[]{:S(2)}) collective-permute-start(bf16[1024,256]{1,0:T(8,128)(2,1)S(1)} %get-tuple-element.34), channel_id=1, source_target_pairs={{0,64},{64,0},{1,65},{65,1},{2,66},{66,2},{3,67},{67,3},{4,68},{68... | collective-permute-start | bytes 1572872 | tf_op jit(solution)/shard_map/ppermute | solution.py:431
  22.8 1.4 %collective-permute-done.5.got_m = bf16[1024,256]{1,0:T(8,128)(2,1)S(1)} collective-permute-done((bf16[1024,256]{1,0:T(8,128)(2,1)S(1)}, bf16[1024,256]{1,0:T(8,128)(2,1)S(1)}, u32[]{:S(2)}, u32[]{:S(2)}) %collective-permute-start.5) | collective-permute-done | bytes 524320 | tf_op jit(solution)/shard_map/ppermute | solution.py:419
  24.2 4.4 %second_middle.1 = (bf16[768,256]{1,0:T(8,128)(2,1)S(1)}, f32[256,4608]{1,0:T(8,128)S(1)}) custom-call(bf16[1024,256]{1,0:T(8,128)(2,1)S(1)} %collective-permute-done.5.got_m, bf16[2048,256]{1,0:T(8,128)(2,1)S(1)} %get-tuple-element.26.arr, bf16[2048,256]{1,0:T(8,128)(2,1)S(1)} %get-tuple-element.27.sta, bf16[2,256,256]{2,1,0:T(8,128)(2,1)S(1)} %collective-permute-done.up, ...), custom_call_target="tpu_custom_call" | custom-call | flops 5737807872 | bytes 4194304 | tf_op jit(solution)/shard_map/second_middle/pallas_call | solution.py:371
  28.7 6.7 %collective-permute-done.2.got_e = bf16[1024,256]{1,0:T(8,128)(2,1)S(1)} collective-permute-done((bf16[1024,256]{1,0:T(8,128)(2,1)S(1)}, bf16[1024,256]{1,0:T(8,128)(2,1)S(1)}, u32[]{:S(2)}, u32[]{:S(2)}) %collective-permute-start.2) | collective-permute-done | bytes 524320 | tf_op jit(solution)/shard_map/ppermute | solution.py:431
  35.4 1.3 %collective-permute-start.4 = (bf16[256,256]{1,0:T(8,128)(2,1)S(1)}, bf16[256,256]{1,0:T(8,128)(2,1)S(1)}, u32[]{:S(2)}, u32[]{:S(2)}) collective-permute-start(bf16[256,256]{1,0:T(8,128)(2,1)S(1)} %get-tuple-element.52), channel_id=1, source_target_pairs={{2,0},{4,2},{6,4},{8,6},{10,8},{12,10},{14,12},{16,14},{18,16},{20... | collective-permute-start | bytes 393224 | tf_op jit(solution)/shard_map/ppermute | solution.py:441
  36.7 4.7 %collective-permute-start.3 = (bf16[256,256]{1,0:T(8,128)(2,1)S(1)}, bf16[256,256]{1,0:T(8,128)(2,1)S(1)}, u32[]{:S(2)}, u32[]{:S(2)}) collective-permute-start(bf16[256,256]{1,0:T(8,128)(2,1)S(1)} %get-tuple-element.53), channel_id=1, source_target_pairs={{0,2},{2,4},{4,6},{6,8},{8,10},{10,12},{12,14},{14,16},{16,18},{18... | collective-permute-start | bytes 393224 | tf_op jit(solution)/shard_map/ppermute | solution.py:440
  41.5 4.2 %second_edges.1 = (bf16[1024,256]{1,0:T(8,128)(2,1)S(1)}, f32[256,4608]{1,0:T(8,128)S(1)}) custom-call(bf16[1024,256]{1,0:T(8,128)(2,1)S(1)} %collective-permute-done.5.got_m, bf16[1024,256]{1,0:T(8,128)(2,1)S(1)} %collective-permute-done.2.got_e, bf16[2048,256]{1,0:T(8,128)(2,1)S(1)} %get-tuple-element.27.sta, ...), custom_call_target="tpu_custom_call" | custom-call | flops 3623878656 | bytes 4194304 | tf_op jit(solution)/shard_map/second_edges/pallas_call | solution.py:371
  45.7 2.0 %second_halo.1 = (bf16[512,256]{1,0:T(8,128)(2,1)S(1)}, bf16[128,4608]{1,0:T(8,128)(2,1)S(1)}, f32[128,4608]{1,0:T(8,128)S(1)}) custom-call(bf16[1024,256]{1,0:T(8,128)(2,1)S(1)} %collective-permute-done.2.got_e, bf16[256,256]{1,0:T(8,128)(2,1)S(1)} %collective-permute-done.3.got_up, bf16[256,256]{1,0:T(8,128)(2,1)S(1)} %collective-permute-done.4.got_down, ...), custom_call_target="tpu_custom_call" | custom-call | flops 1207959552 | bytes 4194304 | tf_op jit(solution)/shard_map/second_halo/pallas_call | solution.py:371
  48.4 4.3 %collective-permute-start.6 = (bf16[128,4608]{1,0:T(8,128)(2,1)S(1)}, bf16[128,4608]{1,0:T(8,128)(2,1)S(1)}, u32[]{:S(2)}, u32[]{:S(2)}) collective-permute-start(bf16[128,4608]{1,0:T(8,128)(2,1)S(1)} %get-tuple-element.44), channel_id=1, source_target_pairs={{0,2},{2,0},{1,3},{3,1},{4,6},{6,4},{5,7},{7,5},{8,10},{10,8},{9,1... | collective-permute-start | bytes 3538952 | tf_op jit(solution)/shard_map/ppermute | solution.py:469
  52.7 2.5 %collective-permute-done.6 = bf16[128,4608]{1,0:T(8,128)(2,1)S(1)} collective-permute-done((bf16[128,4608]{1,0:T(8,128)(2,1)S(1)}, bf16[128,4608]{1,0:T(8,128)(2,1)S(1)}, u32[]{:S(2)}, u32[]{:S(2)}) %collective-permute-start.6) | collective-permute-done | bytes 1179680 | tf_op jit(solution)/shard_map/ppermute | solution.py:469
  55.2 1.2 %fusion = bf16[16,8,4608]{2,1,0:T(8,128)(2,1)} fusion(f32[128,4608]{1,0:T(8,128)S(1)} %get-tuple-element.43, bf16[128,4608]{1,0:T(8,128)(2,1)S(1)} %collective-permute-done.6), kind=kLoop, calls=%fused_computation.2 | loop fusion | flops 1769472 | bytes 4718592 | tf_op jit(solution)/shard_map/reshape | solution.py:470
  56.5 8.5 %all-to-all-start = ((bf16[16,8,4608]{2,1,0:T(8,128)(2,1)}), bf16[16,8,4608]{2,1,0:T(8,128)(2,1)}, u32[]{:S(2)}, u32[]{:S(2)}) async-start(bf16[16,8,4608]{2,1,0:T(8,128)(2,1)} %fusion), calls=%async_computation | async-start | bytes 2359296 | tf_op jit(solution)/shard_map/all_to_all | solution.py:471
  65.9 1.0 %copy-done.5 = bf16[1024,256]{1,0:T(8,128)(2,1)S(1)} copy-done((bf16[1024,256]{1,0:T(8,128)(2,1)S(1)}, bf16[1024,256]{1,0:T(8,128)(2,1)}, u32[]{:S(2)}) %copy-start.5) | copy-done | bytes 524312
  68.0 4.8 %second_out.1 = bf16[2048,256]{1,0:T(8,128)(2,1)} custom-call(bf16[1024,256]{1,0:T(8,128)(2,1)S(1)} %collective-permute-done.5.got_m, bf16[1024,256]{1,0:T(8,128)(2,1)S(1)} %collective-permute-done.2.got_e, bf16[768,256]{1,0:T(8,128)(2,1)S(1)} %copy-done.7, bf16[1024,256]{1,0:T(8,128)(2,1)S(1)} %copy-done.5, bf16[512,256]{1,0:T(8,128)(2,1)S(1)} %copy-done.2, ...), custom_call_target="tpu_custom_call" | custom-call | flops 2415919104 | bytes 4194304 | tf_op jit(solution)/shard_map/second_out/pallas_call | solution.py:371
  72.7 12.2 %all-to-all-done = bf16[16,8,4608]{2,1,0:T(8,128)(2,1)} async-done(((bf16[16,8,4608]{2,1,0:T(8,128)(2,1)}), bf16[16,8,4608]{2,1,0:T(8,128)(2,1)}, u32[]{:S(2)}, u32[]{:S(2)}) %all-to-all-start) | async-done | bytes 1179680 | tf_op jit(solution)/shard_map/all_to_all | solution.py:471
  84.9 1.4 %convert_reduce_fusion = f32[8,4608]{1,0:T(8,128)S(1)} fusion(bf16[16,8,4608]{2,1,0:T(8,128)(2,1)} %all-to-all-done), kind=kLoop, calls=%fused_computation | loop fusion | flops 1142784 | bytes 1327104 | tf_op jit(solution)/shard_map/reduce_sum | solution.py:472
  86.4 3.1 %collective-permute-start.7 = (bf16[8,4608]{1,0:T(8,128)(2,1)S(1)}, bf16[8,4608]{1,0:T(8,128)(2,1)S(1)}, u32[]{:S(2)}, u32[]{:S(2)}) collective-permute-start(bf16[8,4608]{1,0:T(8,128)(2,1)S(1)} %convert_element_type.18), channel_id=1, source_target_pairs={{0,65},{1,64},{64,1},{65,0},{2,67},{3,66},{66,3},{67,2},{4,69},{5,... | collective-permute-start | bytes 221192 | tf_op jit(solution)/shard_map/ppermute | solution.py:475
  89.4 2.5 %collective-permute-done.7 = bf16[8,4608]{1,0:T(8,128)(2,1)S(1)} collective-permute-done((bf16[8,4608]{1,0:T(8,128)(2,1)S(1)}, bf16[8,4608]{1,0:T(8,128)(2,1)S(1)}, u32[]{:S(2)}, u32[]{:S(2)}) %collective-permute-start.7) | collective-permute-done | bytes 73760 | tf_op jit(solution)/shard_map/ppermute | solution.py:475
  (23 shorter events, 3.6 us)
Async XLA Ops:
  0.6 15.3 %copy-start = (bf16[1,1,2,3,3,256,256]{6,5,4,3,2,1,0:T(8,128)(2,1)S(1)}, bf16[1,1,2,3,3,256,256]{6,5,4,3,2,1,0:T(8,128)(2,1)}, u32[]{:S(2)}) copy-start(bf16[1,1,2,3,3,256,256]{6,5,4,3,2,1,0:T(8,128)(2,1)} %param.5) | copy-start | bytes 7077892
  9.0 4.8 %collective-permute-start = (bf16[2,256,256]{2,1,0:T(8,128)(2,1)S(1)}, bf16[2,256,256]{2,1,0:T(8,128)(2,1)S(1)}, u32[]{:S(2)}, u32[]{:S(2)}) collective-permute-start(bf16[2,256,256]{2,1,0:T(8,128)(2,1)S(1)} %get-tuple-element.31), channel_id=1, source_target_pairs={{0,2},{2,4},{4,6},{6,8},{8,10},{10,12},{12,14},{14,16},{16,18},{18... | collective-permute-start | bytes 786440 | tf_op jit(solution)/shard_map/ppermute | solution.py:421
  10.3 5.7 %collective-permute-start.1 = (bf16[2,256,256]{2,1,0:T(8,128)(2,1)S(1)}, bf16[2,256,256]{2,1,0:T(8,128)(2,1)S(1)}, u32[]{:S(2)}, u32[]{:S(2)}) collective-permute-start(bf16[2,256,256]{2,1,0:T(8,128)(2,1)S(1)} %get-tuple-element.32), channel_id=1, source_target_pairs={{2,0},{4,2},{6,4},{8,6},{10,8},{12,10},{14,12},{16,14},{18,16},{20... | collective-permute-start | bytes 786440 | tf_op jit(solution)/shard_map/ppermute | solution.py:422
  11.6 12.7 %collective-permute-start.5 = (bf16[1024,256]{1,0:T(8,128)(2,1)S(1)}, bf16[1024,256]{1,0:T(8,128)(2,1)S(1)}, u32[]{:S(2)}, u32[]{:S(2)}) collective-permute-start(bf16[1024,256]{1,0:T(8,128)(2,1)S(1)} %get-tuple-element.36), channel_id=1, source_target_pairs={{0,64},{64,0},{1,65},{65,1},{2,66},{66,2},{3,67},{67,3},{4,68},{68... | collective-permute-start | bytes 1572872 | tf_op jit(solution)/shard_map/ppermute | solution.py:419
  16.0 8.3 %copy-start.3 = (f32[1280,256]{1,0:T(8,128)S(1)}, f32[1280,256]{1,0:T(8,128)}, u32[]{:S(2)}) copy-start(f32[1280,256]{1,0:T(8,128)} %get-tuple-element.40.slope_m) | copy-start | bytes 3932164
  21.4 14.0 %collective-permute-start.2 = (bf16[1024,256]{1,0:T(8,128)(2,1)S(1)}, bf16[1024,256]{1,0:T(8,128)(2,1)S(1)}, u32[]{:S(2)}, u32[]{:S(2)}) collective-permute-start(bf16[1024,256]{1,0:T(8,128)(2,1)S(1)} %get-tuple-element.34), channel_id=1, source_target_pairs={{0,64},{64,0},{1,65},{65,1},{2,66},{66,2},{3,67},{67,3},{4,68},{68... | collective-permute-start | bytes 1572872 | tf_op jit(solution)/shard_map/ppermute | solution.py:431
  28.7 17.0 %copy-start.6 = (bf16[768,256]{1,0:T(8,128)(2,1)}, bf16[768,256]{1,0:T(8,128)(2,1)S(1)}, u32[]{:S(2)}) copy-start(bf16[768,256]{1,0:T(8,128)(2,1)S(1)} %get-tuple-element.45.act2_m) | copy-start | bytes 1179652
  35.4 10.2 %collective-permute-start.4 = (bf16[256,256]{1,0:T(8,128)(2,1)S(1)}, bf16[256,256]{1,0:T(8,128)(2,1)S(1)}, u32[]{:S(2)}, u32[]{:S(2)}) collective-permute-start(bf16[256,256]{1,0:T(8,128)(2,1)S(1)} %get-tuple-element.52), channel_id=1, source_target_pairs={{2,0},{4,2},{6,4},{8,6},{10,8},{12,10},{14,12},{16,14},{18,16},{20... | collective-permute-start | bytes 393224 | tf_op jit(solution)/shard_map/ppermute | solution.py:441
  36.7 8.9 %collective-permute-start.3 = (bf16[256,256]{1,0:T(8,128)(2,1)S(1)}, bf16[256,256]{1,0:T(8,128)(2,1)S(1)}, u32[]{:S(2)}, u32[]{:S(2)}) collective-permute-start(bf16[256,256]{1,0:T(8,128)(2,1)S(1)} %get-tuple-element.53), channel_id=1, source_target_pairs={{0,2},{2,4},{4,6},{6,8},{8,10},{10,12},{12,14},{14,16},{16,18},{18... | collective-permute-start | bytes 393224 | tf_op jit(solution)/shard_map/ppermute | solution.py:440
  45.6 2.1 %copy-start.4 = (bf16[1024,256]{1,0:T(8,128)(2,1)}, bf16[1024,256]{1,0:T(8,128)(2,1)S(1)}, u32[]{:S(2)}) copy-start(bf16[1024,256]{1,0:T(8,128)(2,1)S(1)} %get-tuple-element.46.act2_e) | copy-start | bytes 1572868
  47.7 0.7 copy-start.1
  48.4 6.8 %collective-permute-start.6 = (bf16[128,4608]{1,0:T(8,128)(2,1)S(1)}, bf16[128,4608]{1,0:T(8,128)(2,1)S(1)}, u32[]{:S(2)}, u32[]{:S(2)}) collective-permute-start(bf16[128,4608]{1,0:T(8,128)(2,1)S(1)} %get-tuple-element.44), channel_id=1, source_target_pairs={{0,2},{2,0},{1,3},{3,1},{4,6},{6,4},{5,7},{7,5},{8,10},{10,8},{9,1... | collective-permute-start | bytes 3538952 | tf_op jit(solution)/shard_map/ppermute | solution.py:469
  56.5 28.4 %all-to-all-start = ((bf16[16,8,4608]{2,1,0:T(8,128)(2,1)}), bf16[16,8,4608]{2,1,0:T(8,128)(2,1)}, u32[]{:S(2)}, u32[]{:S(2)}) async-start(bf16[16,8,4608]{2,1,0:T(8,128)(2,1)} %fusion), calls=%async_computation | async-start | bytes 2359296 | tf_op jit(solution)/shard_map/all_to_all | solution.py:471
  65.0 1.0 %copy-start.2 = (bf16[512,256]{1,0:T(8,128)(2,1)S(1)}, bf16[512,256]{1,0:T(8,128)(2,1)}, u32[]{:S(2)}) copy-start(bf16[512,256]{1,0:T(8,128)(2,1)} %copy-done.1) | copy-start | bytes 786436
  65.9 1.0 %copy-start.5 = (bf16[1024,256]{1,0:T(8,128)(2,1)S(1)}, bf16[1024,256]{1,0:T(8,128)(2,1)}, u32[]{:S(2)}) copy-start(bf16[1024,256]{1,0:T(8,128)(2,1)} %copy-done.4) | copy-start | bytes 1572868
  67.0 1.0 %copy-start.7 = (bf16[768,256]{1,0:T(8,128)(2,1)S(1)}, bf16[768,256]{1,0:T(8,128)(2,1)}, u32[]{:S(2)}) copy-start(bf16[768,256]{1,0:T(8,128)(2,1)} %copy-done.6) | copy-start | bytes 1179652
  86.4 5.6 %collective-permute-start.7 = (bf16[8,4608]{1,0:T(8,128)(2,1)S(1)}, bf16[8,4608]{1,0:T(8,128)(2,1)S(1)}, u32[]{:S(2)}, u32[]{:S(2)}) collective-permute-start(bf16[8,4608]{1,0:T(8,128)(2,1)S(1)} %convert_element_type.18), channel_id=1, source_target_pairs={{0,65},{1,64},{64,1},{65,0},{2,67},{3,66},{66,3},{67,2},{4,69},{5,... | collective-permute-start | bytes 221192 | tf_op jit(solution)/shard_map/ppermute | solution.py:475

commit v2 on v1

--- a/solution.py
+++ b/solution.py
@@ -16,7 +16,7 @@
 CH = 256
 TAPS = 9 * CH
 MIB = 1 << 20
-LIMIT_A = 49
+LIMIT_A = 50
 
 
 def rows(first, count):
@@ -118,14 +118,14 @@
 
 
 def kernel_a(
-    arr_hbm, sta_hbm, w_hbm, out_m, act_m, hid_m, slope_m, low, high, arr, sta, s3, a3, c3, w, sems
+    arr_hbm, sta_hbm, w_hbm, out_m, act_m, hid_m, slope_m, low, high, sta, s3, a3, c3, w, arr, steep, sems
 ):
     two = 2 * COLS
     size = arr_hbm.shape[0]
     moves = (
         (sta_hbm, sta),
+        (w_hbm.at[0], w.at[0]),
         (arr_hbm, arr),
-        (w_hbm.at[0], w.at[0]),
         (w_hbm.at[1], w.at[1]),
         (arr_hbm.at[pl.ds(size - two, two)], low.at[0]),
         (sta_hbm.at[pl.ds(size - two, two)], low.at[1]),
@@ -138,34 +138,30 @@
     copies[0].wait()
     fill3(s3, 0, sta, 2, 12)
     copies[1].wait()
-    fill3(a3, 0, arr, 2, 12)
-    for copy in copies[2:]:
-        copy.wait()
-
-    def body(leading):
-
-        def inner(step):
-            row = 5 * step
+    copies[2].wait()
+
+    def body(leading):
+        fill3(a3, 0, arr, 2, 12)
+        for row in (0, 5):
             pre = conv(s3, row, 5, w, 0, False)
             hid, slope = activate(pre)
             hid_m[rows(row, 5), :] = hid.astype(BF16)
-            slope_m[rows(row, 5), :] = slope
+            if leading:
+                slope_m[rows(row, 5), :] = slope.astype(BF16)
+            else:
+                steep[rows(row, 5), :] = slope
+        for copy in copies[3:]:
+            copy.wait()
+        for row in (0, 5):
             if leading:
                 act, _ = activate(conv(a3, row, 5, w, 0, False))
             else:
-                act = conv(a3, row, 5, w, 1, True) * slope
+                act = conv(a3, row, 5, w, 1, True) * steep[rows(row, 5), :]
             act_m[rows(row, 5), :] = act.astype(BF16)
             store3(c3, row, act, 5)
-
-        def last(step):
-            row = 4 * step
+        for row in (0, 4):
             total = conv(c3, row, 4, w, 1 if leading else 0, not leading)
             out_m[rows(row, 4), :] = (total + arr[rows(4 + row, 4), :].astype(F32)).astype(BF16)
-
-        for step in range(2):
-            inner(step)
-        for step in range(2):
-            last(step)
 
     by_role(body)
 
@@ -193,7 +189,7 @@
             else:
                 mask = jnp.where(spot == 3, has_down, 1.0)
             hid_e[rows(4 * half, 4), :] = (hid * mask).astype(BF16)
-            slope_e[rows(4 * half, 4), :] = slope
+            slope_e[rows(4 * half, 4), :] = slope.astype(BF16)
             if leading:
                 act, _ = activate(conv(a3, 6 * half, 4, w, 0, False))
             else:
@@ -220,7 +216,7 @@
         fill3(r3, 0, got_m, 0, 8)
         total = conv(r3, 0, 6, w, 1 if leading else 0, leading)
         if leading:
-            act = total * slope_m[rows(2, 6), :]
+            act = total * slope_m[rows(2, 6), :].astype(F32)
             act2_m[...] = act.astype(BF16)
             store3(z3, 0, act, 6)
             for a in range(3):
@@ -269,7 +265,7 @@
                     slope = jnp.concatenate([slope_e[rows(2, 2), :], slope_m[rows(0, 2), :]], axis=0)
                 else:
                     slope = jnp.concatenate([slope_m[rows(8, 2), :], slope_e[rows(4, 2), :]], axis=0)
-                act = total * slope
+                act = total * slope.astype(F32)
                 store3(z3, 4 * half, act, 4)
             else:
                 act, _ = activate(total)
@@ -319,7 +315,7 @@
         for half in range(2):
             total = conv(r3, 4 * half, 2, w, 1 if leading else 0, leading)
             if leading:
-                act = total * slope_e[rows(6 * half, 2), :]
+                act = total * slope_e[rows(6 * half, 2), :].astype(F32)
             else:
                 act, _ = activate(total)
             if half == 0:
@@ -365,7 +361,7 @@
     by_role(body)
 
 
-def call(body, name, outs, scratch, args, row_units, limit=18, space=pltpu.VMEM, sems=0):
+def call(body, outs, scratch, args, row_units, limit=18, space=pltpu.VMEM, sems=0):
     block = pl.BlockSpec(memory_space=pltpu.VMEM)
     semaphores = [pltpu.SemaphoreType.DMA((sems,))] if sems else []
     return pl.pallas_call(
@@ -380,11 +376,10 @@
             bytes_accessed=4 * MIB,
             transcendentals=0,
         ),
-        name=name,
     )(*args)
 
 
-def body(arrivals, stashed, weights):
+def tick(arrivals, stashed, weights):
     arr = arrivals.reshape(-1, CH)
     sta = stashed.reshape(-1, CH)
     w = weights[0, 0]
@@ -402,71 +397,64 @@
 
     two = 2 * COLS
     edge = ((2, two, CH), BF16)
-    out_m, act_m, hid_m, slope_m, low, high, arr, sta = call(
+    out_m, act_m, hid_m, slope_m, low, high, sta_v = call(
         kernel_a,
-        "first_middle",
-        [img(8), img(10), img(10), img(10, F32), edge, edge, img(16), img(16)],
-        [img3(12), img3(12), img3(10), (w.shape, BF16)],
+        [img(8), img(10), img(10), img(10), edge, edge, img(16)],
+        [img3(12), img3(12), img3(10), (w.shape, BF16), img(16), img(10, F32)],
         (arr, sta, w),
         28,
         limit=LIMIT_A,
         space=pltpu.HBM,
         sems=8,
     )
+    sta = sta_v
     ahead = [(i, i + 1) for i in range(space - 1)]
     back = [(j, i) for i, j in ahead]
     swap = [(0, 1), (1, 0)]
     got_m = lax.ppermute(out_m, "segment", swap)
-    act_m, low, high = lax.optimization_barrier((act_m, low, high))
     up = lax.ppermute(low, SPACE, ahead)
     down = lax.ppermute(high, SPACE, back)
     out_e, act_e, hid_e, slope_e = call(
         kernel_b,
-        "first_edges",
-        [img(8), img(8), img(8), img(8, F32)],
+        [img(8), img(8), img(8), img(8)],
         [img3(12), img3(12), img3(12)],
         (arr, sta, up, down, act_m, w),
         24,
     )
     got_e = lax.ppermute(out_e, "segment", swap)
+    both = ("segment",) + SPACE
+    across_ahead = [((s * space + i), ((1 - s) * space + j)) for s in range(2) for i, j in ahead]
+    across_back = [((s * space + i), ((1 - s) * space + j)) for s in range(2) for i, j in back]
+    got_up = lax.ppermute(out_e[-two:], both, across_ahead)
+    got_down = lax.ppermute(out_e[:two], both, across_back)
     act2_m, grad_c = call(
         kernel_c,
-        "second_middle",
         [img(6), grad_shape],
         [img3(8), img3(16), img3(16), img(18)],
         (got_m, arr, sta, up, down, act_m, act_e, hid_m, hid_e, slope_m, w),
         38,
     )
-    got_up = lax.ppermute(got_e[-two:], SPACE, ahead)
-    got_down = lax.ppermute(got_e[:two], SPACE, back)
     act2_e, grad_d = call(
         kernel_d,
-        "second_edges",
         [img(8), grad_shape],
         [img3(12), img3(8), img(12)],
         (got_m, got_e, sta, hid_m, hid_e, slope_m, slope_e, grad_c, w),
         24,
     )
-    act2_h, send, keep = call(
+    act2_h, sent, keep = call(
         functools.partial(kernel_e, scale),
-        "second_halo",
         [img(4), ((CH // 2, 2 * TAPS), BF16), ((CH // 2, 2 * TAPS), F32)],
         [img3(8), img3(2), img(6), ((CH, TAPS), F32)],
         (got_e, got_up, got_down, sta, up, down, slope_e, grad_c, grad_d, w),
         8,
     )
     (departing,) = call(
-        kernel_f,
-        "second_out",
-        [img(16)],
-        [img3(18), img(16)],
-        (got_m, got_e, act2_m, act2_e, act2_h, w),
-        16,
+        kernel_f, [img(16)], [img3(18), img(16)], (got_m, got_e, act2_m, act2_e, act2_h, w), 16
     )
 
     chips = space // 2
     share = CH // space
-    other = lax.ppermute(send, "space_2", swap)
+    other = lax.ppermute(sent, "space_2", swap)
     pieces = (keep + other.astype(F32)).astype(BF16).reshape(chips, share, 2 * TAPS)
     pieces = lax.all_to_all(pieces, ("space_0", "space_1"), 0, 0, tiled=True)
     owned = jnp.sum(pieces.astype(F32), axis=0)
@@ -494,4 +482,4 @@
         P("mirror", "segment", SPACE, None, None),
         P("mirror", "segment", SPACE, None, None, None, None),
     )
-    return jax.shard_map(body, mesh=split, in_specs=in_specs, out_specs=out_specs, check_vma=False)
+    return jax.shard_map(tick, mesh=split, in_specs=in_specs, out_specs=out_specs, check_vma=False)

time: 93.3 us -> 87.4 us (0.937)
  waiting for transfers between devices: 27.5 us -> 20.2 us
  starting transfers between devices: 28.1 us -> 29.8 us
    ppermute x8, waiting for transfers between devices: 15.4 us -> 8.25 us  [the longest x1 2.54 us: tick(): partner = lax.ppermute(owned.astype(BF16), ('segment', 'mirror'), pairs)]
  transfers between devices with their start and end apart: 9 -> 9, of which waited for: 6 -> 5; matrix products, arithmetic and copies ran while one was open for 0% -> 0% of each run, Pallas kernels for 20% -> 21%
where the time goes in v2:
time: 87.4 us; the launch traced here: 87 us
  starting transfers between devices  29.8 us (34%)
  Pallas kernels  28.2 us (32%)
  waiting for transfers between devices  20.2 us (23%)
  local copies, waits for them, and re-layouts  5.33 us (6%)
  other arithmetic  2.72 us (3%)
    pallas_call x6, Pallas kernels, call(): pl.pallas_call(body, out_shape=[jax.ShapeDtypeStruct(shape, dtype) for sh...  28.2 us
    all_to_all x1, waiting for transfers between devices, tick(): pieces = lax.all_to_all(pieces, ('space_0', 'space_1'), 0, 0, tiled=True)  11.9 us
    all_to_all x1, starting transfers between devices, tick(): pieces = lax.all_to_all(pieces, ('space_0', 'space_1'), 0, 0, tiled=True)  9.22 us
    ppermute x1, starting transfers between devices, tick(): got_up = lax.ppermute(out_e[-two:], both, across_ahead)  7.46 us
    unnamed x17, local copies, waits for them, and re-layouts  5.2 us
    ppermute x1, starting transfers between devices, tick(): partner = lax.ppermute(owned.astype(BF16), ('segment', 'mirror'), pairs)  3.1 us
    ppermute x1, waiting for transfers between devices, tick(): partner = lax.ppermute(owned.astype(BF16), ('segment', 'mirror'), pairs)  2.54 us
    ppermute x1, waiting for transfers between devices, tick(): other = lax.ppermute(sent, 'space_2', swap)  2.47 us
  transfers between devices with their start and end apart: 9, of which 5 were waited for; matrix products, arithmetic and copies ran while one was open for 0% of the time, Pallas kernels for 21%

profile of v2, /device:TPU:0, one launch (start us, length us, event | category | flops | bytes accessed | tf_op | source)
XLA Modules:
  0.0 87.0 jit_solution(1639161226015000123)
XLA Ops:
  0.6 7.6 %shard_map.50 = (bf16[1024,256]{1,0:T(8,128)(2,1)S(1)}, bf16[1280,256]{1,0:T(8,128)(2,1)S(1)}, bf16[1280,256]{1,0:T(8,128)(2,1)S(1)}, bf16[1280,256]{1,0:T(8,128...) custom-call(bf16[2048,256]{1,0:T(8,128)(2,1)} %bitcast.12, ...), custom_call_target="tpu_custom_call" | custom-call | flops 4227858432 | bytes 4194304 | tf_op jit(solution)/shard_map/pallas_call | solution.py:367
  8.3 1.3 %collective-permute-start = (bf16[2,256,256]{2,1,0:T(8,128)(2,1)S(1)}, bf16[2,256,256]{2,1,0:T(8,128)(2,1)S(1)}, u32[]{:S(2)}, u32[]{:S(2)}) collective-permute-start(bf16[2,256,256]{2,1,0:T(8,128)(2,1)S(1)} %get-tuple-element.23), channel_id=1, source_target_pairs={{0,2},{2,4},{4,6},{6,8},{8,10},{10,12},{12,14},{14,16},{16,18},{18... | collective-permute-start | bytes 786440 | tf_op jit(solution)/shard_map/ppermute | solution.py:415
  9.6 1.3 %collective-permute-start.1 = (bf16[2,256,256]{2,1,0:T(8,128)(2,1)S(1)}, bf16[2,256,256]{2,1,0:T(8,128)(2,1)S(1)}, u32[]{:S(2)}, u32[]{:S(2)}) collective-permute-start(bf16[2,256,256]{2,1,0:T(8,128)(2,1)S(1)} %get-tuple-element.24), channel_id=1, source_target_pairs={{2,0},{4,2},{6,4},{8,6},{10,8},{12,10},{14,12},{16,14},{18,16},{20... | collective-permute-start | bytes 786440 | tf_op jit(solution)/shard_map/ppermute | solution.py:416
  10.9 2.1 %collective-permute-start.5 = (bf16[1024,256]{1,0:T(8,128)(2,1)S(1)}, bf16[1024,256]{1,0:T(8,128)(2,1)S(1)}, u32[]{:S(2)}, u32[]{:S(2)}) collective-permute-start(bf16[1024,256]{1,0:T(8,128)(2,1)S(1)} %get-tuple-element.28), channel_id=1, source_target_pairs={{0,64},{64,0},{1,65},{65,1},{2,66},{66,2},{3,67},{67,3},{4,68},{68... | collective-permute-start | bytes 1572872 | tf_op jit(solution)/shard_map/ppermute | solution.py:414
  13.0 2.3 %collective-permute-done.1.down = bf16[2,256,256]{2,1,0:T(8,128)(2,1)S(1)} collective-permute-done((bf16[2,256,256]{2,1,0:T(8,128)(2,1)S(1)}, bf16[2,256,256]{2,1,0:T(8,128)(2,1)S(1)}, u32[]{:S(2)}, u32[]{:S(2)}) %collective-permute-start.1) | collective-permute-done | bytes 262176 | tf_op jit(solution)/shard_map/ppermute | solution.py:416
  15.3 5.2 %shard_map.51 = (bf16[1024,256]{1,0:T(8,128)(2,1)S(1)}, bf16[1024,256]{1,0:T(8,128)(2,1)S(1)}, bf16[1024,256]{1,0:T(8,128)(2,1)S(1)}, bf16[1024,256]{1,0:T(8,128)(2,1)S(1)}) custom-call(bf16[2048,256]{1,0:T(8,128)(2,1)S(1)} %bitcast.13, bf16[2048,256]{1,0:T(8,128)(2,1)S(1)} %get-tuple-element.22.sta, bf16[2,256,256]{2,1,0:T(8,128)(2,1)S(1)} %collective-permute-done.up, ...), custom_call_target="tpu_custom_call" | custom-call | flops 3623878656 | bytes 4194304 | tf_op jit(solution)/shard_map/pallas_call | solution.py:367
  20.5 1.6 %collective-permute-start.2 = (bf16[1024,256]{1,0:T(8,128)(2,1)S(1)}, bf16[1024,256]{1,0:T(8,128)(2,1)S(1)}, u32[]{:S(2)}, u32[]{:S(2)}) collective-permute-start(bf16[1024,256]{1,0:T(8,128)(2,1)S(1)} %get-tuple-element.26), channel_id=1, source_target_pairs={{0,64},{64,0},{1,65},{65,1},{2,66},{66,2},{3,67},{67,3},{4,68},{68... | collective-permute-start | bytes 1572872 | tf_op jit(solution)/shard_map/ppermute | solution.py:424
  22.1 1.3 %collective-permute-start.4 = (bf16[256,256]{1,0:T(8,128)(2,1)S(1)}, bf16[256,256]{1,0:T(8,128)(2,1)S(1)}, u32[]{:S(2)}, u32[]{:S(2)}) collective-permute-start(bf16[256,256]{1,0:T(8,128)(2,1)S(1)} %get-tuple-element.44), channel_id=1, source_target_pairs={{2,64},{4,66},{6,68},{8,70},{10,72},{12,74},{14,76},{16,78},{18,80... | collective-permute-start | bytes 393224 | tf_op jit(solution)/shard_map/ppermute | solution.py:429
  23.4 7.5 %collective-permute-start.3 = (bf16[256,256]{1,0:T(8,128)(2,1)S(1)}, bf16[256,256]{1,0:T(8,128)(2,1)S(1)}, u32[]{:S(2)}, u32[]{:S(2)}) collective-permute-start(bf16[256,256]{1,0:T(8,128)(2,1)S(1)} %get-tuple-element.45), channel_id=1, source_target_pairs={{0,66},{2,68},{4,70},{6,72},{8,74},{10,76},{12,78},{14,80},{16,82}... | collective-permute-start | bytes 393224 | tf_op jit(solution)/shard_map/ppermute | solution.py:428
  30.9 4.7 %shard_map.52 = (bf16[768,256]{1,0:T(8,128)(2,1)S(1)}, f32[256,4608]{1,0:T(8,128)S(1)}) custom-call(bf16[1024,256]{1,0:T(8,128)(2,1)S(1)} %collective-permute-done.5.got_m, bf16[2048,256]{1,0:T(8,128)(2,1)S(1)} %bitcast.14, bf16[2048,256]{1,0:T(8,128)(2,1)S(1)} %get-tuple-element.22.sta, bf16[2,256,256]{2,1,0:T(8,128)(2,1)S(1)} %collective-permute-done.up, ...), custom_call_target="tpu_custom_call" | custom-call | flops 5737807872 | bytes 4194304 | tf_op jit(solution)/shard_map/pallas_call | solution.py:367
  36.3 3.9 %shard_map.53 = (bf16[1024,256]{1,0:T(8,128)(2,1)S(1)}, f32[256,4608]{1,0:T(8,128)S(1)}) custom-call(bf16[1024,256]{1,0:T(8,128)(2,1)S(1)} %collective-permute-done.5.got_m, bf16[1024,256]{1,0:T(8,128)(2,1)S(1)} %collective-permute-done.2.got_e, bf16[2048,256]{1,0:T(8,128)(2,1)S(1)} %get-tuple-element.22.sta, bf16[1280,256]{1,0:T(8,128)(2,1)S(1)} %get-tuple-element.30.hid_m, ...), custom_call_target="tpu_custom_call" | custom-call | flops 3623878656 | bytes 4194304 | tf_op jit(solution)/shard_map/pallas_call | solution.py:367
  40.3 0.9 %collective-permute-done.4.got_down = bf16[256,256]{1,0:T(8,128)(2,1)S(1)} collective-permute-done((bf16[256,256]{1,0:T(8,128)(2,1)S(1)}, bf16[256,256]{1,0:T(8,128)(2,1)S(1)}, u32[]{:S(2)}, u32[]{:S(2)}) %collective-permute-start.4) | collective-permute-done | bytes 131104 | tf_op jit(solution)/shard_map/ppermute | solution.py:429
  41.2 2.0 %shard_map.54 = (bf16[512,256]{1,0:T(8,128)(2,1)S(1)}, bf16[128,4608]{1,0:T(8,128)(2,1)S(1)}, f32[128,4608]{1,0:T(8,128)S(1)}) custom-call(bf16[1024,256]{1,0:T(8,128)(2,1)S(1)} %collective-permute-done.2.got_e, bf16[256,256]{1,0:T(8,128)(2,1)S(1)} %collective-permute-done.3.got_up, bf16[256,256]{1,0:T(8,128)(2,1)S(1)} %collective-permute-done.4.got_down, ...), custom_call_target="tpu_custom_call" | custom-call | flops 1207959552 | bytes 4194304 | tf_op jit(solution)/shard_map/pallas_call | solution.py:367
  44.0 2.4 %collective-permute-start.6 = (bf16[128,4608]{1,0:T(8,128)(2,1)S(1)}, bf16[128,4608]{1,0:T(8,128)(2,1)S(1)}, u32[]{:S(2)}, u32[]{:S(2)}) collective-permute-start(bf16[128,4608]{1,0:T(8,128)(2,1)S(1)} %get-tuple-element.36), channel_id=1, source_target_pairs={{0,2},{2,0},{1,3},{3,1},{4,6},{6,4},{5,7},{7,5},{8,10},{10,8},{9,1... | collective-permute-start | bytes 3538952 | tf_op jit(solution)/shard_map/ppermute | solution.py:457
  46.4 2.5 %collective-permute-done.6 = bf16[128,4608]{1,0:T(8,128)(2,1)S(1)} collective-permute-done((bf16[128,4608]{1,0:T(8,128)(2,1)S(1)}, bf16[128,4608]{1,0:T(8,128)(2,1)S(1)}, u32[]{:S(2)}, u32[]{:S(2)}) %collective-permute-start.6) | collective-permute-done | bytes 1179680 | tf_op jit(solution)/shard_map/ppermute | solution.py:457
  48.9 1.2 %fusion = bf16[16,8,4608]{2,1,0:T(8,128)(2,1)} fusion(f32[128,4608]{1,0:T(8,128)S(1)} %get-tuple-element.35, bf16[128,4608]{1,0:T(8,128)(2,1)S(1)} %collective-permute-done.6), kind=kLoop, calls=%fused_computation.2 | loop fusion | flops 1769472 | bytes 4718592 | tf_op jit(solution)/shard_map/reshape | solution.py:458
  50.1 9.2 %all-to-all-start = ((bf16[16,8,4608]{2,1,0:T(8,128)(2,1)}), bf16[16,8,4608]{2,1,0:T(8,128)(2,1)}, u32[]{:S(2)}, u32[]{:S(2)}) async-start(bf16[16,8,4608]{2,1,0:T(8,128)(2,1)} %fusion), calls=%async_computation | async-start | bytes 2359296 | tf_op jit(solution)/shard_map/all_to_all | solution.py:459
  60.3 1.0 %copy-done.5 = bf16[1024,256]{1,0:T(8,128)(2,1)S(1)} copy-done((bf16[1024,256]{1,0:T(8,128)(2,1)S(1)}, bf16[1024,256]{1,0:T(8,128)(2,1)}, u32[]{:S(2)}) %copy-start.5) | copy-done | bytes 524312
  61.4 1.0 %copy-done.7 = bf16[768,256]{1,0:T(8,128)(2,1)S(1)} copy-done((bf16[768,256]{1,0:T(8,128)(2,1)S(1)}, bf16[768,256]{1,0:T(8,128)(2,1)}, u32[]{:S(2)}) %copy-start.7) | copy-done | bytes 393240
  62.3 4.8 %shard_map.55 = bf16[2048,256]{1,0:T(8,128)(2,1)} custom-call(bf16[1024,256]{1,0:T(8,128)(2,1)S(1)} %collective-permute-done.5.got_m, bf16[1024,256]{1,0:T(8,128)(2,1)S(1)} %collective-permute-done.2.got_e, bf16[768,256]{1,0:T(8,128)(2,1)S(1)} %copy-done.7, bf16[1024,256]{1,0:T(8,128)(2,1)S(1)} %copy-done.5, bf16[512,256]{1,0:T(8,128)(2,1)S(1)} %copy-done.3, ...), custom_call_target="tpu_custom_call" | custom-call | flops 2415919104 | bytes 4194304 | tf_op jit(solution)/shard_map/pallas_call | solution.py:367
  67.1 11.9 %all-to-all-done = bf16[16,8,4608]{2,1,0:T(8,128)(2,1)} async-done(((bf16[16,8,4608]{2,1,0:T(8,128)(2,1)}), bf16[16,8,4608]{2,1,0:T(8,128)(2,1)}, u32[]{:S(2)}, u32[]{:S(2)}) %all-to-all-start) | async-done | bytes 1179680 | tf_op jit(solution)/shard_map/all_to_all | solution.py:459
  79.0 1.4 %convert_reduce_fusion = f32[8,4608]{1,0:T(8,128)S(1)} fusion(bf16[16,8,4608]{2,1,0:T(8,128)(2,1)} %all-to-all-done), kind=kLoop, calls=%fused_computation | loop fusion | flops 1142784 | bytes 1327104 | tf_op jit(solution)/shard_map/reduce_sum | solution.py:460
  80.5 3.1 %collective-permute-start.7 = (bf16[8,4608]{1,0:T(8,128)(2,1)S(1)}, bf16[8,4608]{1,0:T(8,128)(2,1)S(1)}, u32[]{:S(2)}, u32[]{:S(2)}) collective-permute-start(bf16[8,4608]{1,0:T(8,128)(2,1)S(1)} %convert_element_type.18), channel_id=1, source_target_pairs={{0,65},{1,64},{64,1},{65,0},{2,67},{3,66},{66,3},{67,2},{4,69},{5,... | collective-permute-start | bytes 221192 | tf_op jit(solution)/shard_map/ppermute | solution.py:463
  83.6 2.5 %collective-permute-done.7 = bf16[8,4608]{1,0:T(8,128)(2,1)S(1)} collective-permute-done((bf16[8,4608]{1,0:T(8,128)(2,1)S(1)}, bf16[8,4608]{1,0:T(8,128)(2,1)S(1)}, u32[]{:S(2)}, u32[]{:S(2)}) %collective-permute-start.7) | collective-permute-done | bytes 73760 | tf_op jit(solution)/shard_map/ppermute | solution.py:463
  (23 shorter events, 3.3 us)
Async XLA Ops:
  0.6 14.6 %copy-start = (bf16[1,1,2,3,3,256,256]{6,5,4,3,2,1,0:T(8,128)(2,1)S(1)}, bf16[1,1,2,3,3,256,256]{6,5,4,3,2,1,0:T(8,128)(2,1)}, u32[]{:S(2)}) copy-start(bf16[1,1,2,3,3,256,256]{6,5,4,3,2,1,0:T(8,128)(2,1)} %param.5) | copy-start | bytes 7077892
  0.6 14.6 %copy-start.1 = (bf16[1,1,16,128,256]{4,3,2,1,0:T(8,128)(2,1)S(1)}, bf16[1,1,16,128,256]{4,3,2,1,0:T(8,128)(2,1)}, u32[]{:S(2)}) copy-start(bf16[1,1,16,128,256]{4,3,2,1,0:T(8,128)(2,1)} %param.3) | copy-start | bytes 3145732
  8.3 4.7 %collective-permute-start = (bf16[2,256,256]{2,1,0:T(8,128)(2,1)S(1)}, bf16[2,256,256]{2,1,0:T(8,128)(2,1)S(1)}, u32[]{:S(2)}, u32[]{:S(2)}) collective-permute-start(bf16[2,256,256]{2,1,0:T(8,128)(2,1)S(1)} %get-tuple-element.23), channel_id=1, source_target_pairs={{0,2},{2,4},{4,6},{6,8},{8,10},{10,12},{12,14},{14,16},{16,18},{18... | collective-permute-start | bytes 786440 | tf_op jit(solution)/shard_map/ppermute | solution.py:415
  9.6 5.7 %collective-permute-start.1 = (bf16[2,256,256]{2,1,0:T(8,128)(2,1)S(1)}, bf16[2,256,256]{2,1,0:T(8,128)(2,1)S(1)}, u32[]{:S(2)}, u32[]{:S(2)}) collective-permute-start(bf16[2,256,256]{2,1,0:T(8,128)(2,1)S(1)} %get-tuple-element.24), channel_id=1, source_target_pairs={{2,0},{4,2},{6,4},{8,6},{10,8},{12,10},{14,12},{16,14},{18,16},{20... | collective-permute-start | bytes 786440 | tf_op jit(solution)/shard_map/ppermute | solution.py:416
  10.9 20.0 %collective-permute-start.5 = (bf16[1024,256]{1,0:T(8,128)(2,1)S(1)}, bf16[1024,256]{1,0:T(8,128)(2,1)S(1)}, u32[]{:S(2)}, u32[]{:S(2)}) collective-permute-start(bf16[1024,256]{1,0:T(8,128)(2,1)S(1)} %get-tuple-element.28), channel_id=1, source_target_pairs={{0,64},{64,0},{1,65},{65,1},{2,66},{66,2},{3,67},{67,3},{4,68},{68... | collective-permute-start | bytes 1572872 | tf_op jit(solution)/shard_map/ppermute | solution.py:414
  20.5 15.8 %collective-permute-start.2 = (bf16[1024,256]{1,0:T(8,128)(2,1)S(1)}, bf16[1024,256]{1,0:T(8,128)(2,1)S(1)}, u32[]{:S(2)}, u32[]{:S(2)}) collective-permute-start(bf16[1024,256]{1,0:T(8,128)(2,1)S(1)} %get-tuple-element.26), channel_id=1, source_target_pairs={{0,64},{64,0},{1,65},{65,1},{2,66},{66,2},{3,67},{67,3},{4,68},{68... | collective-permute-start | bytes 1572872 | tf_op jit(solution)/shard_map/ppermute | solution.py:424
  22.1 19.1 %collective-permute-start.4 = (bf16[256,256]{1,0:T(8,128)(2,1)S(1)}, bf16[256,256]{1,0:T(8,128)(2,1)S(1)}, u32[]{:S(2)}, u32[]{:S(2)}) collective-permute-start(bf16[256,256]{1,0:T(8,128)(2,1)S(1)} %get-tuple-element.44), channel_id=1, source_target_pairs={{2,64},{4,66},{6,68},{8,70},{10,72},{12,74},{14,76},{16,78},{18,80... | collective-permute-start | bytes 393224 | tf_op jit(solution)/shard_map/ppermute | solution.py:429
  23.4 17.8 %collective-permute-start.3 = (bf16[256,256]{1,0:T(8,128)(2,1)S(1)}, bf16[256,256]{1,0:T(8,128)(2,1)S(1)}, u32[]{:S(2)}, u32[]{:S(2)}) collective-permute-start(bf16[256,256]{1,0:T(8,128)(2,1)S(1)} %get-tuple-element.45), channel_id=1, source_target_pairs={{0,66},{2,68},{4,70},{6,72},{8,74},{10,76},{12,78},{14,80},{16,82}... | collective-permute-start | bytes 393224 | tf_op jit(solution)/shard_map/ppermute | solution.py:428
  35.6 0.8 copy-start.6
  40.3 3.0 %copy-start.4 = (bf16[1024,256]{1,0:T(8,128)(2,1)}, bf16[1024,256]{1,0:T(8,128)(2,1)S(1)}, u32[]{:S(2)}) copy-start(bf16[1024,256]{1,0:T(8,128)(2,1)S(1)} %get-tuple-element.38.act2_e) | copy-start | bytes 1572868
  43.3 0.7 copy-start.2
  44.0 4.9 %collective-permute-start.6 = (bf16[128,4608]{1,0:T(8,128)(2,1)S(1)}, bf16[128,4608]{1,0:T(8,128)(2,1)S(1)}, u32[]{:S(2)}, u32[]{:S(2)}) collective-permute-start(bf16[128,4608]{1,0:T(8,128)(2,1)S(1)} %get-tuple-element.36), channel_id=1, source_target_pairs={{0,2},{2,0},{1,3},{3,1},{4,6},{6,4},{5,7},{7,5},{8,10},{10,8},{9,1... | collective-permute-start | bytes 3538952 | tf_op jit(solution)/shard_map/ppermute | solution.py:457
  50.1 28.9 %all-to-all-start = ((bf16[16,8,4608]{2,1,0:T(8,128)(2,1)}), bf16[16,8,4608]{2,1,0:T(8,128)(2,1)}, u32[]{:S(2)}, u32[]{:S(2)}) async-start(bf16[16,8,4608]{2,1,0:T(8,128)(2,1)} %fusion), calls=%async_computation | async-start | bytes 2359296 | tf_op jit(solution)/shard_map/all_to_all | solution.py:459
  59.4 1.0 %copy-start.3 = (bf16[512,256]{1,0:T(8,128)(2,1)S(1)}, bf16[512,256]{1,0:T(8,128)(2,1)}, u32[]{:S(2)}) copy-start(bf16[512,256]{1,0:T(8,128)(2,1)} %copy-done.2) | copy-start | bytes 786436
  60.3 1.0 %copy-start.5 = (bf16[1024,256]{1,0:T(8,128)(2,1)S(1)}, bf16[1024,256]{1,0:T(8,128)(2,1)}, u32[]{:S(2)}) copy-start(bf16[1024,256]{1,0:T(8,128)(2,1)} %copy-done.4) | copy-start | bytes 1572868
  61.3 1.0 %copy-start.7 = (bf16[768,256]{1,0:T(8,128)(2,1)S(1)}, bf16[768,256]{1,0:T(8,128)(2,1)}, u32[]{:S(2)}) copy-start(bf16[768,256]{1,0:T(8,128)(2,1)} %copy-done.6) | copy-start | bytes 1179652
  80.5 5.6 %collective-permute-start.7 = (bf16[8,4608]{1,0:T(8,128)(2,1)S(1)}, bf16[8,4608]{1,0:T(8,128)(2,1)S(1)}, u32[]{:S(2)}, u32[]{:S(2)}) collective-permute-start(bf16[8,4608]{1,0:T(8,128)(2,1)S(1)} %convert_element_type.18), channel_id=1, source_target_pairs={{0,65},{1,64},{64,1},{65,0},{2,67},{3,66},{66,3},{67,2},{4,69},{5,... | collective-permute-start | bytes 221192 | tf_op jit(solution)/shard_map/ppermute | solution.py:463

commit v3 on v2

--- a/solution.py
+++ b/solution.py
@@ -117,30 +117,40 @@
     return (place > 0).astype(F32), (place < count - 1).astype(F32)
 
 
+def above(near, far):
+    return jnp.where(lax.axis_index("space_2") == 1, near.astype(F32), far.astype(F32))
+
+
+def below(near, far):
+    return jnp.where(lax.axis_index("space_2") == 0, near.astype(F32), far.astype(F32))
+
+
 def kernel_a(
-    arr_hbm, sta_hbm, w_hbm, out_m, act_m, hid_m, slope_m, low, high, sta, s3, a3, c3, w, arr, steep, sems
+    arr_hbm, sta_hbm, w_hbm, out_m, act_m, hid_m, slope_m, near, far, sta, s3, a3, c3, w, arr, steep, sems
 ):
     two = 2 * COLS
     size = arr_hbm.shape[0]
+    core = lax.axis_index("space_2")
+    inner_at = pl.ds(pl.multiple_of((1 - core) * (size - two), two), two)
+    outer_at = pl.ds(pl.multiple_of(core * (size - two), two), two)
     moves = (
         (sta_hbm, sta),
         (w_hbm.at[0], w.at[0]),
         (arr_hbm, arr),
         (w_hbm.at[1], w.at[1]),
-        (arr_hbm.at[pl.ds(size - two, two)], low.at[0]),
-        (sta_hbm.at[pl.ds(size - two, two)], low.at[1]),
-        (arr_hbm.at[pl.ds(0, two)], high.at[0]),
-        (sta_hbm.at[pl.ds(0, two)], high.at[1]),
+        (arr_hbm.at[inner_at], near.at[0]),
+        (sta_hbm.at[inner_at], near.at[1]),
+        (arr_hbm.at[outer_at], far.at[0]),
+        (sta_hbm.at[outer_at], far.at[1]),
     )
     copies = [pltpu.make_async_copy(src, dst, sems.at[i]) for i, (src, dst) in enumerate(moves)]
     for copy in copies:
         copy.start()
-    copies[0].wait()
-    fill3(s3, 0, sta, 2, 12)
-    copies[1].wait()
-    copies[2].wait()
+    for copy in copies[:3]:
+        copy.wait()
 
     def body(leading):
+        fill3(s3, 0, sta, 2, 12)
         fill3(a3, 0, arr, 2, 12)
         for row in (0, 5):
             pre = conv(s3, row, 5, w, 0, False)
@@ -166,21 +176,25 @@
     by_role(body)
 
 
-def kernel_b(arr, sta, up, down, act_m, w, out_e, act_e, hid_e, slope_e, s3, a3, c3):
+def kernel_b(arr, sta, near, far, act_m, w, out_e, act_e, hid_e, slope_e, border, s3, a3, c3):
     has_up, has_down = edge_flags()
 
     def body(leading):
         for half in range(2):
             if half == 0:
-                store3(s3, 0, up[1], 2)
+                up = above(near[1], far[1])
+                border[rows(0, 1), :] = up[COLS:].astype(BF16)
+                store3(s3, 0, up, 2)
                 fill3(s3, 2, sta, 0, 4)
-                store3(a3, 0, up[0], 2)
+                store3(a3, 0, above(near[0], far[0]), 2)
                 fill3(a3, 2, arr, 0, 4)
             else:
                 fill3(s3, 6, sta, 12, 4)
-                store3(s3, 10, down[1], 2)
+                down = below(near[1], far[1])
+                border[rows(1, 1), :] = down[:COLS].astype(BF16)
+                store3(s3, 10, down, 2)
                 fill3(a3, 6, arr, 12, 4)
-                store3(a3, 10, down[0], 2)
+                store3(a3, 10, below(near[0], far[0]), 2)
             pre = conv(s3, 6 * half, 4, w, 0, False)
             hid, slope = activate(pre)
             spot = lax.broadcasted_iota(jnp.int32, (4 * COLS, CH), 0) // COLS
@@ -210,7 +224,7 @@
 
 
 def kernel_c(
-    got_m, arr, sta, up, down, act_m, act_e, hid_m, hid_e, slope_m, w, act2_m, grad, r3, y3, z3, whole
+    got_m, arr, sta, border, act_m, act_e, hid_m, hid_e, slope_m, w, act2_m, grad, r3, y3, z3, whole
 ):
     def body(leading):
         fill3(r3, 0, got_m, 0, 8)
@@ -244,9 +258,9 @@
             fill3(z3, 0, act_e, 1, 3)
             fill3(z3, 3, act_m, 0, 10)
             fill3(z3, 13, act_e, 4, 3)
-            whole[rows(0, 1), :] = up[1, rows(1, 1), :]
+            whole[rows(0, 1), :] = border[rows(0, 1), :]
             whole[rows(1, 16), :] = sta[...]
-            whole[rows(17, 1), :] = down[1, rows(0, 1), :]
+            whole[rows(17, 1), :] = border[rows(1, 1), :]
             repeat(3, first_grad)
 
     by_role(body)
@@ -287,7 +301,7 @@
 
 
 def kernel_e(
-    scale, got_e, got_up, got_down, sta, up, down, slope_e, grad_c, grad_d, w, act2_h, send, keep, r3, z3, x2, tot
+    scale, got_e, got_near, got_far, sta, border, slope_e, grad_c, grad_d, w, act2_h, send, keep, r3, z3, x2, tot
 ):
     has_up, has_down = edge_flags()
     core = lax.axis_index("space_2")
@@ -307,10 +321,10 @@
                 dst[pl.ds(16 * pair, 16), to_at : to_at + width] = (val * scale).astype(dst.dtype)
 
     def body(leading):
-        store3(r3, 0, got_up[...], 2)
+        store3(r3, 0, above(got_near[...], got_far[...]), 2)
         fill3(r3, 2, got_e, 0, 2)
         fill3(r3, 4, got_e, 6, 2)
-        store3(r3, 6, got_down[...], 2)
+        store3(r3, 6, below(got_near[...], got_far[...]), 2)
         spot = lax.broadcasted_iota(jnp.int32, (2 * COLS, CH), 0) // COLS
         for half in range(2):
             total = conv(r3, 4 * half, 2, w, 1 if leading else 0, leading)
@@ -325,10 +339,10 @@
             act2_h[rows(2 * half, 2), :] = act.astype(BF16)
         if leading:
             store3(z3, 0, act2_h[rows(1, 2), :], 2)
-            x2[rows(0, 1), :] = up[1, rows(1, 1), :]
+            x2[rows(0, 1), :] = border[rows(0, 1), :]
             x2[rows(1, 2), :] = sta[rows(0, 2), :]
             x2[rows(3, 2), :] = sta[rows(14, 2), :]
-            x2[rows(5, 1), :] = down[1, rows(0, 1), :]
+            x2[rows(5, 1), :] = border[rows(1, 1), :]
             for a in range(3):
                 left = jnp.concatenate([x2[rows(a, 1), :], x2[rows(3 + a, 1), :]], axis=0)
                 put_grad(tot, 0, a, get_grad(grad_d, 0, a) + outer(left, z3[...]))
@@ -338,6 +352,18 @@
             emit(grad_c, 0, 0, 2 * TAPS)
 
     by_role(body)
+
+
+def kernel_pick(got_e, inner, outer):
+    core = lax.axis_index("space_2")
+    inner[...] = got_e[rows(6 * (1 - core), 2), :]
+    outer[...] = got_e[rows(6 * core, 2), :]
+
+
+def kernel_sum(keep, other, total):
+    for row in range(0, keep.shape[0], 16):
+        part = pl.ds(row, 16)
+        total[part, :] = (keep[part, :] + other[part, :].astype(F32)).astype(BF16)
 
 
 def kernel_f(got_m, got_e, act2_m, act2_e, act2_h, w, out, c3, kept):
@@ -397,7 +423,7 @@
 
     two = 2 * COLS
     edge = ((2, two, CH), BF16)
-    out_m, act_m, hid_m, slope_m, low, high, sta_v = call(
+    out_m, act_m, hid_m, slope_m, near, far, sta_v = call(
         kernel_a,
         [img(8), img(10), img(10), img(10), edge, edge, img(16)],
         [img3(12), img3(12), img3(10), (w.shape, BF16), img(16), img(10, F32)],
@@ -408,30 +434,28 @@
         sems=8,
     )
     sta = sta_v
-    ahead = [(i, i + 1) for i in range(space - 1)]
-    back = [(j, i) for i, j in ahead]
+    hop = [(i, i + 1) for i in range(1, space - 1, 2)]
+    hop = hop + [(j, i) for i, j in hop]
     swap = [(0, 1), (1, 0)]
     got_m = lax.ppermute(out_m, "segment", swap)
-    up = lax.ppermute(low, SPACE, ahead)
-    down = lax.ppermute(high, SPACE, back)
-    out_e, act_e, hid_e, slope_e = call(
+    near = lax.ppermute(near, "space_2", swap)
+    far = lax.ppermute(far, SPACE, hop)
+    out_e, act_e, hid_e, slope_e, border = call(
         kernel_b,
-        [img(8), img(8), img(8), img(8)],
+        [img(8), img(8), img(8), img(8), img(2)],
         [img3(12), img3(12), img3(12)],
-        (arr, sta, up, down, act_m, w),
+        (arr, sta, near, far, act_m, w),
         24,
     )
     got_e = lax.ppermute(out_e, "segment", swap)
-    both = ("segment",) + SPACE
-    across_ahead = [((s * space + i), ((1 - s) * space + j)) for s in range(2) for i, j in ahead]
-    across_back = [((s * space + i), ((1 - s) * space + j)) for s in range(2) for i, j in back]
-    got_up = lax.ppermute(out_e[-two:], both, across_ahead)
-    got_down = lax.ppermute(out_e[:two], both, across_back)
+    inner_rows, outer_rows = call(kernel_pick, [img(2), img(2)], [], (got_e,), 0, limit=4)
+    got_near = lax.ppermute(inner_rows, "space_2", swap)
+    got_far = lax.ppermute(outer_rows, SPACE, hop)
     act2_m, grad_c = call(
         kernel_c,
         [img(6), grad_shape],
         [img3(8), img3(16), img3(16), img(18)],
-        (got_m, arr, sta, up, down, act_m, act_e, hid_m, hid_e, slope_m, w),
+        (got_m, arr, sta, border, act_m, act_e, hid_m, hid_e, slope_m, w),
         38,
     )
     act2_e, grad_d = call(
@@ -445,7 +469,7 @@
         functools.partial(kernel_e, scale),
         [img(4), ((CH // 2, 2 * TAPS), BF16), ((CH // 2, 2 * TAPS), F32)],
         [img3(8), img3(2), img(6), ((CH, TAPS), F32)],
-        (got_e, got_up, got_down, sta, up, down, slope_e, grad_c, grad_d, w),
+        (got_e, got_near, got_far, sta, border, slope_e, grad_c, grad_d, w),
         8,
     )
     (departing,) = call(
@@ -455,7 +479,8 @@
     chips = space // 2
     share = CH // space
     other = lax.ppermute(sent, "space_2", swap)
-    pieces = (keep + other.astype(F32)).astype(BF16).reshape(chips, share, 2 * TAPS)
+    (pieces,) = call(kernel_sum, [(keep.shape, BF16)], [], (keep, other), 0, limit=8)
+    pieces = pieces.reshape(chips, share, 2 * TAPS)
     pieces = lax.all_to_all(pieces, ("space_0", "space_1"), 0, 0, tiled=True)
     owned = jnp.sum(pieces.astype(F32), axis=0)
     owned, departing = lax.optimization_barrier((owned, departing))

time: 87.4 us -> 86.7 us (level)
  waiting for transfers between devices: 20.2 us -> 28.2 us
  starting transfers between devices: 29.8 us -> 22.2 us
  Pallas kernels: 28.2 us -> 29.8 us
  local copies, waits for them, and re-layouts: 5.33 us -> 3.85 us
  other arithmetic: 2.72 us -> 1.47 us
    ppermute x4, starting transfers between devices: 11.3 us -> 3.73 us  [the longest x1 2.31 us: tick(): got_near = lax.ppermute(inner_rows, 'space_2', swap)]
    ppermute x1, waiting for transfers between devices: 0.01 us -> 6.57 us  [tick(): got_e = lax.ppermute(out_e, 'segment', swap)]
    ppermute x1, waiting for transfers between devices: 0.01 us -> 4.48 us  [tick(): got_m = lax.ppermute(out_m, 'segment', swap)]
    ppermute x4, waiting for transfers between devices: 3.22 us -> 0.01 us  [the longest x1 0.01 us: tick(): got_near = lax.ppermute(inner_rows, 'space_2', swap)]
    ppermute x1, starting transfers between devices: 2.42 us -> 4.81 us  [tick(): other = lax.ppermute(sent, 'space_2', swap)]
    pallas_call x6 -> x8, Pallas kernels: 28.2 us -> 29.8 us  [call(): pl.pallas_call(body, out_shape=[jax.ShapeDtypeStruct(shape, dtype) for sh...]
    unnamed x17, local copies, waits for them, and re-layouts: 5.2 us -> 3.74 us
    reshape x1 -> x0, other arithmetic: 1.25 us -> none  [tick(): (keep + other.astype(F32)).astype(BF16).reshape(chips, share, 2 * TAPS)]
  transfers between devices with their start and end apart: 9 -> 9, of which waited for: 5 -> 5; matrix products, arithmetic and copies ran while one was open for 0% -> 0% of each run, Pallas kernels for 21% -> 22%
where the time goes in v3:
time: 86.7 us; the launch traced here: 86.4 us
  Pallas kernels  29.8 us (34%)
  waiting for transfers between devices  28.2 us (33%)
  starting transfers between devices  22.2 us (26%)
  local copies, waits for them, and re-layouts  3.85 us (4%)
  other arithmetic  1.47 us (2%)
    pallas_call x8, Pallas kernels, call(): pl.pallas_call(body, out_shape=[jax.ShapeDtypeStruct(shape, dtype) for sh...  29.8 us
    all_to_all x1, waiting for transfers between devices, tick(): pieces = lax.all_to_all(pieces, ('space_0', 'space_1'), 0, 0, tiled=True)  12.2 us
    all_to_all x1, starting transfers between devices, tick(): pieces = lax.all_to_all(pieces, ('space_0', 'space_1'), 0, 0, tiled=True)  8.08 us
    ppermute x1, waiting for transfers between devices, tick(): got_e = lax.ppermute(out_e, 'segment', swap)  6.57 us
    ppermute x1, starting transfers between devices, tick(): other = lax.ppermute(sent, 'space_2', swap)  4.81 us
    ppermute x1, waiting for transfers between devices, tick(): got_m = lax.ppermute(out_m, 'segment', swap)  4.48 us
    unnamed x17, local copies, waits for them, and re-layouts  3.74 us
    ppermute x1, starting transfers between devices, tick(): partner = lax.ppermute(owned.astype(BF16), ('segment', 'mirror'), pairs)  3.1 us
  transfers between devices with their start and end apart: 9, of which 5 were waited for; matrix products, arithmetic and copies ran while one was open for 0% of the time, Pallas kernels for 22%

profile of v3, /device:TPU:0, one launch (start us, length us, event | category | flops | bytes accessed | tf_op | source)
XLA Modules:
  0.0 86.4 jit_solution(14013043454435026799)
XLA Ops:
  0.6 7.8 %shard_map.50 = (bf16[1024,256]{1,0:T(8,128)(2,1)S(1)}, bf16[1280,256]{1,0:T(8,128)(2,1)S(1)}, bf16[1280,256]{1,0:T(8,128)(2,1)S(1)}, bf16[1280,256]{1,0:T(8,128...) custom-call(bf16[2048,256]{1,0:T(8,128)(2,1)} %bitcast.11, ...), custom_call_target="tpu_custom_call" | custom-call | flops 4227858432 | bytes 4194304 | tf_op jit(solution)/shard_map/pallas_call | solution.py:393
  8.5 0.7 collective-permute-start.1
  9.2 1.7 %collective-permute-start.5 = (bf16[1024,256]{1,0:T(8,128)(2,1)S(1)}, bf16[1024,256]{1,0:T(8,128)(2,1)S(1)}, u32[]{:S(2)}, u32[]{:S(2)}) collective-permute-start(bf16[1024,256]{1,0:T(8,128)(2,1)S(1)} %get-tuple-element.34), channel_id=1, source_target_pairs={{0,64},{64,0},{1,65},{65,1},{2,66},{66,2},{3,67},{67,3},{4,68},{68... | collective-permute-start | bytes 1572872 | tf_op jit(solution)/shard_map/ppermute | solution.py:440
  10.9 5.5 %shard_map.51 = (bf16[1024,256]{1,0:T(8,128)(2,1)S(1)}, bf16[1024,256]{1,0:T(8,128)(2,1)S(1)}, bf16[1024,256]{1,0:T(8,128)(2,1)S(1)}, bf16[1024,256]{1,0:T(8,128)(2,1)S(1)}, bf16[256,256]{1,0:T(8,128)(2,1)S(1)}) custom-call(bf16[2048,256]{1,0:T(8,128)(2,1)S(1)} %bitcast.12, bf16[2048,256]{1,0:T(8,128)(2,1)S(1)} %get-tuple-element.25.sta, ...), custom_call_target="tpu_custom_call" | custom-call | flops 3623878656 | bytes 4194304 | tf_op jit(solution)/shard_map/pallas_call | solution.py:393
  16.3 0.8 collective-permute-start.2
  17.2 4.5 %collective-permute-done.5.got_m = bf16[1024,256]{1,0:T(8,128)(2,1)S(1)} collective-permute-done((bf16[1024,256]{1,0:T(8,128)(2,1)S(1)}, bf16[1024,256]{1,0:T(8,128)(2,1)S(1)}, u32[]{:S(2)}, u32[]{:S(2)}) %collective-permute-start.5) | collective-permute-done | bytes 524320 | tf_op jit(solution)/shard_map/ppermute | solution.py:440
  21.7 4.7 %shard_map.53 = (bf16[768,256]{1,0:T(8,128)(2,1)S(1)}, f32[256,4608]{1,0:T(8,128)S(1)}) custom-call(bf16[1024,256]{1,0:T(8,128)(2,1)S(1)} %collective-permute-done.5.got_m, bf16[2048,256]{1,0:T(8,128)(2,1)S(1)} %bitcast.13, bf16[2048,256]{1,0:T(8,128)(2,1)S(1)} %get-tuple-element.25.sta, bf16[256,256]{1,0:T(8,128)(2,1)S(1)} %get-tuple-element.32.border, ...), custom_call_target="tpu_custom_call" | custom-call | flops 5737807872 | bytes 4194304 | tf_op jit(solution)/shard_map/pallas_call | solution.py:393
  26.3 6.6 %collective-permute-done.2.got_e = bf16[1024,256]{1,0:T(8,128)(2,1)S(1)} collective-permute-done((bf16[1024,256]{1,0:T(8,128)(2,1)S(1)}, bf16[1024,256]{1,0:T(8,128)(2,1)S(1)}, u32[]{:S(2)}, u32[]{:S(2)}) %collective-permute-start.2) | collective-permute-done | bytes 524320 | tf_op jit(solution)/shard_map/ppermute | solution.py:450
  32.9 2.3 %collective-permute-start.3 = (bf16[256,256]{1,0:T(8,128)(2,1)S(1)}, bf16[256,256]{1,0:T(8,128)(2,1)S(1)}, u32[]{:S(2)}, u32[]{:S(2)}) collective-permute-start(bf16[256,256]{1,0:T(8,128)(2,1)S(1)} %get-tuple-element.30), channel_id=1, source_target_pairs={{0,2},{2,0},{1,3},{3,1},{4,6},{6,4},{5,7},{7,5},{8,10},{10,8},{9,1... | collective-permute-start | bytes 393224 | tf_op jit(solution)/shard_map/ppermute | solution.py:452
  35.9 3.9 %shard_map.54 = (bf16[1024,256]{1,0:T(8,128)(2,1)S(1)}, f32[256,4608]{1,0:T(8,128)S(1)}) custom-call(bf16[1024,256]{1,0:T(8,128)(2,1)S(1)} %collective-permute-done.5.got_m, bf16[1024,256]{1,0:T(8,128)(2,1)S(1)} %collective-permute-done.2.got_e, bf16[2048,256]{1,0:T(8,128)(2,1)S(1)} %get-tuple-element.25.sta, bf16[1280,256]{1,0:T(8,128)(2,1)S(1)} %get-tuple-element.36.hid_m, ...), custom_call_target="tpu_custom_call" | custom-call | flops 3623878656 | bytes 4194304 | tf_op jit(solution)/shard_map/pallas_call | solution.py:393
  39.9 2.0 %shard_map.55 = (bf16[512,256]{1,0:T(8,128)(2,1)S(1)}, bf16[128,4608]{1,0:T(8,128)(2,1)S(1)}, f32[128,4608]{1,0:T(8,128)S(1)}) custom-call(bf16[1024,256]{1,0:T(8,128)(2,1)S(1)} %collective-permute-done.2.got_e, bf16[256,256]{1,0:T(8,128)(2,1)S(1)} %collective-permute-done.3.got_near, bf16[256,256]{1,0:T(8,128)(2,1)S(1)} %collective-permute-done.4.got_far, ...), custom_call_target="tpu_custom_call" | custom-call | flops 1207959552 | bytes 4194304 | tf_op jit(solution)/shard_map/pallas_call | solution.py:393
  41.9 4.8 %collective-permute-start.6 = (bf16[128,4608]{1,0:T(8,128)(2,1)S(1)}, bf16[128,4608]{1,0:T(8,128)(2,1)S(1)}, u32[]{:S(2)}, u32[]{:S(2)}) collective-permute-start(bf16[128,4608]{1,0:T(8,128)(2,1)S(1)} %get-tuple-element.42), channel_id=1, source_target_pairs={{0,2},{2,0},{1,3},{3,1},{4,6},{6,4},{5,7},{7,5},{8,10},{10,8},{9,1... | collective-permute-start | bytes 3538952 | tf_op jit(solution)/shard_map/ppermute | solution.py:481
  46.7 2.5 %collective-permute-done.6.other = bf16[128,4608]{1,0:T(8,128)(2,1)S(1)} collective-permute-done((bf16[128,4608]{1,0:T(8,128)(2,1)S(1)}, bf16[128,4608]{1,0:T(8,128)(2,1)S(1)}, u32[]{:S(2)}, u32[]{:S(2)}) %collective-permute-start.6) | collective-permute-done | bytes 1179680 | tf_op jit(solution)/shard_map/ppermute | solution.py:481
  49.2 1.2 %shard_map.56 = bf16[128,4608]{1,0:T(8,128)(2,1)} custom-call(f32[128,4608]{1,0:T(8,128)S(1)} %get-tuple-element.41.keep, bf16[128,4608]{1,0:T(8,128)(2,1)S(1)} %collective-permute-done.6.other), custom_call_target="tpu_custom_call" | custom-call | bytes 4194304 | tf_op jit(solution)/shard_map/pallas_call | solution.py:393
  50.4 8.1 %all-to-all-start = ((bf16[16,8,4608]{2,1,0:T(8,128)(2,1)}), bf16[16,8,4608]{2,1,0:T(8,128)(2,1)}, u32[]{:S(2)}, u32[]{:S(2)}) async-start(bf16[16,8,4608]{2,1,0:T(8,128)(2,1)} %bitcast.3), calls=%async_computation | async-start | bytes 2359296 | tf_op jit(solution)/shard_map/all_to_all | solution.py:484
  58.5 0.9 %copy-done.3 = bf16[512,256]{1,0:T(8,128)(2,1)S(1)} copy-done((bf16[512,256]{1,0:T(8,128)(2,1)S(1)}, bf16[512,256]{1,0:T(8,128)(2,1)}, u32[]{:S(2)}) %copy-start.3) | copy-done | bytes 262168
  59.5 1.0 %copy-done.5 = bf16[1024,256]{1,0:T(8,128)(2,1)S(1)} copy-done((bf16[1024,256]{1,0:T(8,128)(2,1)S(1)}, bf16[1024,256]{1,0:T(8,128)(2,1)}, u32[]{:S(2)}) %copy-start.5) | copy-done | bytes 524312
  60.5 1.0 %copy-done.7 = bf16[768,256]{1,0:T(8,128)(2,1)S(1)} copy-done((bf16[768,256]{1,0:T(8,128)(2,1)S(1)}, bf16[768,256]{1,0:T(8,128)(2,1)}, u32[]{:S(2)}) %copy-start.7) | copy-done | bytes 393240
  61.5 4.8 %shard_map.57 = bf16[2048,256]{1,0:T(8,128)(2,1)} custom-call(bf16[1024,256]{1,0:T(8,128)(2,1)S(1)} %collective-permute-done.5.got_m, bf16[1024,256]{1,0:T(8,128)(2,1)S(1)} %collective-permute-done.2.got_e, bf16[768,256]{1,0:T(8,128)(2,1)S(1)} %copy-done.7, bf16[1024,256]{1,0:T(8,128)(2,1)S(1)} %copy-done.5, bf16[512,256]{1,0:T(8,128)(2,1)S(1)} %copy-done.3, ...), custom_call_target="tpu_custom_call" | custom-call | flops 2415919104 | bytes 4194304 | tf_op jit(solution)/shard_map/pallas_call | solution.py:393
  66.3 12.2 %all-to-all-done = bf16[16,8,4608]{2,1,0:T(8,128)(2,1)} async-done(((bf16[16,8,4608]{2,1,0:T(8,128)(2,1)}), bf16[16,8,4608]{2,1,0:T(8,128)(2,1)}, u32[]{:S(2)}, u32[]{:S(2)}) %all-to-all-start) | async-done | bytes 1179680 | tf_op jit(solution)/shard_map/all_to_all | solution.py:484
  78.4 1.4 %convert_reduce_fusion = f32[8,4608]{1,0:T(8,128)S(1)} fusion(bf16[16,8,4608]{2,1,0:T(8,128)(2,1)} %all-to-all-done), kind=kLoop, calls=%fused_computation | loop fusion | flops 1142784 | bytes 1327104 | tf_op jit(solution)/shard_map/reduce_sum | solution.py:485
  79.9 3.1 %collective-permute-start.7 = (bf16[8,4608]{1,0:T(8,128)(2,1)S(1)}, bf16[8,4608]{1,0:T(8,128)(2,1)S(1)}, u32[]{:S(2)}, u32[]{:S(2)}) collective-permute-start(bf16[8,4608]{1,0:T(8,128)(2,1)S(1)} %convert_element_type.10), channel_id=1, source_target_pairs={{0,65},{1,64},{64,1},{65,0},{2,67},{3,66},{66,3},{67,2},{4,69},{5,... | collective-permute-start | bytes 221192 | tf_op jit(solution)/shard_map/ppermute | solution.py:488
  83.0 2.5 %collective-permute-done.7 = bf16[8,4608]{1,0:T(8,128)(2,1)S(1)} collective-permute-done((bf16[8,4608]{1,0:T(8,128)(2,1)S(1)}, bf16[8,4608]{1,0:T(8,128)(2,1)S(1)}, u32[]{:S(2)}, u32[]{:S(2)}) %collective-permute-start.7) | collective-permute-done | bytes 73760 | tf_op jit(solution)/shard_map/ppermute | solution.py:488
  85.6 0.7 copy.5
  (23 shorter events, 0.9 us)
Async XLA Ops:
  0.6 10.2 %copy-start = (bf16[1,1,2,3,3,256,256]{6,5,4,3,2,1,0:T(8,128)(2,1)S(1)}, bf16[1,1,2,3,3,256,256]{6,5,4,3,2,1,0:T(8,128)(2,1)}, u32[]{:S(2)}) copy-start(bf16[1,1,2,3,3,256,256]{6,5,4,3,2,1,0:T(8,128)(2,1)} %param.5) | copy-start | bytes 7077892
  0.6 10.2 %copy-start.1 = (bf16[1,1,16,128,256]{4,3,2,1,0:T(8,128)(2,1)S(1)}, bf16[1,1,16,128,256]{4,3,2,1,0:T(8,128)(2,1)}, u32[]{:S(2)}) copy-start(bf16[1,1,16,128,256]{4,3,2,1,0:T(8,128)(2,1)} %param.3) | copy-start | bytes 3145732
  8.4 2.5 %collective-permute-start = (bf16[2,256,256]{2,1,0:T(8,128)(2,1)S(1)}, bf16[2,256,256]{2,1,0:T(8,128)(2,1)S(1)}, u32[]{:S(2)}, u32[]{:S(2)}) collective-permute-start(bf16[2,256,256]{2,1,0:T(8,128)(2,1)S(1)} %get-tuple-element.26), channel_id=1, source_target_pairs={{0,2},{2,0},{1,3},{3,1},{4,6},{6,4},{5,7},{7,5},{8,10},{10,8},{9,1... | collective-permute-start | bytes 786440 | tf_op jit(solution)/shard_map/ppermute | solution.py:441
  8.5 2.4 %collective-permute-start.1 = (bf16[2,256,256]{2,1,0:T(8,128)(2,1)S(1)}, bf16[2,256,256]{2,1,0:T(8,128)(2,1)S(1)}, u32[]{:S(2)}, u32[]{:S(2)}) collective-permute-start(bf16[2,256,256]{2,1,0:T(8,128)(2,1)S(1)} %get-tuple-element.27), channel_id=1, source_target_pairs={{2,4},{6,8},{10,12},{14,16},{18,20},{22,24},{26,28},{30,32},{34,36... | collective-permute-start | bytes 786440 | tf_op jit(solution)/shard_map/ppermute | solution.py:442
  9.2 12.5 %collective-permute-start.5 = (bf16[1024,256]{1,0:T(8,128)(2,1)S(1)}, bf16[1024,256]{1,0:T(8,128)(2,1)S(1)}, u32[]{:S(2)}, u32[]{:S(2)}) collective-permute-start(bf16[1024,256]{1,0:T(8,128)(2,1)S(1)} %get-tuple-element.34), channel_id=1, source_target_pairs={{0,64},{64,0},{1,65},{65,1},{2,66},{66,2},{3,67},{67,3},{4,68},{68... | collective-permute-start | bytes 1572872 | tf_op jit(solution)/shard_map/ppermute | solution.py:440
  16.3 16.5 %collective-permute-start.2 = (bf16[1024,256]{1,0:T(8,128)(2,1)S(1)}, bf16[1024,256]{1,0:T(8,128)(2,1)S(1)}, u32[]{:S(2)}, u32[]{:S(2)}) collective-permute-start(bf16[1024,256]{1,0:T(8,128)(2,1)S(1)} %get-tuple-element.29), channel_id=1, source_target_pairs={{0,64},{64,0},{1,65},{65,1},{2,66},{66,2},{3,67},{67,3},{4,68},{68... | collective-permute-start | bytes 1572872 | tf_op jit(solution)/shard_map/ppermute | solution.py:450
  26.3 13.5 %copy-start.6 = (bf16[768,256]{1,0:T(8,128)(2,1)}, bf16[768,256]{1,0:T(8,128)(2,1)S(1)}, u32[]{:S(2)}) copy-start(bf16[768,256]{1,0:T(8,128)(2,1)S(1)} %get-tuple-element.43.act2_m) | copy-start | bytes 1179652
  32.9 7.0 %collective-permute-start.3 = (bf16[256,256]{1,0:T(8,128)(2,1)S(1)}, bf16[256,256]{1,0:T(8,128)(2,1)S(1)}, u32[]{:S(2)}, u32[]{:S(2)}) collective-permute-start(bf16[256,256]{1,0:T(8,128)(2,1)S(1)} %get-tuple-element.30), channel_id=1, source_target_pairs={{0,2},{2,0},{1,3},{3,1},{4,6},{6,4},{5,7},{7,5},{8,10},{10,8},{9,1... | collective-permute-start | bytes 393224 | tf_op jit(solution)/shard_map/ppermute | solution.py:452
  35.2 4.6 %collective-permute-start.4 = (bf16[256,256]{1,0:T(8,128)(2,1)S(1)}, bf16[256,256]{1,0:T(8,128)(2,1)S(1)}, u32[]{:S(2)}, u32[]{:S(2)}) collective-permute-start(bf16[256,256]{1,0:T(8,128)(2,1)S(1)} %get-tuple-element.31), channel_id=1, source_target_pairs={{2,4},{6,8},{10,12},{14,16},{18,20},{22,24},{26,28},{30,32},{34,36... | collective-permute-start | bytes 393224 | tf_op jit(solution)/shard_map/ppermute | solution.py:453
  39.8 2.1 %copy-start.4 = (bf16[1024,256]{1,0:T(8,128)(2,1)}, bf16[1024,256]{1,0:T(8,128)(2,1)S(1)}, u32[]{:S(2)}) copy-start(bf16[1024,256]{1,0:T(8,128)(2,1)S(1)} %get-tuple-element.44.act2_e) | copy-start | bytes 1572868
  41.9 8.5 %copy-start.2 = (bf16[512,256]{1,0:T(8,128)(2,1)}, bf16[512,256]{1,0:T(8,128)(2,1)S(1)}, u32[]{:S(2)}) copy-start(bf16[512,256]{1,0:T(8,128)(2,1)S(1)} %get-tuple-element.45.act2_h) | copy-start | bytes 786436
  41.9 7.3 %collective-permute-start.6 = (bf16[128,4608]{1,0:T(8,128)(2,1)S(1)}, bf16[128,4608]{1,0:T(8,128)(2,1)S(1)}, u32[]{:S(2)}, u32[]{:S(2)}) collective-permute-start(bf16[128,4608]{1,0:T(8,128)(2,1)S(1)} %get-tuple-element.42), channel_id=1, source_target_pairs={{0,2},{2,0},{1,3},{3,1},{4,6},{6,4},{5,7},{7,5},{8,10},{10,8},{9,1... | collective-permute-start | bytes 3538952 | tf_op jit(solution)/shard_map/ppermute | solution.py:481
  50.4 28.0 %all-to-all-start = ((bf16[16,8,4608]{2,1,0:T(8,128)(2,1)}), bf16[16,8,4608]{2,1,0:T(8,128)(2,1)}, u32[]{:S(2)}, u32[]{:S(2)}) async-start(bf16[16,8,4608]{2,1,0:T(8,128)(2,1)} %bitcast.3), calls=%async_computation | async-start | bytes 2359296 | tf_op jit(solution)/shard_map/all_to_all | solution.py:484
  58.5 1.0 %copy-start.3 = (bf16[512,256]{1,0:T(8,128)(2,1)S(1)}, bf16[512,256]{1,0:T(8,128)(2,1)}, u32[]{:S(2)}) copy-start(bf16[512,256]{1,0:T(8,128)(2,1)} %copy-done.2) | copy-start | bytes 786436
  59.5 1.0 %copy-start.5 = (bf16[1024,256]{1,0:T(8,128)(2,1)S(1)}, bf16[1024,256]{1,0:T(8,128)(2,1)}, u32[]{:S(2)}) copy-start(bf16[1024,256]{1,0:T(8,128)(2,1)} %copy-done.4) | copy-start | bytes 1572868
  60.5 1.0 %copy-start.7 = (bf16[768,256]{1,0:T(8,128)(2,1)S(1)}, bf16[768,256]{1,0:T(8,128)(2,1)}, u32[]{:S(2)}) copy-start(bf16[768,256]{1,0:T(8,128)(2,1)} %copy-done.6) | copy-start | bytes 1179652
  79.9 5.6 %collective-permute-start.7 = (bf16[8,4608]{1,0:T(8,128)(2,1)S(1)}, bf16[8,4608]{1,0:T(8,128)(2,1)S(1)}, u32[]{:S(2)}, u32[]{:S(2)}) collective-permute-start(bf16[8,4608]{1,0:T(8,128)(2,1)S(1)} %convert_element_type.10), channel_id=1, source_target_pairs={{0,65},{1,64},{64,1},{65,0},{2,67},{3,66},{66,3},{67,2},{4,69},{5,... | collective-permute-start | bytes 221192 | tf_op jit(solution)/shard_map/ppermute | solution.py:488

commit v4 on v3

--- a/solution.py
+++ b/solution.py
@@ -53,10 +53,12 @@
 
 
 def conv(src3, first, count, weights, which, transposed):
+    firsts = first if isinstance(first, tuple) else (first,)
     total = None
     for a in range(3):
         for b in range(3):
-            window = src3[rows(first + a, count), b * CH : (b + 1) * CH]
+            parts = [src3[rows(at + a, count), b * CH : (b + 1) * CH] for at in firsts]
+            window = parts[0] if len(parts) == 1 else jnp.concatenate(parts, axis=0)
             if transposed:
                 part = lax.dot_general(
                     window,
@@ -146,22 +148,19 @@
     copies = [pltpu.make_async_copy(src, dst, sems.at[i]) for i, (src, dst) in enumerate(moves)]
     for copy in copies:
         copy.start()
-    for copy in copies[:3]:
+    for copy in copies[:2]:
         copy.wait()
-
-    def body(leading):
-        fill3(s3, 0, sta, 2, 12)
+    fill3(s3, 0, sta, 2, 12)
+    for row in (0, 5):
+        hid, slope = activate(conv(s3, row, 5, w, 0, False))
+        hid_m[rows(row, 5), :] = hid.astype(BF16)
+        slope_m[rows(row, 5), :] = slope.astype(BF16)
+        steep[rows(row, 5), :] = slope
+    for copy in copies[2:]:
+        copy.wait()
+
+    def body(leading):
         fill3(a3, 0, arr, 2, 12)
-        for row in (0, 5):
-            pre = conv(s3, row, 5, w, 0, False)
-            hid, slope = activate(pre)
-            hid_m[rows(row, 5), :] = hid.astype(BF16)
-            if leading:
-                slope_m[rows(row, 5), :] = slope.astype(BF16)
-            else:
-                steep[rows(row, 5), :] = slope
-        for copy in copies[3:]:
-            copy.wait()
         for row in (0, 5):
             if leading:
                 act, _ = activate(conv(a3, row, 5, w, 0, False))
@@ -176,49 +175,81 @@
     by_role(body)
 
 
-def kernel_b(arr, sta, near, far, act_m, w, out_e, act_e, hid_e, slope_e, border, s3, a3, c3):
+def kernel_q(arr, sta, act_m, w, out_q, act_q, hid_q, slope_q, s3, a3, c3, steep):
+    fill3(s3, 0, sta, 0, 4)
+    fill3(s3, 4, sta, 12, 4)
+    hid, slope = activate(conv(s3, (0, 4), 2, w, 0, False))
+    hid_q[...] = hid.astype(BF16)
+    slope_q[...] = slope.astype(BF16)
+    steep[...] = slope
+
+    def body(leading):
+        fill3(a3, 0, arr, 0, 4)
+        fill3(a3, 4, arr, 12, 4)
+        fill3(c3, 2, act_m, 0, 2)
+        fill3(c3, 4, act_m, 8, 2)
+        if leading:
+            act, _ = activate(conv(a3, (0, 4), 2, w, 0, False))
+        else:
+            act = conv(a3, (0, 4), 2, w, 1, True) * steep[...]
+        act_q[...] = act.astype(BF16)
+        store3(c3, 0, act[: 2 * COLS], 2)
+        store3(c3, 6, act[2 * COLS :], 2)
+        total = conv(c3, (0, 4), 2, w, 1 if leading else 0, not leading)
+        for half in range(2):
+            kept = arr[rows(2 + 10 * half, 2), :].astype(F32)
+            out_q[rows(2 * half, 2), :] = (total[2 * half * COLS : (2 * half + 2) * COLS] + kept).astype(BF16)
+
+    by_role(body)
+
+
+def kernel_b(
+    arr, sta, near, far, out_q, act_q, hid_q, slope_q, w, out_e, act_e, hid_e, slope_e, border, s3, a3, c3, steep
+):
     has_up, has_down = edge_flags()
 
-    def body(leading):
+    def spread(dst, mid, val):
+        val = val.astype(BF16)
+        dst[rows(0, 2), :] = val[: 2 * COLS]
+        dst[rows(2, 4), :] = mid[...]
+        dst[rows(6, 2), :] = val[2 * COLS :]
+
+    up, down = above(near[1], far[1]), below(near[1], far[1])
+    border[rows(0, 1), :] = up[COLS:].astype(BF16)
+    border[rows(1, 1), :] = down[:COLS].astype(BF16)
+    store3(s3, 0, up, 2)
+    fill3(s3, 2, sta, 0, 2)
+    fill3(s3, 4, sta, 14, 2)
+    store3(s3, 6, down, 2)
+    spot = lax.broadcasted_iota(jnp.int32, (4 * COLS, CH), 0) // COLS
+    mask = jnp.where(spot == 0, has_up, jnp.where(spot == 3, has_down, 1.0))
+    hid, slope = activate(conv(s3, (0, 4), 2, w, 0, False))
+    spread(hid_e, hid_q, hid * mask)
+    spread(slope_e, slope_q, slope)
+    steep[...] = slope * mask
+
+    def body(leading):
+        store3(a3, 0, above(near[0], far[0]), 2)
+        fill3(a3, 2, arr, 0, 2)
+        fill3(a3, 4, arr, 14, 2)
+        store3(a3, 6, below(near[0], far[0]), 2)
+        fill3(c3, 2, act_q, 0, 2)
+        fill3(c3, 4, act_q, 2, 2)
+        if leading:
+            act, _ = activate(conv(a3, (0, 4), 2, w, 0, False))
+            spot = lax.broadcasted_iota(jnp.int32, (4 * COLS, CH), 0) // COLS
+            act = act * jnp.where(spot == 0, has_up, jnp.where(spot == 3, has_down, 1.0))
+        else:
+            act = conv(a3, (0, 4), 2, w, 1, True) * steep[...]
+        spread(act_e, act_q, act)
+        store3(c3, 0, act[: 2 * COLS], 2)
+        store3(c3, 6, act[2 * COLS :], 2)
+        total = conv(c3, (0, 4), 2, w, 1 if leading else 0, not leading)
         for half in range(2):
-            if half == 0:
-                up = above(near[1], far[1])
-                border[rows(0, 1), :] = up[COLS:].astype(BF16)
-                store3(s3, 0, up, 2)
-                fill3(s3, 2, sta, 0, 4)
-                store3(a3, 0, above(near[0], far[0]), 2)
-                fill3(a3, 2, arr, 0, 4)
-            else:
-                fill3(s3, 6, sta, 12, 4)
-                down = below(near[1], far[1])
-                border[rows(1, 1), :] = down[:COLS].astype(BF16)
-                store3(s3, 10, down, 2)
-                fill3(a3, 6, arr, 12, 4)
-                store3(a3, 10, below(near[0], far[0]), 2)
-            pre = conv(s3, 6 * half, 4, w, 0, False)
-            hid, slope = activate(pre)
-            spot = lax.broadcasted_iota(jnp.int32, (4 * COLS, CH), 0) // COLS
-            if half == 0:
-                mask = jnp.where(spot == 0, has_up, 1.0)
-            else:
-                mask = jnp.where(spot == 3, has_down, 1.0)
-            hid_e[rows(4 * half, 4), :] = (hid * mask).astype(BF16)
-            slope_e[rows(4 * half, 4), :] = slope.astype(BF16)
-            if leading:
-                act, _ = activate(conv(a3, 6 * half, 4, w, 0, False))
-            else:
-                act = conv(a3, 6 * half, 4, w, 1, True) * slope
-            act = act * mask
-            act_e[rows(4 * half, 4), :] = act.astype(BF16)
-            if half == 0:
-                store3(c3, 0, act, 4)
-                fill3(c3, 4, act_m, 0, 2)
-            else:
-                fill3(c3, 6, act_m, 8, 2)
-                store3(c3, 8, act, 4)
-            total = conv(c3, 6 * half, 4, w, 1 if leading else 0, not leading)
-            kept = arr[rows(12 * half, 4), :].astype(F32)
-            out_e[rows(4 * half, 4), :] = (total + kept).astype(BF16)
+            kept = arr[rows(14 * half, 2), :].astype(F32)
+            part = total[2 * half * COLS : (2 * half + 2) * COLS] + kept
+            out_e[rows(6 * half, 2), :] = part.astype(BF16)
+        out_e[rows(2, 4), :] = out_q[...]
 
     by_role(body)
 
@@ -272,18 +303,22 @@
         fill3(r3, 4, got_m, 0, 2)
         fill3(r3, 6, got_m, 6, 2)
         fill3(r3, 8, got_e, 4, 4)
-        for half in range(2):
-            total = conv(r3, 6 * half, 4, w, 1 if leading else 0, leading)
-            if leading:
-                if half == 0:
-                    slope = jnp.concatenate([slope_e[rows(2, 2), :], slope_m[rows(0, 2), :]], axis=0)
-                else:
-                    slope = jnp.concatenate([slope_m[rows(8, 2), :], slope_e[rows(4, 2), :]], axis=0)
-                act = total * slope.astype(F32)
-                store3(z3, 4 * half, act, 4)
-            else:
-                act, _ = activate(total)
-            act2_e[rows(4 * half, 4), :] = act.astype(BF16)
+        total = conv(r3, (0, 6), 4, w, 1 if leading else 0, leading)
+        if leading:
+            slope = jnp.concatenate(
+                [
+                    slope_e[rows(2, 2), :],
+                    slope_m[rows(0, 2), :],
+                    slope_m[rows(8, 2), :],
+                    slope_e[rows(4, 2), :],
+                ],
+                axis=0,
+            )
+            act = total * slope.astype(F32)
+            store3(z3, 0, act, 8)
+        else:
+            act, _ = activate(total)
+        act2_e[...] = act.astype(BF16)
         if leading:
             h6[rows(0, 4), :] = hid_e[rows(0, 4), :]
             h6[rows(4, 2), :] = hid_m[rows(0, 2), :]
@@ -325,18 +360,15 @@
         fill3(r3, 2, got_e, 0, 2)
         fill3(r3, 4, got_e, 6, 2)
         store3(r3, 6, below(got_near[...], got_far[...]), 2)
-        spot = lax.broadcasted_iota(jnp.int32, (2 * COLS, CH), 0) // COLS
-        for half in range(2):
-            total = conv(r3, 4 * half, 2, w, 1 if leading else 0, leading)
-            if leading:
-                act = total * slope_e[rows(6 * half, 2), :].astype(F32)
-            else:
-                act, _ = activate(total)
-            if half == 0:
-                act = act * jnp.where(spot == 0, has_up, 1.0)
-            else:
-                act = act * jnp.where(spot == 1, has_down, 1.0)
-            act2_h[rows(2 * half, 2), :] = act.astype(BF16)
+        spot = lax.broadcasted_iota(jnp.int32, (4 * COLS, CH), 0) // COLS
+        total = conv(r3, (0, 4), 2, w, 1 if leading else 0, leading)
+        if leading:
+            slope = jnp.concatenate([slope_e[rows(0, 2), :], slope_e[rows(6, 2), :]], axis=0)
+            act = total * slope.astype(F32)
+        else:
+            act, _ = activate(total)
+        act = act * jnp.where(spot == 0, has_up, jnp.where(spot == 3, has_down, 1.0))
+        act2_h[...] = act.astype(BF16)
         if leading:
             store3(z3, 0, act2_h[rows(1, 2), :], 2)
             x2[rows(0, 1), :] = border[rows(0, 1), :]
@@ -440,12 +472,19 @@
     got_m = lax.ppermute(out_m, "segment", swap)
     near = lax.ppermute(near, "space_2", swap)
     far = lax.ppermute(far, SPACE, hop)
+    quad = call(
+        kernel_q,
+        [img(4), img(4), img(4), img(4)],
+        [img3(8), img3(8), img3(8), img(4, F32)],
+        (arr, sta, act_m, w),
+        12,
+    )
     out_e, act_e, hid_e, slope_e, border = call(
         kernel_b,
         [img(8), img(8), img(8), img(8), img(2)],
-        [img3(12), img3(12), img3(12)],
-        (arr, sta, near, far, act_m, w),
-        24,
+        [img3(8), img3(8), img3(8), img(4, F32)],
+        (arr, sta, near, far, *quad, w),
+        12,
     )
     got_e = lax.ppermute(out_e, "segment", swap)
     inner_rows, outer_rows = call(kernel_pick, [img(2), img(2)], [], (got_e,), 0, limit=4)

time: 86.7 us -> 87.8 us (1.013)
  Pallas kernels: 29.8 us -> 33.3 us
  waiting for transfers between devices: 28.2 us -> 26.2 us
    pallas_call x8 -> x9, Pallas kernels: 29.8 us -> 33.3 us  [call(): pl.pallas_call(body, out_shape=[jax.ShapeDtypeStruct(shape, dtype) for sh...]
    ppermute x1, waiting for transfers between devices: 6.57 us -> 4.51 us  [tick(): got_e = lax.ppermute(out_e, 'segment', swap)]
    ppermute x1, starting transfers between devices: 4.81 us -> 6.44 us  [tick(): other = lax.ppermute(sent, 'space_2', swap)]
  transfers between devices with their start and end apart: 9 -> 9, of which waited for: 5 -> 5; matrix products, arithmetic and copies ran while one was open for 0% -> 0% of each run, Pallas kernels for 22% -> 25%
where the time goes in v4:
time: 87.8 us; the launch traced here: 87.4 us
  Pallas kernels  33.3 us (38%)
  waiting for transfers between devices  26.2 us (30%)
  starting transfers between devices  21.8 us (25%)
  local copies, waits for them, and re-layouts  3.85 us (4%)
  other arithmetic  1.47 us (2%)
    pallas_call x9, Pallas kernels, call(): pl.pallas_call(body, out_shape=[jax.ShapeDtypeStruct(shape, dtype) for sh...  33.3 us
    all_to_all x1, waiting for transfers between devices, tick(): pieces = lax.all_to_all(pieces, ('space_0', 'space_1'), 0, 0, tiled=True)  12.2 us
    all_to_all x1, starting transfers between devices, tick(): pieces = lax.all_to_all(pieces, ('space_0', 'space_1'), 0, 0, tiled=True)  7.44 us
    ppermute x1, starting transfers between devices, tick(): other = lax.ppermute(sent, 'space_2', swap)  6.44 us
    ppermute x1, waiting for transfers between devices, tick(): got_e = lax.ppermute(out_e, 'segment', swap)  4.51 us
    unnamed x17, local copies, waits for them, and re-layouts  3.74 us
    ppermute x1, waiting for transfers between devices, tick(): got_m = lax.ppermute(out_m, 'segment', swap)  3.66 us
    ppermute x1, waiting for transfers between devices, tick(): partner = lax.ppermute(owned.astype(BF16), ('segment', 'mirror'), pairs)  3.38 us
  transfers between devices with their start and end apart: 9, of which 5 were waited for; matrix products, arithmetic and copies ran while one was open for 0% of the time, Pallas kernels for 25%

profile of v4, /device:TPU:0, one launch (start us, length us, event | category | flops | bytes accessed | tf_op | source)
XLA Modules:
  0.0 87.4 jit_solution(9502796738999861191)
XLA Ops:
  0.6 7.3 %shard_map.50 = (bf16[1024,256]{1,0:T(8,128)(2,1)S(1)}, bf16[1280,256]{1,0:T(8,128)(2,1)S(1)}, bf16[1280,256]{1,0:T(8,128)(2,1)S(1)}, bf16[1280,256]{1,0:T(8,128...) custom-call(bf16[2048,256]{1,0:T(8,128)(2,1)} %bitcast.12, ...), custom_call_target="tpu_custom_call" | custom-call | flops 4227858432 | bytes 4194304 | tf_op jit(solution)/shard_map/pallas_call | solution.py:425
  7.9 1.7 %collective-permute-start.5 = (bf16[1024,256]{1,0:T(8,128)(2,1)S(1)}, bf16[1024,256]{1,0:T(8,128)(2,1)S(1)}, u32[]{:S(2)}, u32[]{:S(2)}) collective-permute-start(bf16[1024,256]{1,0:T(8,128)(2,1)S(1)} %get-tuple-element.42), channel_id=1, source_target_pairs={{0,64},{64,0},{1,65},{65,1},{2,66},{66,2},{3,67},{67,3},{4,68},{68... | collective-permute-start | bytes 1572872 | tf_op jit(solution)/shard_map/ppermute | solution.py:472
  9.6 0.7 collective-permute-start.1
  10.3 3.4 %shard_map.51 = (bf16[512,256]{1,0:T(8,128)(2,1)S(1)}, bf16[512,256]{1,0:T(8,128)(2,1)S(1)}, bf16[512,256]{1,0:T(8,128)(2,1)S(1)}, bf16[512,256]{1,0:T(8,128)(2,1)S(1)}) custom-call(bf16[2048,256]{1,0:T(8,128)(2,1)S(1)} %bitcast.13, bf16[2048,256]{1,0:T(8,128)(2,1)S(1)} %get-tuple-element.29.sta, bf16[1280,256]{1,0:T(8,128)(2,1)S(1)} %get-tuple-element.32.act_m, ...), custom_call_target="tpu_custom_call" | custom-call | flops 1811939328 | bytes 4194304 | tf_op jit(solution)/shard_map/pallas_call | solution.py:425
  13.8 3.6 %shard_map.52 = (bf16[1024,256]{1,0:T(8,128)(2,1)S(1)}, bf16[1024,256]{1,0:T(8,128)(2,1)S(1)}, bf16[1024,256]{1,0:T(8,128)(2,1)S(1)}, bf16[1024,256]{1,0:T(8,128)(2,1)S(1)}, bf16[256,256]{1,0:T(8,128)(2,1)S(1)}) custom-call(bf16[2048,256]{1,0:T(8,128)(2,1)S(1)} %bitcast.14, bf16[2048,256]{1,0:T(8,128)(2,1)S(1)} %get-tuple-element.29.sta, ...), custom_call_target="tpu_custom_call" | custom-call | flops 1811939328 | bytes 4194304 | tf_op jit(solution)/shard_map/pallas_call | solution.py:425
  17.9 3.7 %collective-permute-done.5.got_m = bf16[1024,256]{1,0:T(8,128)(2,1)S(1)} collective-permute-done((bf16[1024,256]{1,0:T(8,128)(2,1)S(1)}, bf16[1024,256]{1,0:T(8,128)(2,1)S(1)}, u32[]{:S(2)}, u32[]{:S(2)}) %collective-permute-start.5) | collective-permute-done | bytes 524320 | tf_op jit(solution)/shard_map/ppermute | solution.py:472
  21.5 4.4 %shard_map.54 = (bf16[768,256]{1,0:T(8,128)(2,1)S(1)}, f32[256,4608]{1,0:T(8,128)S(1)}) custom-call(bf16[1024,256]{1,0:T(8,128)(2,1)S(1)} %collective-permute-done.5.got_m, bf16[2048,256]{1,0:T(8,128)(2,1)S(1)} %bitcast.15, bf16[2048,256]{1,0:T(8,128)(2,1)S(1)} %get-tuple-element.29.sta, bf16[256,256]{1,0:T(8,128)(2,1)S(1)} %get-tuple-element.40.border, ...), custom_call_target="tpu_custom_call" | custom-call | flops 5737807872 | bytes 4194304 | tf_op jit(solution)/shard_map/pallas_call | solution.py:425
  26.0 4.5 %collective-permute-done.2.got_e = bf16[1024,256]{1,0:T(8,128)(2,1)S(1)} collective-permute-done((bf16[1024,256]{1,0:T(8,128)(2,1)S(1)}, bf16[1024,256]{1,0:T(8,128)(2,1)S(1)}, u32[]{:S(2)}, u32[]{:S(2)}) %collective-permute-start.2) | collective-permute-done | bytes 524320 | tf_op jit(solution)/shard_map/ppermute | solution.py:489
  30.5 2.2 %collective-permute-start.3 = (bf16[256,256]{1,0:T(8,128)(2,1)S(1)}, bf16[256,256]{1,0:T(8,128)(2,1)S(1)}, u32[]{:S(2)}, u32[]{:S(2)}) collective-permute-start(bf16[256,256]{1,0:T(8,128)(2,1)S(1)} %get-tuple-element.38), channel_id=1, source_target_pairs={{0,2},{2,0},{1,3},{3,1},{4,6},{6,4},{5,7},{7,5},{8,10},{10,8},{9,1... | collective-permute-start | bytes 393224 | tf_op jit(solution)/shard_map/ppermute | solution.py:491
  33.4 5.9 %shard_map.55 = (bf16[1024,256]{1,0:T(8,128)(2,1)S(1)}, f32[256,4608]{1,0:T(8,128)S(1)}) custom-call(bf16[1024,256]{1,0:T(8,128)(2,1)S(1)} %collective-permute-done.5.got_m, bf16[1024,256]{1,0:T(8,128)(2,1)S(1)} %collective-permute-done.2.got_e, bf16[2048,256]{1,0:T(8,128)(2,1)S(1)} %get-tuple-element.29.sta, bf16[1280,256]{1,0:T(8,128)(2,1)S(1)} %get-tuple-element.44.hid_m, ...), custom_call_target="tpu_custom_call" | custom-call | flops 3623878656 | bytes 4194304 | tf_op jit(solution)/shard_map/pallas_call | solution.py:425
  39.3 2.6 %shard_map.56 = (bf16[512,256]{1,0:T(8,128)(2,1)S(1)}, bf16[128,4608]{1,0:T(8,128)(2,1)S(1)}, f32[128,4608]{1,0:T(8,128)S(1)}) custom-call(bf16[1024,256]{1,0:T(8,128)(2,1)S(1)} %collective-permute-done.2.got_e, bf16[256,256]{1,0:T(8,128)(2,1)S(1)} %collective-permute-done.3.got_near, bf16[256,256]{1,0:T(8,128)(2,1)S(1)} %collective-permute-done.4.got_far, ...), custom_call_target="tpu_custom_call" | custom-call | flops 1207959552 | bytes 4194304 | tf_op jit(solution)/shard_map/pallas_call | solution.py:425
  42.0 6.4 %collective-permute-start.6 = (bf16[128,4608]{1,0:T(8,128)(2,1)S(1)}, bf16[128,4608]{1,0:T(8,128)(2,1)S(1)}, u32[]{:S(2)}, u32[]{:S(2)}) collective-permute-start(bf16[128,4608]{1,0:T(8,128)(2,1)S(1)} %get-tuple-element.50), channel_id=1, source_target_pairs={{0,2},{2,0},{1,3},{3,1},{4,6},{6,4},{5,7},{7,5},{8,10},{10,8},{9,1... | collective-permute-start | bytes 3538952 | tf_op jit(solution)/shard_map/ppermute | solution.py:520
  48.4 2.5 %collective-permute-done.6.other = bf16[128,4608]{1,0:T(8,128)(2,1)S(1)} collective-permute-done((bf16[128,4608]{1,0:T(8,128)(2,1)S(1)}, bf16[128,4608]{1,0:T(8,128)(2,1)S(1)}, u32[]{:S(2)}, u32[]{:S(2)}) %collective-permute-start.6) | collective-permute-done | bytes 1179680 | tf_op jit(solution)/shard_map/ppermute | solution.py:520
  50.9 1.2 %shard_map.57 = bf16[128,4608]{1,0:T(8,128)(2,1)} custom-call(f32[128,4608]{1,0:T(8,128)S(1)} %get-tuple-element.49.keep, bf16[128,4608]{1,0:T(8,128)(2,1)S(1)} %collective-permute-done.6.other), custom_call_target="tpu_custom_call" | custom-call | bytes 4194304 | tf_op jit(solution)/shard_map/pallas_call | solution.py:425
  52.1 7.4 %all-to-all-start = ((bf16[16,8,4608]{2,1,0:T(8,128)(2,1)}), bf16[16,8,4608]{2,1,0:T(8,128)(2,1)}, u32[]{:S(2)}, u32[]{:S(2)}) async-start(bf16[16,8,4608]{2,1,0:T(8,128)(2,1)} %bitcast.3), calls=%async_computation | async-start | bytes 2359296 | tf_op jit(solution)/shard_map/all_to_all | solution.py:523
  59.6 0.9 %copy-done.3 = bf16[512,256]{1,0:T(8,128)(2,1)S(1)} copy-done((bf16[512,256]{1,0:T(8,128)(2,1)S(1)}, bf16[512,256]{1,0:T(8,128)(2,1)}, u32[]{:S(2)}) %copy-start.3) | copy-done | bytes 262168
  60.5 1.0 %copy-done.5 = bf16[1024,256]{1,0:T(8,128)(2,1)S(1)} copy-done((bf16[1024,256]{1,0:T(8,128)(2,1)S(1)}, bf16[1024,256]{1,0:T(8,128)(2,1)}, u32[]{:S(2)}) %copy-start.5) | copy-done | bytes 524312
  61.5 1.0 %copy-done.7 = bf16[768,256]{1,0:T(8,128)(2,1)S(1)} copy-done((bf16[768,256]{1,0:T(8,128)(2,1)S(1)}, bf16[768,256]{1,0:T(8,128)(2,1)}, u32[]{:S(2)}) %copy-start.7) | copy-done | bytes 393240
  62.5 4.8 %shard_map.58 = bf16[2048,256]{1,0:T(8,128)(2,1)} custom-call(bf16[1024,256]{1,0:T(8,128)(2,1)S(1)} %collective-permute-done.5.got_m, bf16[1024,256]{1,0:T(8,128)(2,1)S(1)} %collective-permute-done.2.got_e, bf16[768,256]{1,0:T(8,128)(2,1)S(1)} %copy-done.7, bf16[1024,256]{1,0:T(8,128)(2,1)S(1)} %copy-done.5, bf16[512,256]{1,0:T(8,128)(2,1)S(1)} %copy-done.3, ...), custom_call_target="tpu_custom_call" | custom-call | flops 2415919104 | bytes 4194304 | tf_op jit(solution)/shard_map/pallas_call | solution.py:425
  67.3 12.2 %all-to-all-done = bf16[16,8,4608]{2,1,0:T(8,128)(2,1)} async-done(((bf16[16,8,4608]{2,1,0:T(8,128)(2,1)}), bf16[16,8,4608]{2,1,0:T(8,128)(2,1)}, u32[]{:S(2)}, u32[]{:S(2)}) %all-to-all-start) | async-done | bytes 1179680 | tf_op jit(solution)/shard_map/all_to_all | solution.py:523
  79.5 1.4 %convert_reduce_fusion = f32[8,4608]{1,0:T(8,128)S(1)} fusion(bf16[16,8,4608]{2,1,0:T(8,128)(2,1)} %all-to-all-done), kind=kLoop, calls=%fused_computation | loop fusion | flops 1142784 | bytes 1327104 | tf_op jit(solution)/shard_map/reduce_sum | solution.py:524
  80.9 2.3 %collective-permute-start.7 = (bf16[8,4608]{1,0:T(8,128)(2,1)S(1)}, bf16[8,4608]{1,0:T(8,128)(2,1)S(1)}, u32[]{:S(2)}, u32[]{:S(2)}) collective-permute-start(bf16[8,4608]{1,0:T(8,128)(2,1)S(1)} %convert_element_type.10), channel_id=1, source_target_pairs={{0,65},{1,64},{64,1},{65,0},{2,67},{3,66},{66,3},{67,2},{4,69},{5,... | collective-permute-start | bytes 221192 | tf_op jit(solution)/shard_map/ppermute | solution.py:527
  83.2 3.4 %collective-permute-done.7 = bf16[8,4608]{1,0:T(8,128)(2,1)S(1)} collective-permute-done((bf16[8,4608]{1,0:T(8,128)(2,1)S(1)}, bf16[8,4608]{1,0:T(8,128)(2,1)S(1)}, u32[]{:S(2)}, u32[]{:S(2)}) %collective-permute-start.7) | collective-permute-done | bytes 73760 | tf_op jit(solution)/shard_map/ppermute | solution.py:527
  86.7 0.7 copy.5
  (24 shorter events, 1.3 us)
Async XLA Ops:
  0.6 9.7 %copy-start = (bf16[1,1,2,3,3,256,256]{6,5,4,3,2,1,0:T(8,128)(2,1)S(1)}, bf16[1,1,2,3,3,256,256]{6,5,4,3,2,1,0:T(8,128)(2,1)}, u32[]{:S(2)}) copy-start(bf16[1,1,2,3,3,256,256]{6,5,4,3,2,1,0:T(8,128)(2,1)} %param.5) | copy-start | bytes 7077892
  0.6 9.7 %copy-start.1 = (bf16[1,1,16,128,256]{4,3,2,1,0:T(8,128)(2,1)S(1)}, bf16[1,1,16,128,256]{4,3,2,1,0:T(8,128)(2,1)}, u32[]{:S(2)}) copy-start(bf16[1,1,16,128,256]{4,3,2,1,0:T(8,128)(2,1)} %param.3) | copy-start | bytes 3145732
  7.9 13.6 %collective-permute-start.5 = (bf16[1024,256]{1,0:T(8,128)(2,1)S(1)}, bf16[1024,256]{1,0:T(8,128)(2,1)S(1)}, u32[]{:S(2)}, u32[]{:S(2)}) collective-permute-start(bf16[1024,256]{1,0:T(8,128)(2,1)S(1)} %get-tuple-element.42), channel_id=1, source_target_pairs={{0,64},{64,0},{1,65},{65,1},{2,66},{66,2},{3,67},{67,3},{4,68},{68... | collective-permute-start | bytes 1572872 | tf_op jit(solution)/shard_map/ppermute | solution.py:472
  9.6 4.1 %collective-permute-start = (bf16[2,256,256]{2,1,0:T(8,128)(2,1)S(1)}, bf16[2,256,256]{2,1,0:T(8,128)(2,1)S(1)}, u32[]{:S(2)}, u32[]{:S(2)}) collective-permute-start(bf16[2,256,256]{2,1,0:T(8,128)(2,1)S(1)} %get-tuple-element.30), channel_id=1, source_target_pairs={{0,2},{2,0},{1,3},{3,1},{4,6},{6,4},{5,7},{7,5},{8,10},{10,8},{9,1... | collective-permute-start | bytes 786440 | tf_op jit(solution)/shard_map/ppermute | solution.py:473
  9.6 4.1 %collective-permute-start.1 = (bf16[2,256,256]{2,1,0:T(8,128)(2,1)S(1)}, bf16[2,256,256]{2,1,0:T(8,128)(2,1)S(1)}, u32[]{:S(2)}, u32[]{:S(2)}) collective-permute-start(bf16[2,256,256]{2,1,0:T(8,128)(2,1)S(1)} %get-tuple-element.31), channel_id=1, source_target_pairs={{2,4},{6,8},{10,12},{14,16},{18,20},{22,24},{26,28},{30,32},{34,36... | collective-permute-start | bytes 786440 | tf_op jit(solution)/shard_map/ppermute | solution.py:474
  17.4 13.1 %collective-permute-start.2 = (bf16[1024,256]{1,0:T(8,128)(2,1)S(1)}, bf16[1024,256]{1,0:T(8,128)(2,1)S(1)}, u32[]{:S(2)}, u32[]{:S(2)}) collective-permute-start(bf16[1024,256]{1,0:T(8,128)(2,1)S(1)} %get-tuple-element.37), channel_id=1, source_target_pairs={{0,64},{64,0},{1,65},{65,1},{2,66},{66,2},{3,67},{67,3},{4,68},{68... | collective-permute-start | bytes 1572872 | tf_op jit(solution)/shard_map/ppermute | solution.py:489
  26.0 7.4 %copy-start.6 = (bf16[768,256]{1,0:T(8,128)(2,1)}, bf16[768,256]{1,0:T(8,128)(2,1)S(1)}, u32[]{:S(2)}) copy-start(bf16[768,256]{1,0:T(8,128)(2,1)S(1)} %get-tuple-element.51.act2_m) | copy-start | bytes 1179652
  30.5 8.8 %collective-permute-start.3 = (bf16[256,256]{1,0:T(8,128)(2,1)S(1)}, bf16[256,256]{1,0:T(8,128)(2,1)S(1)}, u32[]{:S(2)}, u32[]{:S(2)}) collective-permute-start(bf16[256,256]{1,0:T(8,128)(2,1)S(1)} %get-tuple-element.38), channel_id=1, source_target_pairs={{0,2},{2,0},{1,3},{3,1},{4,6},{6,4},{5,7},{7,5},{8,10},{10,8},{9,1... | collective-permute-start | bytes 393224 | tf_op jit(solution)/shard_map/ppermute | solution.py:491
  32.7 6.6 %collective-permute-start.4 = (bf16[256,256]{1,0:T(8,128)(2,1)S(1)}, bf16[256,256]{1,0:T(8,128)(2,1)S(1)}, u32[]{:S(2)}, u32[]{:S(2)}) collective-permute-start(bf16[256,256]{1,0:T(8,128)(2,1)S(1)} %get-tuple-element.39), channel_id=1, source_target_pairs={{2,4},{6,8},{10,12},{14,16},{18,20},{22,24},{26,28},{30,32},{34,36... | collective-permute-start | bytes 393224 | tf_op jit(solution)/shard_map/ppermute | solution.py:492
  39.3 2.7 %copy-start.4 = (bf16[1024,256]{1,0:T(8,128)(2,1)}, bf16[1024,256]{1,0:T(8,128)(2,1)S(1)}, u32[]{:S(2)}) copy-start(bf16[1024,256]{1,0:T(8,128)(2,1)S(1)} %get-tuple-element.52.act2_e) | copy-start | bytes 1572868
  42.0 10.1 %copy-start.2 = (bf16[512,256]{1,0:T(8,128)(2,1)}, bf16[512,256]{1,0:T(8,128)(2,1)S(1)}, u32[]{:S(2)}) copy-start(bf16[512,256]{1,0:T(8,128)(2,1)S(1)} %get-tuple-element.53.act2_h) | copy-start | bytes 786436
  42.0 8.9 %collective-permute-start.6 = (bf16[128,4608]{1,0:T(8,128)(2,1)S(1)}, bf16[128,4608]{1,0:T(8,128)(2,1)S(1)}, u32[]{:S(2)}, u32[]{:S(2)}) collective-permute-start(bf16[128,4608]{1,0:T(8,128)(2,1)S(1)} %get-tuple-element.50), channel_id=1, source_target_pairs={{0,2},{2,0},{1,3},{3,1},{4,6},{6,4},{5,7},{7,5},{8,10},{10,8},{9,1... | collective-permute-start | bytes 3538952 | tf_op jit(solution)/shard_map/ppermute | solution.py:520
  52.1 27.3 %all-to-all-start = ((bf16[16,8,4608]{2,1,0:T(8,128)(2,1)}), bf16[16,8,4608]{2,1,0:T(8,128)(2,1)}, u32[]{:S(2)}, u32[]{:S(2)}) async-start(bf16[16,8,4608]{2,1,0:T(8,128)(2,1)} %bitcast.3), calls=%async_computation | async-start | bytes 2359296 | tf_op jit(solution)/shard_map/all_to_all | solution.py:523
  59.6 1.0 %copy-start.3 = (bf16[512,256]{1,0:T(8,128)(2,1)S(1)}, bf16[512,256]{1,0:T(8,128)(2,1)}, u32[]{:S(2)}) copy-start(bf16[512,256]{1,0:T(8,128)(2,1)} %copy-done.2) | copy-start | bytes 786436
  60.5 1.0 %copy-start.5 = (bf16[1024,256]{1,0:T(8,128)(2,1)S(1)}, bf16[1024,256]{1,0:T(8,128)(2,1)}, u32[]{:S(2)}) copy-start(bf16[1024,256]{1,0:T(8,128)(2,1)} %copy-done.4) | copy-start | bytes 1572868
  61.5 1.0 %copy-start.7 = (bf16[768,256]{1,0:T(8,128)(2,1)S(1)}, bf16[768,256]{1,0:T(8,128)(2,1)}, u32[]{:S(2)}) copy-start(bf16[768,256]{1,0:T(8,128)(2,1)} %copy-done.6) | copy-start | bytes 1179652
  80.9 5.6 %collective-permute-start.7 = (bf16[8,4608]{1,0:T(8,128)(2,1)S(1)}, bf16[8,4608]{1,0:T(8,128)(2,1)S(1)}, u32[]{:S(2)}, u32[]{:S(2)}) collective-permute-start(bf16[8,4608]{1,0:T(8,128)(2,1)S(1)} %convert_element_type.10), channel_id=1, source_target_pairs={{0,65},{1,64},{64,1},{65,0},{2,67},{3,66},{66,3},{67,2},{4,69},{5,... | collective-permute-start | bytes 221192 | tf_op jit(solution)/shard_map/ppermute | solution.py:527

commit v5 on v4

--- a/solution.py
+++ b/solution.py
@@ -17,6 +17,7 @@
 TAPS = 9 * CH
 MIB = 1 << 20
 LIMIT_A = 50
+LIMIT_B = 55
 
 
 def rows(first, count):
@@ -127,23 +128,31 @@
     return jnp.where(lax.axis_index("space_2") == 0, near.astype(F32), far.astype(F32))
 
 
-def kernel_a(
-    arr_hbm, sta_hbm, w_hbm, out_m, act_m, hid_m, slope_m, near, far, sta, s3, a3, c3, w, arr, steep, sems
-):
+def kernel_edges(arr_hbm, sta_hbm, near, far, sems):
     two = 2 * COLS
     size = arr_hbm.shape[0]
     core = lax.axis_index("space_2")
     inner_at = pl.ds(pl.multiple_of((1 - core) * (size - two), two), two)
     outer_at = pl.ds(pl.multiple_of(core * (size - two), two), two)
     moves = (
+        (arr_hbm.at[inner_at], near.at[0]),
+        (sta_hbm.at[inner_at], near.at[1]),
+        (arr_hbm.at[outer_at], far.at[0]),
+        (sta_hbm.at[outer_at], far.at[1]),
+    )
+    copies = [pltpu.make_async_copy(src, dst, sems.at[i]) for i, (src, dst) in enumerate(moves)]
+    for copy in copies:
+        copy.start()
+    for copy in copies:
+        copy.wait()
+
+
+def kernel_a(arr_hbm, sta_hbm, w_hbm, out_m, act_m, hid_m, slope_m, sta, s3, a3, c3, w, arr, steep, sems):
+    moves = (
         (sta_hbm, sta),
         (w_hbm.at[0], w.at[0]),
         (arr_hbm, arr),
         (w_hbm.at[1], w.at[1]),
-        (arr_hbm.at[inner_at], near.at[0]),
-        (sta_hbm.at[inner_at], near.at[1]),
-        (arr_hbm.at[outer_at], far.at[0]),
-        (sta_hbm.at[outer_at], far.at[1]),
     )
     copies = [pltpu.make_async_copy(src, dst, sems.at[i]) for i, (src, dst) in enumerate(moves)]
     for copy in copies:
@@ -303,22 +312,18 @@
         fill3(r3, 4, got_m, 0, 2)
         fill3(r3, 6, got_m, 6, 2)
         fill3(r3, 8, got_e, 4, 4)
-        total = conv(r3, (0, 6), 4, w, 1 if leading else 0, leading)
-        if leading:
-            slope = jnp.concatenate(
-                [
-                    slope_e[rows(2, 2), :],
-                    slope_m[rows(0, 2), :],
-                    slope_m[rows(8, 2), :],
-                    slope_e[rows(4, 2), :],
-                ],
-                axis=0,
-            )
-            act = total * slope.astype(F32)
-            store3(z3, 0, act, 8)
-        else:
-            act, _ = activate(total)
-        act2_e[...] = act.astype(BF16)
+        for half in range(2):
+            total = conv(r3, 6 * half, 4, w, 1 if leading else 0, leading)
+            if leading:
+                if half == 0:
+                    slope = jnp.concatenate([slope_e[rows(2, 2), :], slope_m[rows(0, 2), :]], axis=0)
+                else:
+                    slope = jnp.concatenate([slope_m[rows(8, 2), :], slope_e[rows(4, 2), :]], axis=0)
+                act = total * slope.astype(F32)
+                store3(z3, 4 * half, act, 4)
+            else:
+                act, _ = activate(total)
+            act2_e[rows(4 * half, 4), :] = act.astype(BF16)
         if leading:
             h6[rows(0, 4), :] = hid_e[rows(0, 4), :]
             h6[rows(4, 2), :] = hid_m[rows(0, 2), :]
@@ -360,15 +365,18 @@
         fill3(r3, 2, got_e, 0, 2)
         fill3(r3, 4, got_e, 6, 2)
         store3(r3, 6, below(got_near[...], got_far[...]), 2)
-        spot = lax.broadcasted_iota(jnp.int32, (4 * COLS, CH), 0) // COLS
-        total = conv(r3, (0, 4), 2, w, 1 if leading else 0, leading)
-        if leading:
-            slope = jnp.concatenate([slope_e[rows(0, 2), :], slope_e[rows(6, 2), :]], axis=0)
-            act = total * slope.astype(F32)
-        else:
-            act, _ = activate(total)
-        act = act * jnp.where(spot == 0, has_up, jnp.where(spot == 3, has_down, 1.0))
-        act2_h[...] = act.astype(BF16)
+        spot = lax.broadcasted_iota(jnp.int32, (2 * COLS, CH), 0) // COLS
+        for half in range(2):
+            total = conv(r3, 4 * half, 2, w, 1 if leading else 0, leading)
+            if leading:
+                act = total * slope_e[rows(6 * half, 2), :].astype(F32)
+            else:
+                act, _ = activate(total)
+            if half == 0:
+                act = act * jnp.where(spot == 0, has_up, 1.0)
+            else:
+                act = act * jnp.where(spot == 1, has_down, 1.0)
+            act2_h[rows(2 * half, 2), :] = act.astype(BF16)
         if leading:
             store3(z3, 0, act2_h[rows(1, 2), :], 2)
             x2[rows(0, 1), :] = border[rows(0, 1), :]
@@ -455,23 +463,25 @@
 
     two = 2 * COLS
     edge = ((2, two, CH), BF16)
-    out_m, act_m, hid_m, slope_m, near, far, sta_v = call(
+    near, far = call(
+        kernel_edges, [edge, edge], [], (arr, sta), 0, limit=LIMIT_B, space=pltpu.HBM, sems=4
+    )
+    hop = [(i, i + 1) for i in range(1, space - 1, 2)]
+    hop = hop + [(j, i) for i, j in hop]
+    swap = [(0, 1), (1, 0)]
+    near = lax.ppermute(near, "space_2", swap)
+    far = lax.ppermute(far, SPACE, hop)
+    out_m, act_m, hid_m, slope_m, sta = call(
         kernel_a,
-        [img(8), img(10), img(10), img(10), edge, edge, img(16)],
+        [img(8), img(10), img(10), img(10), img(16)],
         [img3(12), img3(12), img3(10), (w.shape, BF16), img(16), img(10, F32)],
         (arr, sta, w),
         28,
         limit=LIMIT_A,
         space=pltpu.HBM,
-        sems=8,
-    )
-    sta = sta_v
-    hop = [(i, i + 1) for i in range(1, space - 1, 2)]
-    hop = hop + [(j, i) for i, j in hop]
-    swap = [(0, 1), (1, 0)]
+        sems=4,
+    )
     got_m = lax.ppermute(out_m, "segment", swap)
-    near = lax.ppermute(near, "space_2", swap)
-    far = lax.ppermute(far, SPACE, hop)
     quad = call(
         kernel_q,
         [img(4), img(4), img(4), img(4)],

time: 87.8 us -> 88.3 us (level)
  starting transfers between devices: 21.8 us -> 24.6 us
  waiting for transfers between devices: 26.2 us -> 24.4 us
    ppermute x1, waiting for transfers between devices: 3.66 us -> 1.63 us  [tick(): got_m = lax.ppermute(out_m, 'segment', swap)]
    ppermute x1, starting transfers between devices: 2.18 us -> 3.47 us  [tick(): got_near = lax.ppermute(inner_rows, 'space_2', swap)]
    pallas_call x9 -> x10, Pallas kernels: 33.3 us -> 32.8 us  [call(): pl.pallas_call(body, out_shape=[jax.ShapeDtypeStruct(shape, dtype) for sh...]
where the time goes in v5:
time: 88.3 us; the launch traced here: 88 us
  Pallas kernels  32.8 us (37%)
  starting transfers between devices  24.6 us (28%)
  waiting for transfers between devices  24.4 us (28%)
  local copies, waits for them, and re-layouts  3.85 us (4%)
  other arithmetic  1.47 us (2%)
    pallas_call x10, Pallas kernels, call(): pl.pallas_call(body, out_shape=[jax.ShapeDtypeStruct(shape, dtype) for sh...  32.8 us
    all_to_all x1, waiting for transfers between devices, tick(): pieces = lax.all_to_all(pieces, ('space_0', 'space_1'), 0, 0, tiled=True)  12.2 us
    all_to_all x1, starting transfers between devices, tick(): pieces = lax.all_to_all(pieces, ('space_0', 'space_1'), 0, 0, tiled=True)  8.14 us
    ppermute x1, starting transfers between devices, tick(): other = lax.ppermute(sent, 'space_2', swap)  7.12 us
    ppermute x1, waiting for transfers between devices, tick(): got_e = lax.ppermute(out_e, 'segment', swap)  4.74 us
    unnamed x17, local copies, waits for them, and re-layouts  3.74 us
    ppermute x1, starting transfers between devices, tick(): got_near = lax.ppermute(inner_rows, 'space_2', swap)  3.47 us
    ppermute x1, waiting for transfers between devices, tick(): partner = lax.ppermute(owned.astype(BF16), ('segment', 'mirror'), pairs)  3.35 us
  transfers between devices with their start and end apart: 9, of which 5 were waited for; matrix products, arithmetic and copies ran while one was open for 0% of the time, Pallas kernels for 25%

profile of v5, /device:TPU:0, one launch (start us, length us, event | category | flops | bytes accessed | tf_op | source)
XLA Modules:
  0.0 88.0 jit_solution(18234469852020738562)
XLA Ops:
  0.7 7.2 %shard_map.50 = (bf16[1024,256]{1,0:T(8,128)(2,1)S(1)}, bf16[1280,256]{1,0:T(8,128)(2,1)S(1)}, bf16[1280,256]{1,0:T(8,128)(2,1)S(1)}, bf16[1280,256]{1,0:T(8,128)(2,1)S(1)}, bf16[2048,256]{1,0:T(8,128)(2,1)S(1)}) custom-call(bf16[2048,256]{1,0:T(8,128)(2,1)} %bitcast.12, bf16[2048,256]{1,0:T(8,128)(2,1)} %bitcast.17, bf16[2,3,3,256,256]{4,3,2,1,0:T(8,128)(2,1)} %bitcast.5), custom_call_target="tpu_custom_call" | custom-call | flops 4227858432 | bytes 4194304 | tf_op jit(solution)/shard_map/pallas_call | solution.py:433
  7.9 1.7 %collective-permute-start.5 = (bf16[1024,256]{1,0:T(8,128)(2,1)S(1)}, bf16[1024,256]{1,0:T(8,128)(2,1)S(1)}, u32[]{:S(2)}, u32[]{:S(2)}) collective-permute-start(bf16[1024,256]{1,0:T(8,128)(2,1)S(1)} %get-tuple-element.42), channel_id=1, source_target_pairs={{0,64},{64,0},{1,65},{65,1},{2,66},{66,2},{3,67},{67,3},{4,68},{68... | collective-permute-start | bytes 1572872 | tf_op jit(solution)/shard_map/ppermute | solution.py:484
  9.6 1.9 %shard_map.51 = (bf16[2,256,256]{2,1,0:T(8,128)(2,1)}, bf16[2,256,256]{2,1,0:T(8,128)(2,1)}) custom-call(bf16[2048,256]{1,0:T(8,128)(2,1)} %bitcast.13, bf16[2048,256]{1,0:T(8,128)(2,1)} %bitcast.18), custom_call_target="tpu_custom_call" | custom-call | bytes 4194304 | tf_op jit(solution)/shard_map/pallas_call | solution.py:433
  12.3 3.4 %shard_map.52 = (bf16[512,256]{1,0:T(8,128)(2,1)S(1)}, bf16[512,256]{1,0:T(8,128)(2,1)S(1)}, bf16[512,256]{1,0:T(8,128)(2,1)S(1)}, bf16[512,256]{1,0:T(8,128)(2,1)S(1)}) custom-call(bf16[2048,256]{1,0:T(8,128)(2,1)S(1)} %bitcast.14, bf16[2048,256]{1,0:T(8,128)(2,1)S(1)} %get-tuple-element.29.sta, bf16[1280,256]{1,0:T(8,128)(2,1)S(1)} %get-tuple-element.32.act_m, ...), custom_call_target="tpu_custom_call" | custom-call | flops 1811939328 | bytes 4194304 | tf_op jit(solution)/shard_map/pallas_call | solution.py:433
  15.7 3.6 %shard_map.53 = (bf16[1024,256]{1,0:T(8,128)(2,1)S(1)}, bf16[1024,256]{1,0:T(8,128)(2,1)S(1)}, bf16[1024,256]{1,0:T(8,128)(2,1)S(1)}, bf16[1024,256]{1,0:T(8,128)(2,1)S(1)}, bf16[256,256]{1,0:T(8,128)(2,1)S(1)}) custom-call(bf16[2048,256]{1,0:T(8,128)(2,1)S(1)} %bitcast.15, bf16[2048,256]{1,0:T(8,128)(2,1)S(1)} %get-tuple-element.29.sta, ...), custom_call_target="tpu_custom_call" | custom-call | flops 1811939328 | bytes 4194304 | tf_op jit(solution)/shard_map/pallas_call | solution.py:433
  19.9 1.6 %collective-permute-done.5.got_m = bf16[1024,256]{1,0:T(8,128)(2,1)S(1)} collective-permute-done((bf16[1024,256]{1,0:T(8,128)(2,1)S(1)}, bf16[1024,256]{1,0:T(8,128)(2,1)S(1)}, u32[]{:S(2)}, u32[]{:S(2)}) %collective-permute-start.5) | collective-permute-done | bytes 524320 | tf_op jit(solution)/shard_map/ppermute | solution.py:484
  21.5 4.4 %shard_map.55 = (bf16[768,256]{1,0:T(8,128)(2,1)S(1)}, f32[256,4608]{1,0:T(8,128)S(1)}) custom-call(bf16[1024,256]{1,0:T(8,128)(2,1)S(1)} %collective-permute-done.5.got_m, bf16[2048,256]{1,0:T(8,128)(2,1)S(1)} %bitcast.16, bf16[2048,256]{1,0:T(8,128)(2,1)S(1)} %get-tuple-element.29.sta, bf16[256,256]{1,0:T(8,128)(2,1)S(1)} %get-tuple-element.40.border, ...), custom_call_target="tpu_custom_call" | custom-call | flops 5737807872 | bytes 4194304 | tf_op jit(solution)/shard_map/pallas_call | solution.py:433
  26.0 4.7 %collective-permute-done.2.got_e = bf16[1024,256]{1,0:T(8,128)(2,1)S(1)} collective-permute-done((bf16[1024,256]{1,0:T(8,128)(2,1)S(1)}, bf16[1024,256]{1,0:T(8,128)(2,1)S(1)}, u32[]{:S(2)}, u32[]{:S(2)}) %collective-permute-start.2) | collective-permute-done | bytes 524320 | tf_op jit(solution)/shard_map/ppermute | solution.py:499
  30.7 3.5 %collective-permute-start.3 = (bf16[256,256]{1,0:T(8,128)(2,1)S(1)}, bf16[256,256]{1,0:T(8,128)(2,1)S(1)}, u32[]{:S(2)}, u32[]{:S(2)}) collective-permute-start(bf16[256,256]{1,0:T(8,128)(2,1)S(1)} %get-tuple-element.38), channel_id=1, source_target_pairs={{0,2},{2,0},{1,3},{3,1},{4,6},{6,4},{5,7},{7,5},{8,10},{10,8},{9,1... | collective-permute-start | bytes 393224 | tf_op jit(solution)/shard_map/ppermute | solution.py:501
  34.9 4.2 %shard_map.56 = (bf16[1024,256]{1,0:T(8,128)(2,1)S(1)}, f32[256,4608]{1,0:T(8,128)S(1)}) custom-call(bf16[1024,256]{1,0:T(8,128)(2,1)S(1)} %collective-permute-done.5.got_m, bf16[1024,256]{1,0:T(8,128)(2,1)S(1)} %collective-permute-done.2.got_e, bf16[2048,256]{1,0:T(8,128)(2,1)S(1)} %get-tuple-element.29.sta, bf16[1280,256]{1,0:T(8,128)(2,1)S(1)} %get-tuple-element.44.hid_m, ...), custom_call_target="tpu_custom_call" | custom-call | flops 3623878656 | bytes 4194304 | tf_op jit(solution)/shard_map/pallas_call | solution.py:433
  39.1 2.0 %shard_map.57 = (bf16[512,256]{1,0:T(8,128)(2,1)S(1)}, bf16[128,4608]{1,0:T(8,128)(2,1)S(1)}, f32[128,4608]{1,0:T(8,128)S(1)}) custom-call(bf16[1024,256]{1,0:T(8,128)(2,1)S(1)} %collective-permute-done.2.got_e, bf16[256,256]{1,0:T(8,128)(2,1)S(1)} %collective-permute-done.3.got_near, bf16[256,256]{1,0:T(8,128)(2,1)S(1)} %collective-permute-done.4.got_far, ...), custom_call_target="tpu_custom_call" | custom-call | flops 1207959552 | bytes 4194304 | tf_op jit(solution)/shard_map/pallas_call | solution.py:433
  41.1 7.1 %collective-permute-start.6 = (bf16[128,4608]{1,0:T(8,128)(2,1)S(1)}, bf16[128,4608]{1,0:T(8,128)(2,1)S(1)}, u32[]{:S(2)}, u32[]{:S(2)}) collective-permute-start(bf16[128,4608]{1,0:T(8,128)(2,1)S(1)} %get-tuple-element.50), channel_id=1, source_target_pairs={{0,2},{2,0},{1,3},{3,1},{4,6},{6,4},{5,7},{7,5},{8,10},{10,8},{9,1... | collective-permute-start | bytes 3538952 | tf_op jit(solution)/shard_map/ppermute | solution.py:530
  48.2 2.5 %collective-permute-done.6.other = bf16[128,4608]{1,0:T(8,128)(2,1)S(1)} collective-permute-done((bf16[128,4608]{1,0:T(8,128)(2,1)S(1)}, bf16[128,4608]{1,0:T(8,128)(2,1)S(1)}, u32[]{:S(2)}, u32[]{:S(2)}) %collective-permute-start.6) | collective-permute-done | bytes 1179680 | tf_op jit(solution)/shard_map/ppermute | solution.py:530
  50.7 1.2 %shard_map.58 = bf16[128,4608]{1,0:T(8,128)(2,1)} custom-call(f32[128,4608]{1,0:T(8,128)S(1)} %get-tuple-element.49.keep, bf16[128,4608]{1,0:T(8,128)(2,1)S(1)} %collective-permute-done.6.other), custom_call_target="tpu_custom_call" | custom-call | bytes 4194304 | tf_op jit(solution)/shard_map/pallas_call | solution.py:433
  51.9 8.1 %all-to-all-start = ((bf16[16,8,4608]{2,1,0:T(8,128)(2,1)}), bf16[16,8,4608]{2,1,0:T(8,128)(2,1)}, u32[]{:S(2)}, u32[]{:S(2)}) async-start(bf16[16,8,4608]{2,1,0:T(8,128)(2,1)} %bitcast.3), calls=%async_computation | async-start | bytes 2359296 | tf_op jit(solution)/shard_map/all_to_all | solution.py:533
  60.1 0.9 %copy-done.3 = bf16[512,256]{1,0:T(8,128)(2,1)S(1)} copy-done((bf16[512,256]{1,0:T(8,128)(2,1)S(1)}, bf16[512,256]{1,0:T(8,128)(2,1)}, u32[]{:S(2)}) %copy-start.3) | copy-done | bytes 262168
  61.0 1.0 %copy-done.5 = bf16[1024,256]{1,0:T(8,128)(2,1)S(1)} copy-done((bf16[1024,256]{1,0:T(8,128)(2,1)S(1)}, bf16[1024,256]{1,0:T(8,128)(2,1)}, u32[]{:S(2)}) %copy-start.5) | copy-done | bytes 524312
  62.1 1.0 %copy-done.7 = bf16[768,256]{1,0:T(8,128)(2,1)S(1)} copy-done((bf16[768,256]{1,0:T(8,128)(2,1)S(1)}, bf16[768,256]{1,0:T(8,128)(2,1)}, u32[]{:S(2)}) %copy-start.7) | copy-done | bytes 393240
  63.1 4.8 %shard_map.59 = bf16[2048,256]{1,0:T(8,128)(2,1)} custom-call(bf16[1024,256]{1,0:T(8,128)(2,1)S(1)} %collective-permute-done.5.got_m, bf16[1024,256]{1,0:T(8,128)(2,1)S(1)} %collective-permute-done.2.got_e, bf16[768,256]{1,0:T(8,128)(2,1)S(1)} %copy-done.7, bf16[1024,256]{1,0:T(8,128)(2,1)S(1)} %copy-done.5, bf16[512,256]{1,0:T(8,128)(2,1)S(1)} %copy-done.3, ...), custom_call_target="tpu_custom_call" | custom-call | flops 2415919104 | bytes 4194304 | tf_op jit(solution)/shard_map/pallas_call | solution.py:433
  67.8 12.2 %all-to-all-done = bf16[16,8,4608]{2,1,0:T(8,128)(2,1)} async-done(((bf16[16,8,4608]{2,1,0:T(8,128)(2,1)}), bf16[16,8,4608]{2,1,0:T(8,128)(2,1)}, u32[]{:S(2)}, u32[]{:S(2)}) %all-to-all-start) | async-done | bytes 1179680 | tf_op jit(solution)/shard_map/all_to_all | solution.py:533
  80.0 1.4 %convert_reduce_fusion = f32[8,4608]{1,0:T(8,128)S(1)} fusion(bf16[16,8,4608]{2,1,0:T(8,128)(2,1)} %all-to-all-done), kind=kLoop, calls=%fused_computation | loop fusion | flops 1142784 | bytes 1327104 | tf_op jit(solution)/shard_map/reduce_sum | solution.py:534
  81.4 2.3 %collective-permute-start.7 = (bf16[8,4608]{1,0:T(8,128)(2,1)S(1)}, bf16[8,4608]{1,0:T(8,128)(2,1)S(1)}, u32[]{:S(2)}, u32[]{:S(2)}) collective-permute-start(bf16[8,4608]{1,0:T(8,128)(2,1)S(1)} %convert_element_type.10), channel_id=1, source_target_pairs={{0,65},{1,64},{64,1},{65,0},{2,67},{3,66},{66,3},{67,2},{4,69},{5,... | collective-permute-start | bytes 221192 | tf_op jit(solution)/shard_map/ppermute | solution.py:537
  83.7 3.4 %collective-permute-done.7 = bf16[8,4608]{1,0:T(8,128)(2,1)S(1)} collective-permute-done((bf16[8,4608]{1,0:T(8,128)(2,1)S(1)}, bf16[8,4608]{1,0:T(8,128)(2,1)S(1)}, u32[]{:S(2)}, u32[]{:S(2)}) %collective-permute-start.7) | collective-permute-done | bytes 73760 | tf_op jit(solution)/shard_map/ppermute | solution.py:537
  87.2 0.7 copy.5
  (25 shorter events, 2.1 us)
Async XLA Ops:
  0.6 11.7 %copy-start = (bf16[1,1,2,3,3,256,256]{6,5,4,3,2,1,0:T(8,128)(2,1)S(1)}, bf16[1,1,2,3,3,256,256]{6,5,4,3,2,1,0:T(8,128)(2,1)}, u32[]{:S(2)}) copy-start(bf16[1,1,2,3,3,256,256]{6,5,4,3,2,1,0:T(8,128)(2,1)} %param.5) | copy-start | bytes 7077892
  0.6 11.7 %copy-start.1 = (bf16[1,1,16,128,256]{4,3,2,1,0:T(8,128)(2,1)S(1)}, bf16[1,1,16,128,256]{4,3,2,1,0:T(8,128)(2,1)}, u32[]{:S(2)}) copy-start(bf16[1,1,16,128,256]{4,3,2,1,0:T(8,128)(2,1)} %param.3) | copy-start | bytes 3145732
  7.9 13.6 %collective-permute-start.5 = (bf16[1024,256]{1,0:T(8,128)(2,1)S(1)}, bf16[1024,256]{1,0:T(8,128)(2,1)S(1)}, u32[]{:S(2)}, u32[]{:S(2)}) collective-permute-start(bf16[1024,256]{1,0:T(8,128)(2,1)S(1)} %get-tuple-element.42), channel_id=1, source_target_pairs={{0,64},{64,0},{1,65},{65,1},{2,66},{66,2},{3,67},{67,3},{4,68},{68... | collective-permute-start | bytes 1572872 | tf_op jit(solution)/shard_map/ppermute | solution.py:484
  11.5 4.2 %collective-permute-start = (bf16[2,256,256]{2,1,0:T(8,128)(2,1)}, bf16[2,256,256]{2,1,0:T(8,128)(2,1)S(1)}, u32[]{:S(2)}, u32[]{:S(2)}) collective-permute-start(bf16[2,256,256]{2,1,0:T(8,128)(2,1)} %get-tuple-element.30), channel_id=1, source_target_pairs={{0,2},{2,0},{1,3},{3,1},{4,6},{6,4},{5,7},{7,5},{8,10},{10,8},{9,1... | collective-permute-start | bytes 786440 | tf_op jit(solution)/shard_map/ppermute | solution.py:472
  11.6 4.1 %collective-permute-start.1 = (bf16[2,256,256]{2,1,0:T(8,128)(2,1)}, bf16[2,256,256]{2,1,0:T(8,128)(2,1)S(1)}, u32[]{:S(2)}, u32[]{:S(2)}) collective-permute-start(bf16[2,256,256]{2,1,0:T(8,128)(2,1)} %get-tuple-element.31), channel_id=1, source_target_pairs={{2,4},{6,8},{10,12},{14,16},{18,20},{22,24},{26,28},{30,32},{34,36... | collective-permute-start | bytes 786440 | tf_op jit(solution)/shard_map/ppermute | solution.py:473
  19.4 11.3 %collective-permute-start.2 = (bf16[1024,256]{1,0:T(8,128)(2,1)S(1)}, bf16[1024,256]{1,0:T(8,128)(2,1)S(1)}, u32[]{:S(2)}, u32[]{:S(2)}) collective-permute-start(bf16[1024,256]{1,0:T(8,128)(2,1)S(1)} %get-tuple-element.37), channel_id=1, source_target_pairs={{0,64},{64,0},{1,65},{65,1},{2,66},{66,2},{3,67},{67,3},{4,68},{68... | collective-permute-start | bytes 1572872 | tf_op jit(solution)/shard_map/ppermute | solution.py:499
  25.9 13.1 %copy-start.6 = (bf16[768,256]{1,0:T(8,128)(2,1)}, bf16[768,256]{1,0:T(8,128)(2,1)S(1)}, u32[]{:S(2)}) copy-start(bf16[768,256]{1,0:T(8,128)(2,1)S(1)} %get-tuple-element.51.act2_m) | copy-start | bytes 1179652
  30.7 8.3 %collective-permute-start.3 = (bf16[256,256]{1,0:T(8,128)(2,1)S(1)}, bf16[256,256]{1,0:T(8,128)(2,1)S(1)}, u32[]{:S(2)}, u32[]{:S(2)}) collective-permute-start(bf16[256,256]{1,0:T(8,128)(2,1)S(1)} %get-tuple-element.38), channel_id=1, source_target_pairs={{0,2},{2,0},{1,3},{3,1},{4,6},{6,4},{5,7},{7,5},{8,10},{10,8},{9,1... | collective-permute-start | bytes 393224 | tf_op jit(solution)/shard_map/ppermute | solution.py:501
  34.2 4.9 %collective-permute-start.4 = (bf16[256,256]{1,0:T(8,128)(2,1)S(1)}, bf16[256,256]{1,0:T(8,128)(2,1)S(1)}, u32[]{:S(2)}, u32[]{:S(2)}) collective-permute-start(bf16[256,256]{1,0:T(8,128)(2,1)S(1)} %get-tuple-element.39), channel_id=1, source_target_pairs={{2,4},{6,8},{10,12},{14,16},{18,20},{22,24},{26,28},{30,32},{34,36... | collective-permute-start | bytes 393224 | tf_op jit(solution)/shard_map/ppermute | solution.py:502
  39.0 2.1 %copy-start.4 = (bf16[1024,256]{1,0:T(8,128)(2,1)}, bf16[1024,256]{1,0:T(8,128)(2,1)S(1)}, u32[]{:S(2)}) copy-start(bf16[1024,256]{1,0:T(8,128)(2,1)S(1)} %get-tuple-element.52.act2_e) | copy-start | bytes 1572868
  41.1 10.8 %copy-start.2 = (bf16[512,256]{1,0:T(8,128)(2,1)}, bf16[512,256]{1,0:T(8,128)(2,1)S(1)}, u32[]{:S(2)}) copy-start(bf16[512,256]{1,0:T(8,128)(2,1)S(1)} %get-tuple-element.53.act2_h) | copy-start | bytes 786436
  41.1 9.6 %collective-permute-start.6 = (bf16[128,4608]{1,0:T(8,128)(2,1)S(1)}, bf16[128,4608]{1,0:T(8,128)(2,1)S(1)}, u32[]{:S(2)}, u32[]{:S(2)}) collective-permute-start(bf16[128,4608]{1,0:T(8,128)(2,1)S(1)} %get-tuple-element.50), channel_id=1, source_target_pairs={{0,2},{2,0},{1,3},{3,1},{4,6},{6,4},{5,7},{7,5},{8,10},{10,8},{9,1... | collective-permute-start | bytes 3538952 | tf_op jit(solution)/shard_map/ppermute | solution.py:530
  51.9 28.0 %all-to-all-start = ((bf16[16,8,4608]{2,1,0:T(8,128)(2,1)}), bf16[16,8,4608]{2,1,0:T(8,128)(2,1)}, u32[]{:S(2)}, u32[]{:S(2)}) async-start(bf16[16,8,4608]{2,1,0:T(8,128)(2,1)} %bitcast.3), calls=%async_computation | async-start | bytes 2359296 | tf_op jit(solution)/shard_map/all_to_all | solution.py:533
  60.1 1.0 %copy-start.3 = (bf16[512,256]{1,0:T(8,128)(2,1)S(1)}, bf16[512,256]{1,0:T(8,128)(2,1)}, u32[]{:S(2)}) copy-start(bf16[512,256]{1,0:T(8,128)(2,1)} %copy-done.2) | copy-start | bytes 786436
  61.0 1.0 %copy-start.5 = (bf16[1024,256]{1,0:T(8,128)(2,1)S(1)}, bf16[1024,256]{1,0:T(8,128)(2,1)}, u32[]{:S(2)}) copy-start(bf16[1024,256]{1,0:T(8,128)(2,1)} %copy-done.4) | copy-start | bytes 1572868
  62.1 1.0 %copy-start.7 = (bf16[768,256]{1,0:T(8,128)(2,1)S(1)}, bf16[768,256]{1,0:T(8,128)(2,1)}, u32[]{:S(2)}) copy-start(bf16[768,256]{1,0:T(8,128)(2,1)} %copy-done.6) | copy-start | bytes 1179652
  81.4 5.6 %collective-permute-start.7 = (bf16[8,4608]{1,0:T(8,128)(2,1)S(1)}, bf16[8,4608]{1,0:T(8,128)(2,1)S(1)}, u32[]{:S(2)}, u32[]{:S(2)}) collective-permute-start(bf16[8,4608]{1,0:T(8,128)(2,1)S(1)} %convert_element_type.10), channel_id=1, source_target_pairs={{0,65},{1,64},{64,1},{65,0},{2,67},{3,66},{66,3},{67,2},{4,69},{5,... | collective-permute-start | bytes 221192 | tf_op jit(solution)/shard_map/ppermute | solution.py:537
